TPU v7x, 32 devices: a whole 2x2x4 slice. The times are simulated.
32 devices in a mesh: mx: 8 (over y, x, core), my: 4 (over z).
Axes of the slice: x: 2, y: 2, z: 4, core: 2. Of those that a mesh axis runs over, the one named last changes fastest.
Arguments:
- positions: float32 [3, 4096], P(None, ('mx', 'my')), may hold values from -6 to 6
- velocities: float32 [3, 4096], P(None, ('mx', 'my')), may hold values from -6 to 6
- rest_positions: float32 [3, 4096], P(None, ('mx', 'my')), may hold values from -6 to 6
- inverse_mass: float32 [4096], P(('mx', 'my')), may hold values from 0.5 to 2
- element_nodes: int32 [8, 8192], P(None, ('mx', 'my')), may hold values from 0 to 127
- modulus: float32 [8192], P(('mx', 'my')), may hold values from 0.1 to 1
- stiffness: float32 [24, 24], replicated, may hold values from -0.7 to 4.7
- shared_lists: int32 [4, 4096], P(None, ('mx', 'my')), may hold values from 0 to 127
- patch_nodes: int32 [512, 128], P(('mx', 'my')), may hold values from 0 to 127
- patch_owner: int32 [512], P(('mx', 'my')), may hold values from 0 to 3, as said below
- pair_map: int32 [512, 128], P(('mx', 'my')), may hold values from 0 to 127
Outputs:
- new_positions: float32 [3, 4096], P(None, ('mx', 'my'))
- new_velocities: float32 [3, 4096], P(None, ('mx', 'my'))
Inputs may be any that keep to these rules, and one draw needn't show every extreme that they name: `patch_owner`: on every device, at most 8 of its 16 patches name one owner, and exactly 8 name some owner.
All inputs are finite; a program needn't handle non-finite values.
Results may differ from a plain program's by a relative error of at most 0.0003.
Values sent between devices are 32-bit elements; how exact they have to be, the bound alone decides.
No kernel may reach another device: no remote copies, remote signals or barrier semaphores. Data moves between devices by JAX's collectives and lax.ppermute only.
A program may use at most 64 MiB of HBM per device.

v0:
```python
import jax
import jax.numpy as jnp
from jax import lax
from jax.sharding import PartitionSpec as P

STEPS = 2


time_step = 0.1
penalty = 4.0
damping = 0.5
contact_reach = 4.0
exact = lax.Precision.HIGHEST


def with_halo(value, sides, width):
    for axis, dim in sides:
        size, length = (lax.axis_size(axis), value.shape[dim])
        up = [(i, (i + 1) % size) for i in range(size - 1)]
        down = [(j, i) for i, j in up]
        last = lax.slice_in_dim(value, length - width, length, axis=dim)
        first = lax.slice_in_dim(value, 0, width, axis=dim)
        before = lax.ppermute(last, axis, up)
        after = lax.ppermute(first, axis, down)
        value = jnp.concatenate([before, value, after], axis=dim)
    return value


def one_hot_table(indices, count):
    columns = jnp.arange(count, dtype=jnp.int32)
    return (indices[..., None] == columns).astype(jnp.float32)


def element_forces(displaced, element_hot, modulus, stiffness):
    elements_count = element_hot.shape[1]
    local_disp = jnp.einsum("cn,aen->cae", displaced, element_hot, precision=exact).reshape(
        24, elements_count
    )
    product = jnp.dot(stiffness, local_disp, precision=exact)
    forces = (-modulus[None, :] * product).reshape(3, 8, elements_count)
    return jnp.einsum("cae,aen->cn", forces, element_hot, precision=exact)


def pair_forces(states, partner):
    offset = partner[:, 0:3] - states[:, 0:3]
    distance = jnp.sum(offset * offset, axis=1, keepdims=True)
    weight = jnp.exp(-distance / contact_reach)
    return -penalty * weight * offset + damping * weight * (partner[:, 3:6] - states[:, 3:6])


def owner_contact(states, pair_hot, live_flags):
    count = states.shape[0]
    before = jnp.cumsum(live_flags) - live_flags
    total_live = jnp.maximum(jnp.sum(live_flags), 1.0)
    wanted = jnp.mod(before + 1.0, total_live)
    link = (
        live_flags[:, None]
        * live_flags[None, :]
        * (before[None, :] == wanted[:, None]).astype(jnp.float32)
    )
    partner_rows = jnp.dot(link, states.reshape(count, -1), precision=exact).reshape(states.shape)
    partner = jnp.einsum("scm,skm->sck", partner_rows, pair_hot, precision=exact)
    forces = pair_forces(states, partner) * live_flags[:, None, None]
    pushes = -jnp.einsum("sck,skm->scm", forces, pair_hot, precision=exact)
    arriving = jnp.einsum("st,sk->tk", link, pushes.reshape(count, -1), precision=exact)
    return forces + arriving.reshape(forces.shape)


def send_full(location, motion, patch_hot, target_slot, pair_values, live_flags, slots):
    members = jnp.einsum(
        "cn,pkn->pck", jnp.concatenate([location, motion], axis=0), patch_hot, precision=exact
    )
    packed = jnp.zeros((slots, 6, members.shape[2]), jnp.float32).at[target_slot].set(members)
    return (
        lax.all_to_all(packed, "my", split_axis=0, concat_axis=0, tiled=True),
        lax.all_to_all(pair_values, "my", split_axis=0, concat_axis=0, tiled=True),
        lax.all_to_all(live_flags, "my", split_axis=0, concat_axis=0, tiled=True),
    )


def body(
    positions,
    velocities,
    rest_positions,
    inverse_mass,
    element_nodes,
    modulus,
    stiffness,
    shared_lists,
    patch_nodes,
    patch_owner,
    pair_map,
):
    width = lax.axis_size("my")
    per_device = patch_owner.shape[0]
    capacity = max(2, 2 * per_device // width)
    slots = width * capacity
    nodes_count = positions.shape[1]
    patch_width = pair_map.shape[1]
    columns = jnp.arange(width, dtype=jnp.int32)
    hits = (patch_owner[:, None] == columns[None, :]).astype(jnp.int32)
    within = jnp.sum(jnp.cumsum(hits, axis=0) * hits, axis=1) - 1
    target_slot = patch_owner * capacity + within
    pair_values = (
        jnp.zeros((slots, patch_width), jnp.float32)
        .at[target_slot]
        .set(pair_map.astype(jnp.float32))
    )
    live_flags = jnp.zeros((slots,), jnp.float32).at[target_slot].set(1.0)
    element_hot = one_hot_table(element_nodes, nodes_count)
    patch_hot = one_hot_table(patch_nodes, nodes_count)
    face_hot = one_hot_table(shared_lists, nodes_count)
    location = positions
    motion = velocities
    pair_hot = None
    received_live = None
    for section in range(STEPS):
        states, received_pairs, received_live = send_full(
            location, motion, patch_hot, target_slot, pair_values, live_flags, slots
        )
        pair_hot = one_hot_table(received_pairs.astype(jnp.int32), patch_width)
        returned = owner_contact(states, pair_hot, received_live)
        back = lax.all_to_all(returned, "my", split_axis=0, concat_axis=0, tiled=True)
        mine = back[target_slot]
        contact = jnp.einsum("pck,pkn->cn", mine, patch_hot, precision=exact)
        assembled = (
            element_forces(location - rest_positions, element_hot, modulus, stiffness) + contact
        )
        face_values = jnp.einsum("cn,lfn->clf", assembled, face_hot, precision=exact)
        faces_x = with_halo(face_values[:, 0:2], (("mx", 1),), 1)
        faces_y = with_halo(face_values[:, 2:4], (("my", 1),), 1)
        incoming = jnp.stack([faces_x[:, 0], faces_x[:, 3], faces_y[:, 0], faces_y[:, 3]], axis=1)
        total = assembled + jnp.einsum("clf,lfn->cn", incoming, face_hot, precision=exact)
        motion = motion + time_step * inverse_mass[None, :] * total
        location = location + time_step * motion
    return (location, motion)


def solution(mesh):
    in_specs = (
        P(None, ("mx", "my")),
        P(None, ("mx", "my")),
        P(None, ("mx", "my")),
        P(("mx", "my")),
        P(None, ("mx", "my")),
        P(("mx", "my")),
        P(),
        P(None, ("mx", "my")),
        P(("mx", "my"), None),
        P(("mx", "my")),
        P(("mx", "my"), None),
    )
    out_specs = (P(None, ("mx", "my")), P(None, ("mx", "my")))
    return jax.shard_map(body, mesh=mesh, in_specs=in_specs, out_specs=out_specs, check_vma=False)
```

profile of v0, /device:TPU:4, one launch (start us, length us, event | category | flops | bytes accessed | tf_op | source)
XLA Modules:
  0.0 111.9 jit_solution(11807350189572363404)
XLA Ops:
  4.2 4.9 %all-to-all-start = ((f32[4,8,1]{1,2,0:T(1,128)}), f32[4,8,1]{1,2,0:T(1,128)S(1)}, u32[]{:S(2)}, u32[]{:S(2)}) async-start(f32[4,8,1]{1,2,0:T(1,128)} %bitcast.5), calls=%async_computation | async-start | bytes 4096 | tf_op jit(solution)/shard_map/all_to_all | solution.py:77
  9.8 1.5 %fusion.21 = f32[3,8,256]{2,0,1:T(4,128)S(1)} fusion(s32[8,256]{1,0:T(8,128)} %param.15, f32[3,128]{1,0:T(4,128)} %param.11, f32[3,128]{1,0:T(4,128)} %param.13), kind=kOutput, calls=%fused_computation.40 | convolution fusion | flops 9699712 | bytes 35840 | tf_op jit(solution)/shard_map/cn,aen->cae/dot_general | solution.py:36
  13.5 2.0 %scatter_fusion = f32[32,6,128]{2,1,0:T(8,128)} fusion(f32[32,6,128]{2,1,0:T(8,128)} %broadcast.122.clone, s32[16]{0:T(128)S(1)} %compare_select_fusion, f32[16,6,128]{2,1,0:T(8,128)S(1)} %convolution_bitcast_fusion.1), kind=kCustom, calls=%fused_computation.3 | custom fusion | bytes 147520 | tf_op jit(solution)/shard_map/scatter | solution.py:73
  16.7 5.1 %all-to-all-start.2 = ((f32[4,8,128]{2,1,0:T(8,128)}), f32[4,8,128]{2,1,0:T(8,128)S(1)}, u32[]{:S(2)}, u32[]{:S(2)}) async-start(f32[4,8,128]{2,1,0:T(8,128)} %bitcast.10), calls=%async_computation.2 | async-start | bytes 32768 | tf_op jit(solution)/shard_map/all_to_all | solution.py:76
  24.6 2.8 %all-to-all-done.2 = f32[4,8,128]{2,1,0:T(8,128)S(1)} async-done(((f32[4,8,128]{2,1,0:T(8,128)}), f32[4,8,128]{2,1,0:T(8,128)S(1)}, u32[]{:S(2)}, u32[]{:S(2)}) %all-to-all-start.2) | async-done | bytes 16416 | tf_op jit(solution)/shard_map/all_to_all | solution.py:76
  27.5 3.3 %all-to-all-start.1 = ((f32[32,6,128]{2,1,0:T(8,128)}), f32[32,6,128]{2,1,0:T(8,128)S(1)}, u32[]{:S(2)}, u32[]{:S(2)}) async-start(f32[32,6,128]{2,1,0:T(8,128)} %scatter_fusion), calls=%async_computation.1 | async-start | bytes 262144 | tf_op jit(solution)/shard_map/all_to_all | solution.py:75
  30.8 5.9 %all-to-all-done.1 = f32[32,6,128]{2,1,0:T(8,128)S(1)} async-done(((f32[32,6,128]{2,1,0:T(8,128)}), f32[32,6,128]{2,1,0:T(8,128)S(1)}, u32[]{:S(2)}, u32[]{:S(2)}) %all-to-all-start.1) | async-done | bytes 98336 | tf_op jit(solution)/shard_map/all_to_all | solution.py:75
  37.0 2.4 %fusion.3 = f32[32,6,128]{2,1,0:T(8,128)S(1)} fusion(s32[32,128]{1,0:T(8,128)S(1)} %convert_bitcast_fusion, f32[32,6,128]{2,0,1:T(8,128)S(1)} %fusion.41), kind=kOutput, calls=%fused_computation.10 | convolution fusion | flops 38273024 | bytes 212992 | tf_op jit(solution)/shard_map/scm,skm->sck/dot_general | solution.py:62
  42.0 3.3 %all-to-all-start.3 = ((f32[32,3,128]{2,1,0:T(4,128)}), f32[32,3,128]{2,1,0:T(4,128)S(1)}, u32[]{:S(2)}, u32[]{:S(2)}) async-start(f32[32,3,128]{2,1,0:T(4,128)} %copy_add_fusion.1), calls=%async_computation.3 | async-start | bytes 131072 | tf_op jit(solution)/shard_map/all_to_all | solution.py:123
  45.3 5.7 %all-to-all-done.3 = f32[32,3,128]{2,1,0:T(4,128)S(1)} async-done(((f32[32,3,128]{2,1,0:T(4,128)}), f32[32,3,128]{2,1,0:T(4,128)S(1)}, u32[]{:S(2)}, u32[]{:S(2)}) %all-to-all-start.3) | async-done | bytes 49184 | tf_op jit(solution)/shard_map/all_to_all | solution.py:123
  52.6 1.9 %collective-permute-start = (f32[3,1,128]{2,0,1:T(4,128)S(1)}, f32[3,1,128]{2,0,1:T(4,128)S(1)}, u32[]{:S(2)}, u32[]{:S(2)}) collective-permute-start(f32[3,1,128]{2,0,1:T(4,128)S(1)} %get-tuple-element.14), channel_id=1, source_target_pairs={{0,4},{4,8},{8,12},{12,16},{16,20},{20,24},{24,28},{1,5},{5,9},{9,... | collective-permute-start | bytes 4616 | tf_op jit(solution)/shard_map/ppermute | solution.py:23
  54.5 4.5 %collective-permute-start.1 = (f32[3,1,128]{2,0,1:T(4,128)S(1)}, f32[3,1,128]{2,0,1:T(4,128)S(1)}, u32[]{:S(2)}, u32[]{:S(2)}) collective-permute-start(f32[3,1,128]{2,0,1:T(4,128)S(1)} %get-tuple-element.17), channel_id=1, source_target_pairs={{4,0},{8,4},{12,8},{16,12},{20,16},{24,20},{28,24},{5,1},{9,5},{13... | collective-permute-start | bytes 4616 | tf_op jit(solution)/shard_map/ppermute | solution.py:24
  59.1 2.8 %collective-permute-start.2 = (f32[3,1,128]{2,0,1:T(4,128)S(1)}, f32[3,1,128]{2,0,1:T(4,128)S(1)}, u32[]{:S(2)}, u32[]{:S(2)}) collective-permute-start(f32[3,1,128]{2,0,1:T(4,128)S(1)} %get-tuple-element.16), channel_id=1, source_target_pairs={{0,1},{1,2},{2,3},{4,5},{5,6},{6,7},{8,9},{9,10},{10,11},{12,13},{... | collective-permute-start | bytes 4616 | tf_op jit(solution)/shard_map/ppermute | solution.py:23
  63.3 4.1 %collective-permute-done.3 = f32[3,1,128]{2,0,1:T(4,128)S(1)} collective-permute-done((f32[3,1,128]{2,0,1:T(4,128)S(1)}, f32[3,1,128]{2,0,1:T(4,128)S(1)}, u32[]{:S(2)}, u32[]{:S(2)}) %collective-permute-start.3) | collective-permute-done | bytes 1568 | tf_op jit(solution)/shard_map/ppermute | solution.py:24
  69.1 2.0 %scatter_fusion.1 = f32[32,6,128]{2,1,0:T(8,128)} fusion(f32[32,6,128]{2,1,0:T(8,128)} %broadcast.122, s32[16]{0:T(128)S(1)} %compare_select_fusion, f32[16,6,128]{2,1,0:T(8,128)S(1)} %convolution_bitcast_fusion), kind=kCustom, calls=%fused_computation.5 | custom fusion | bytes 147520 | tf_op jit(solution)/shard_map/scatter | solution.py:73
  71.1 3.5 %all-to-all-start.4 = ((f32[32,6,128]{2,1,0:T(8,128)}), f32[32,6,128]{2,1,0:T(8,128)S(1)}, u32[]{:S(2)}, u32[]{:S(2)}) async-start(f32[32,6,128]{2,1,0:T(8,128)} %scatter_fusion.1), calls=%async_computation.4 | async-start | bytes 262144 | tf_op jit(solution)/shard_map/all_to_all | solution.py:75
  75.5 5.0 %all-to-all-done.4 = f32[32,6,128]{2,1,0:T(8,128)S(1)} async-done(((f32[32,6,128]{2,1,0:T(8,128)}), f32[32,6,128]{2,1,0:T(8,128)S(1)}, u32[]{:S(2)}, u32[]{:S(2)}) %all-to-all-start.4) | async-done | bytes 98336 | tf_op jit(solution)/shard_map/all_to_all | solution.py:75
  80.8 2.4 %fusion.1 = f32[32,6,128]{2,1,0:T(8,128)S(1)} fusion(s32[32,128]{1,0:T(8,128)S(1)} %convert_bitcast_fusion, f32[32,6,128]{2,0,1:T(8,128)S(1)} %fusion.38), kind=kOutput, calls=%fused_computation.8 | convolution fusion | flops 38273024 | bytes 212992 | tf_op jit(solution)/shard_map/scm,skm->sck/dot_general | solution.py:62
  85.8 3.3 %all-to-all-start.5 = ((f32[32,3,128]{2,1,0:T(4,128)}), f32[32,3,128]{2,1,0:T(4,128)S(1)}, u32[]{:S(2)}, u32[]{:S(2)}) async-start(f32[32,3,128]{2,1,0:T(4,128)} %copy_add_fusion), calls=%async_computation.5 | async-start | bytes 131072 | tf_op jit(solution)/shard_map/all_to_all | solution.py:123
  89.6 5.1 %all-to-all-done.5 = f32[32,3,128]{2,1,0:T(4,128)S(1)} async-done(((f32[32,3,128]{2,1,0:T(4,128)}), f32[32,3,128]{2,1,0:T(4,128)S(1)}, u32[]{:S(2)}, u32[]{:S(2)}) %all-to-all-start.5) | async-done | bytes 49184 | tf_op jit(solution)/shard_map/all_to_all | solution.py:123
  96.3 1.9 %collective-permute-start.4 = (f32[3,1,128]{2,0,1:T(4,128)S(1)}, f32[3,1,128]{2,0,1:T(4,128)S(1)}, u32[]{:S(2)}, u32[]{:S(2)}) collective-permute-start(f32[3,1,128]{2,0,1:T(4,128)S(1)} %get-tuple-element.10), channel_id=1, source_target_pairs={{0,4},{4,8},{8,12},{12,16},{16,20},{20,24},{24,28},{1,5},{5,9},{9,... | collective-permute-start | bytes 4616 | tf_op jit(solution)/shard_map/ppermute | solution.py:23
  98.2 4.5 %collective-permute-start.5 = (f32[3,1,128]{2,0,1:T(4,128)S(1)}, f32[3,1,128]{2,0,1:T(4,128)S(1)}, u32[]{:S(2)}, u32[]{:S(2)}) collective-permute-start(f32[3,1,128]{2,0,1:T(4,128)S(1)} %get-tuple-element.13), channel_id=1, source_target_pairs={{4,0},{8,4},{12,8},{16,12},{20,16},{24,20},{28,24},{5,1},{9,5},{13... | collective-permute-start | bytes 4616 | tf_op jit(solution)/shard_map/ppermute | solution.py:24
  102.8 2.8 %collective-permute-start.6 = (f32[3,1,128]{2,0,1:T(4,128)S(1)}, f32[3,1,128]{2,0,1:T(4,128)S(1)}, u32[]{:S(2)}, u32[]{:S(2)}) collective-permute-start(f32[3,1,128]{2,0,1:T(4,128)S(1)} %get-tuple-element.12), channel_id=1, source_target_pairs={{0,1},{1,2},{2,3},{4,5},{5,6},{6,7},{8,9},{9,10},{10,11},{12,13},{... | collective-permute-start | bytes 4616 | tf_op jit(solution)/shard_map/ppermute | solution.py:23
  106.9 4.1 %collective-permute-done.7 = f32[3,1,128]{2,0,1:T(4,128)S(1)} collective-permute-done((f32[3,1,128]{2,0,1:T(4,128)S(1)}, f32[3,1,128]{2,0,1:T(4,128)S(1)}, u32[]{:S(2)}, u32[]{:S(2)}) %collective-permute-start.7) | collective-permute-done | bytes 1568 | tf_op jit(solution)/shard_map/ppermute | solution.py:24
  (79 shorter events, 25.3 us)
Async XLA Ops:
  0.6 10.6 %copy-start = (f32[24,24]{1,0:T(8,128)S(1)}, f32[24,24]{1,0:T(8,128)}, u32[]{:S(2)}) copy-start(f32[24,24]{1,0:T(8,128)} %param.17) | copy-start | bytes 6916
  4.2 12.5 %all-to-all-start = ((f32[4,8,1]{1,2,0:T(1,128)}), f32[4,8,1]{1,2,0:T(1,128)S(1)}, u32[]{:S(2)}, u32[]{:S(2)}) async-start(f32[4,8,1]{1,2,0:T(1,128)} %bitcast.5), calls=%async_computation | async-start | bytes 4096 | tf_op jit(solution)/shard_map/all_to_all | solution.py:77
  9.8 1.7 %copy-start.2 = (s32[8,256]{1,0:T(8,128)S(1)}, s32[8,256]{1,0:T(8,128)}, u32[]{:S(2)}) copy-start(s32[8,256]{1,0:T(8,128)} %param.15) | copy-start | bytes 24580
  11.4 0.7 copy-start.3
  11.4 0.7 copy-start.4
  11.5 0.7 copy-start.5
  13.5 2.0 %copy-start.1 = (s32[16,128]{1,0:T(8,128)S(1)}, s32[16,128]{1,0:T(8,128)}, u32[]{:S(2)}) copy-start(s32[16,128]{1,0:T(8,128)} %param.21) | copy-start | bytes 24580
  16.7 10.7 %all-to-all-start.2 = ((f32[4,8,128]{2,1,0:T(8,128)}), f32[4,8,128]{2,1,0:T(8,128)S(1)}, u32[]{:S(2)}, u32[]{:S(2)}) async-start(f32[4,8,128]{2,1,0:T(8,128)} %bitcast.10), calls=%async_computation.2 | async-start | bytes 32768 | tf_op jit(solution)/shard_map/all_to_all | solution.py:76
  27.5 9.2 %all-to-all-start.1 = ((f32[32,6,128]{2,1,0:T(8,128)}), f32[32,6,128]{2,1,0:T(8,128)S(1)}, u32[]{:S(2)}, u32[]{:S(2)}) async-start(f32[32,6,128]{2,1,0:T(8,128)} %scatter_fusion), calls=%async_computation.1 | async-start | bytes 262144 | tf_op jit(solution)/shard_map/all_to_all | solution.py:75
  42.0 9.0 %all-to-all-start.3 = ((f32[32,3,128]{2,1,0:T(4,128)}), f32[32,3,128]{2,1,0:T(4,128)S(1)}, u32[]{:S(2)}, u32[]{:S(2)}) async-start(f32[32,3,128]{2,1,0:T(4,128)} %copy_add_fusion.1), calls=%async_computation.3 | async-start | bytes 131072 | tf_op jit(solution)/shard_map/all_to_all | solution.py:123
  51.6 0.7 copy-start.7
  51.6 11.6 %copy-start.8 = (f32[128]{0:T(128)S(1)}, f32[128]{0:T(128)}, u32[]{:S(2)}) copy-start(f32[128]{0:T(128)} %param.14) | copy-start | bytes 1540
  52.6 10.6 %collective-permute-start = (f32[3,1,128]{2,0,1:T(4,128)S(1)}, f32[3,1,128]{2,0,1:T(4,128)S(1)}, u32[]{:S(2)}, u32[]{:S(2)}) collective-permute-start(f32[3,1,128]{2,0,1:T(4,128)S(1)} %get-tuple-element.14), channel_id=1, source_target_pairs={{0,4},{4,8},{8,12},{12,16},{16,20},{20,24},{24,28},{1,5},{5,9},{9,... | collective-permute-start | bytes 4616 | tf_op jit(solution)/shard_map/ppermute | solution.py:23
  54.5 8.7 %collective-permute-start.1 = (f32[3,1,128]{2,0,1:T(4,128)S(1)}, f32[3,1,128]{2,0,1:T(4,128)S(1)}, u32[]{:S(2)}, u32[]{:S(2)}) collective-permute-start(f32[3,1,128]{2,0,1:T(4,128)S(1)} %get-tuple-element.17), channel_id=1, source_target_pairs={{4,0},{8,4},{12,8},{16,12},{20,16},{24,20},{28,24},{5,1},{9,5},{13... | collective-permute-start | bytes 4616 | tf_op jit(solution)/shard_map/ppermute | solution.py:24
  59.1 4.2 %collective-permute-start.2 = (f32[3,1,128]{2,0,1:T(4,128)S(1)}, f32[3,1,128]{2,0,1:T(4,128)S(1)}, u32[]{:S(2)}, u32[]{:S(2)}) collective-permute-start(f32[3,1,128]{2,0,1:T(4,128)S(1)} %get-tuple-element.16), channel_id=1, source_target_pairs={{0,1},{1,2},{2,3},{4,5},{5,6},{6,7},{8,9},{9,10},{10,11},{12,13},{... | collective-permute-start | bytes 4616 | tf_op jit(solution)/shard_map/ppermute | solution.py:23
  61.9 5.5 %collective-permute-start.3 = (f32[3,1,128]{2,0,1:T(4,128)S(1)}, f32[3,1,128]{2,0,1:T(4,128)S(1)}, u32[]{:S(2)}, u32[]{:S(2)}) collective-permute-start(f32[3,1,128]{2,0,1:T(4,128)S(1)} %get-tuple-element.15), channel_id=1, source_target_pairs={{1,0},{2,1},{3,2},{5,4},{6,5},{7,6},{9,8},{10,9},{11,10},{13,12},{... | collective-permute-start | bytes 4616 | tf_op jit(solution)/shard_map/ppermute | solution.py:24
  71.1 3.5 %copy-start.6 = (f32[3,128]{1,0:T(4,128)S(1)}, f32[3,128]{1,0:T(4,128)}, u32[]{:S(2)}) copy-start(f32[3,128]{1,0:T(4,128)} %param.13) | copy-start | bytes 4612
  71.1 9.3 %all-to-all-start.4 = ((f32[32,6,128]{2,1,0:T(8,128)}), f32[32,6,128]{2,1,0:T(8,128)S(1)}, u32[]{:S(2)}, u32[]{:S(2)}) async-start(f32[32,6,128]{2,1,0:T(8,128)} %scatter_fusion.1), calls=%async_computation.4 | async-start | bytes 262144 | tf_op jit(solution)/shard_map/all_to_all | solution.py:75
  85.8 9.0 %all-to-all-start.5 = ((f32[32,3,128]{2,1,0:T(4,128)}), f32[32,3,128]{2,1,0:T(4,128)S(1)}, u32[]{:S(2)}, u32[]{:S(2)}) async-start(f32[32,3,128]{2,1,0:T(4,128)} %copy_add_fusion), calls=%async_computation.5 | async-start | bytes 131072 | tf_op jit(solution)/shard_map/all_to_all | solution.py:123
  96.3 10.6 %collective-permute-start.4 = (f32[3,1,128]{2,0,1:T(4,128)S(1)}, f32[3,1,128]{2,0,1:T(4,128)S(1)}, u32[]{:S(2)}, u32[]{:S(2)}) collective-permute-start(f32[3,1,128]{2,0,1:T(4,128)S(1)} %get-tuple-element.10), channel_id=1, source_target_pairs={{0,4},{4,8},{8,12},{12,16},{16,20},{20,24},{24,28},{1,5},{5,9},{9,... | collective-permute-start | bytes 4616 | tf_op jit(solution)/shard_map/ppermute | solution.py:23
  98.2 8.7 %collective-permute-start.5 = (f32[3,1,128]{2,0,1:T(4,128)S(1)}, f32[3,1,128]{2,0,1:T(4,128)S(1)}, u32[]{:S(2)}, u32[]{:S(2)}) collective-permute-start(f32[3,1,128]{2,0,1:T(4,128)S(1)} %get-tuple-element.13), channel_id=1, source_target_pairs={{4,0},{8,4},{12,8},{16,12},{20,16},{24,20},{28,24},{5,1},{9,5},{13... | collective-permute-start | bytes 4616 | tf_op jit(solution)/shard_map/ppermute | solution.py:24
  102.8 4.2 %collective-permute-start.6 = (f32[3,1,128]{2,0,1:T(4,128)S(1)}, f32[3,1,128]{2,0,1:T(4,128)S(1)}, u32[]{:S(2)}, u32[]{:S(2)}) collective-permute-start(f32[3,1,128]{2,0,1:T(4,128)S(1)} %get-tuple-element.12), channel_id=1, source_target_pairs={{0,1},{1,2},{2,3},{4,5},{5,6},{6,7},{8,9},{9,10},{10,11},{12,13},{... | collective-permute-start | bytes 4616 | tf_op jit(solution)/shard_map/ppermute | solution.py:23
  105.6 5.5 %collective-permute-start.7 = (f32[3,1,128]{2,0,1:T(4,128)S(1)}, f32[3,1,128]{2,0,1:T(4,128)S(1)}, u32[]{:S(2)}, u32[]{:S(2)}) collective-permute-start(f32[3,1,128]{2,0,1:T(4,128)S(1)} %get-tuple-element.11), channel_id=1, source_target_pairs={{1,0},{2,1},{3,2},{5,4},{6,5},{7,6},{9,8},{10,9},{11,10},{13,12},{... | collective-permute-start | bytes 4616 | tf_op jit(solution)/shard_map/ppermute | solution.py:24
where the time goes:
time: 113 us; the launch traced here: 112 us
  starting transfers between devices  44.5 us (39%)
  waiting for transfers between devices  32.8 us (29%)
  matrix products  17 us (15%)
  local copies, waits for them, and re-layouts  8.75 us (8%)
  other arithmetic  7.28 us (6%)
  between operations  1.66 us (1%)
    ppermute x4, starting transfers between devices, with_halo(): after = lax.ppermute(first, axis, down)  11.7 us
    all_to_all x2, waiting for transfers between devices, send_full(): lax.all_to_all(packed, 'my', split_axis=0, concat_axis=0, tiled=True)  10.9 us
    all_to_all x2, waiting for transfers between devices, body(): lax.all_to_all(returned, 'my', split_axis=0, concat_axis=0, tiled=True)  10.8 us
    ppermute x4, starting transfers between devices, with_halo(): before = lax.ppermute(last, axis, up)  9.49 us
    ppermute x4, waiting for transfers between devices, with_halo(): after = lax.ppermute(first, axis, down)  8.28 us
    all_to_all x2, starting transfers between devices, send_full(): lax.all_to_all(packed, 'my', split_axis=0, concat_axis=0, tiled=True)  6.78 us
    all_to_all x2, starting transfers between devices, body(): lax.all_to_all(returned, 'my', split_axis=0, concat_axis=0, tiled=True)  6.56 us
    all_to_all x1, starting transfers between devices, send_full(): lax.all_to_all(pair_values, 'my', split_axis=0, concat_axis=0, tiled=True)  5.1 us
  transfers between devices with their start and end apart: 14, of which 7 were waited for; matrix products, arithmetic and copies ran while one was open for 10% of the time, Pallas kernels for 0%

commit v1 on v0

v1 whole, which is shorter than its diff:
```python
import functools

import jax
import jax.numpy as jnp
from jax import lax
from jax.experimental import pallas as pl
from jax.experimental.pallas import tpu as pltpu
from jax.sharding import PartitionSpec as P

STEPS = 2

time_step = 0.1
penalty = 4.0
damping = 0.5
contact_reach = 4.0
exact = lax.Precision.HIGHEST
LANES = 128
TILE = 8
ROW_MASS, ROW_SPEED, ROW_OWNER, ROW_ELASTIC, ROW_LISTS, ROW_PATCH = 3, 4, 7, 8, 12, 16


def pick(rows, indices):
    return jnp.take_along_axis(rows, indices, axis=1)


def spots(row):
    nodes = lax.broadcasted_iota(jnp.int32, (LANES, row.shape[1]), 0)
    return jnp.where(nodes == row, 1.0, 0.0).astype(jnp.bfloat16)


def put_parts(parts_ref, values, rows, base=0):
    for c, value in enumerate(values):
        high = value.astype(jnp.bfloat16).astype(jnp.float32)
        parts_ref[base + c * rows : base + (c + 1) * rows, :] = high
        parts_ref[base + (4 + c) * rows : base + (5 + c) * rows, :] = value - high


def fold(product):
    turned = product.T
    return turned + pltpu.roll(turned, 4, 0)


def scatter(hot, weights):
    return fold(
        lax.dot_general(hot, weights, (((1,), (1,)), ((), ())), preferred_element_type=jnp.float32)
    )


def tile_parts(tile):
    high = tile.astype(jnp.bfloat16).astype(jnp.float32)
    rest = pltpu.roll(tile - high, 4, 0)
    row = lax.broadcasted_iota(jnp.int32, tile.shape, 0)
    return jnp.where(row < 4, high, rest).astype(jnp.bfloat16)


def elastic_terms(place, rest, connect, modulus, stiffness, parts_ref, hot_ref, weight_ref):
    corners, count = connect.shape
    moved = place - rest
    local = jnp.concatenate(
        [
            jnp.concatenate(
                [
                    pick(
                        jnp.broadcast_to(moved[c : c + 1], (corners, LANES)),
                        connect[:, k * LANES : (k + 1) * LANES],
                    )
                    for k in range(count // LANES)
                ],
                axis=1,
            )
            for c in range(3)
        ],
        axis=0,
    )
    product = jnp.dot(stiffness, local, precision=exact, preferred_element_type=jnp.float32)
    forces = -modulus * product
    for k in range(count // LANES):
        put_parts(
            parts_ref,
            [forces[c * corners : (c + 1) * corners, k * LANES : (k + 1) * LANES] for c in range(3)],
            corners,
            k * TILE * corners,
        )
    for a in range(corners):
        span = pl.ds(a * count, count)
        hot_ref[:, span] = spots(connect[a : a + 1])
        for k in range(count // LANES):
            weight_ref[:, pl.ds(a * count + k * LANES, LANES)] = parts_ref[
                pl.ds(k * TILE * corners + a, TILE, stride=corners), :
            ].astype(jnp.bfloat16)


def pair_forces(mine, partner):
    offset = [b - a for a, b in zip(mine[:3], partner[:3])]
    distance = offset[0] * offset[0] + offset[1] * offset[1] + offset[2] * offset[2]
    weight = jnp.exp(-distance / contact_reach)
    return [
        -penalty * weight * o + damping * weight * (b - a)
        for o, a, b in zip(offset, mine[3:], partner[3:])
    ]


def choose(rows, device):
    chosen = jnp.broadcast_to(rows[0], device.shape)
    for d, row in enumerate(rows[1:], 1):
        chosen = jnp.where(device == d, row, chosen)
    return chosen


def pack_kernel(
    place_ref, speed_ref, rest_ref, mass_ref, connect_ref, modulus_ref, stiff_ref, lists_ref, patch_ref, owner_ref,
    map_ref, out_ref, parts_ref, hot_ref, weight_ref,
):
    patches = patch_ref.shape[0]
    elastic_terms(
        place_ref[...], rest_ref[...], connect_ref[...], modulus_ref[...], stiff_ref[...], parts_ref, hot_ref, weight_ref
    )
    out_ref[ROW_ELASTIC : ROW_ELASTIC + TILE, :] = scatter(hot_ref[...], weight_ref[...])
    out_ref[0:3, :] = place_ref[...]
    out_ref[ROW_MASS : ROW_MASS + 1, :] = mass_ref[...]
    out_ref[ROW_SPEED : ROW_SPEED + 3, :] = speed_ref[...]
    out_ref[ROW_OWNER : ROW_OWNER + 1, :] = jnp.zeros((1, LANES), jnp.float32)
    out_ref[ROW_OWNER : ROW_OWNER + 1, 0:patches] = owner_ref[...].astype(jnp.float32)
    out_ref[ROW_LISTS : ROW_LISTS + 4, :] = lists_ref[...].astype(jnp.float32)
    out_ref[ROW_PATCH : ROW_PATCH + patches, :] = patch_ref[...].astype(jnp.float32)
    out_ref[ROW_PATCH + patches :, :] = map_ref[...].astype(jnp.float32)


def row_kernel(width, patches, row_ref, total_ref, pair_ref, other_ref, table_ref, parts_ref, back_ref, idx_ref, hot_ref, weight_ref):
    me = lax.axis_index("my")
    side = lax.rem(lax.axis_index("mx"), 2)
    count = width * patches
    slot = [jnp.bitwise_xor(me, u) for u in range(width)]
    state = [row_ref[slot[u], 0:TILE, :] for u in range(width)]
    nodes = jnp.concatenate([row_ref[slot[u], ROW_PATCH : ROW_PATCH + patches, :] for u in range(width)], axis=0)
    pairs = jnp.concatenate([row_ref[slot[u], ROW_PATCH + patches :, :] for u in range(width)], axis=0)
    lane = lax.broadcasted_iota(jnp.int32, (patches, LANES), 1)
    line = lax.broadcasted_iota(jnp.int32, (patches, LANES), 0)
    owner_col = jnp.concatenate(
        [
            jnp.sum(jnp.where(lane == line, state[u][ROW_OWNER : ROW_OWNER + 1], 0.0), axis=1, keepdims=True)
            for u in range(width)
        ],
        axis=0,
    )
    p = lax.broadcasted_iota(jnp.int32, (count, count), 0).astype(jnp.float32)
    q = lax.broadcasted_iota(jnp.int32, (count, count), 1).astype(jnp.float32)
    owner_row = jnp.sum(jnp.where(p == q, owner_col, 0.0), axis=0, keepdims=True)
    same = owner_col == owner_row
    after = jnp.min(jnp.where(same, jnp.where(q > p, q, q + count), 3.0 * count), axis=1, keepdims=True)
    after = jnp.where(after >= count, after - count, after)
    before = jnp.max(jnp.where(same, jnp.where(q < p, q + count, q), -1.0), axis=1, keepdims=True)
    before = jnp.where(before >= count, before - count, before)
    link = jnp.where(q == after, 1.0, 0.0).astype(jnp.bfloat16)
    back = jnp.where(q == before, 1.0, 0.0).astype(jnp.bfloat16)

    def route(table, rows):
        return jnp.dot(table, rows.astype(jnp.bfloat16), preferred_element_type=jnp.float32)

    target = pick(route(link, nodes), pairs.astype(jnp.int32))
    device = jnp.broadcast_to(jnp.floor(after / patches), (count, LANES))
    node_ids, target_ids = nodes.astype(jnp.int32), target.astype(jnp.int32)
    device_ids = device.astype(jnp.int32)
    mine, partner = [], []
    for c in (0, 1, 2, 4, 5, 6):
        rows = [state[u][c : c + 1] for u in range(width)]
        own = jnp.concatenate([jnp.broadcast_to(row, (patches, LANES)) for row in rows], axis=0)
        mine.append(pick(own, node_ids))
        partner.append(pick(choose(rows, device_ids), target_ids))
    forces = pair_forces(mine, partner)
    put_parts(parts_ref, forces, count)
    for g in (0, 1, 2, 4, 5, 6):
        back_ref[g * count : (g + 1) * count, :] = -route(back, parts_ref[g * count : (g + 1) * count, :])
    landing = route(back, target)
    from_nodes = route(back, nodes)
    idx_ref[0:count, :] = node_ids
    idx_ref[count : 2 * count, :] = landing.astype(jnp.int32)
    idx_ref[2 * count : 3 * count, :] = target_ids
    idx_ref[3 * count : 4 * count, :] = from_nodes.astype(jnp.int32)
    idx_ref[4 * count : 5 * count, :] = device_ids
    idx_ref[5 * count : 6 * count, :] = jnp.broadcast_to(jnp.floor(before / patches), (count, LANES)).astype(jnp.int32)
    for g in range(6):
        table_ref[g * patches : (g + 1) * patches, :] = idx_ref[pl.ds(g * count + me * patches, patches), :]

    def unit(u):
        for s in range(patches):
            at = u * patches + s
            hot_ref[:, s * LANES : (s + 1) * LANES] = spots(idx_ref[pl.ds(at, 1), :])
            weight_ref[:, s * LANES : (s + 1) * LANES] = parts_ref[pl.ds(at, TILE, stride=count), :].astype(jnp.bfloat16)
            far = patches + s
            hot_ref[:, far * LANES : (far + 1) * LANES] = spots(idx_ref[pl.ds(count + at, 1), :])
            weight_ref[:, far * LANES : (far + 1) * LANES] = back_ref[pl.ds(at, TILE, stride=count), :].astype(jnp.bfloat16)
        place = jnp.bitwise_xor(me, u)
        info = row_ref[place, ROW_ELASTIC : ROW_ELASTIC + TILE, :]
        total = scatter(hot_ref[...], weight_ref[...]) + info
        total_ref[u] = total
        lists = info.astype(jnp.int32)
        low = pick(total, jnp.broadcast_to(lists[4:5], (TILE, LANES)))
        high = pick(total, jnp.broadcast_to(lists[5:6], (TILE, LANES)))
        pair_ref[u] = jnp.where(side == 0, high, low)[0:4]
        other_ref[u] = jnp.where(side == 0, low, high)[0:4]

    if width <= 4:
        for u in range(width):
            unit(u)
    else:
        lax.fori_loop(0, width, lambda u, carry: (unit(u), carry)[1], 0)


def faces(tiles, lists, hot_ref, weight_ref):
    for k, tile in enumerate(tiles):
        hot_ref[:, k * LANES : (k + 1) * LANES] = spots(lists[k])
        weight_ref[:, k * LANES : (k + 1) * LANES] = tile_parts(tile)
    return scatter(hot_ref[:, 0 : len(tiles) * LANES], weight_ref[:, 0 : len(tiles) * LANES])


def step_kernel(
    width, patches, row_ref, total_ref, pair_ref, other_ref, table_ref, rest_ref, connect_ref, modulus_ref, stiff_ref,
    state_ref, near_ref, send_ref, next_ref, fparts_ref, parts_ref, hot_ref, weight_ref,
):
    me = lax.axis_index("my")
    side = lax.rem(lax.axis_index("mx"), 2)
    blank = jnp.zeros((4, LANES), jnp.float32)

    def unit(u):
        info = row_ref[jnp.bitwise_xor(me, u), 0 : 2 * TILE, :]
        lists = info[TILE:].astype(jnp.int32)
        lower, upper = lists[4:5], lists[5:6]
        down, up = jnp.maximum(u - 1, 0), jnp.minimum(u + 1, width - 1)
        down_list = row_ref[jnp.bitwise_xor(me, down), ROW_LISTS + 3 : ROW_LISTS + 4, :].astype(jnp.int32)
        up_list = row_ref[jnp.bitwise_xor(me, up), ROW_LISTS + 2 : ROW_LISTS + 3, :].astype(jnp.int32)
        low = pick(total_ref[down], jnp.broadcast_to(down_list, (TILE, LANES)))
        high = pick(total_ref[up], jnp.broadcast_to(up_list, (TILE, LANES)))
        low = jnp.where(u > 0, low, 0.0)
        high = jnp.where(u < width - 1, high, 0.0)
        tiles = [
            jnp.concatenate([pair_ref[u], blank], axis=0),
            jnp.concatenate([other_ref[u], blank], axis=0),
            low,
            high,
        ]
        near, far = jnp.where(side == 0, upper, lower), jnp.where(side == 0, lower, upper)
        total = total_ref[u] + faces(tiles, [near, far, lists[6:7], lists[7:8]], hot_ref, weight_ref)
        speed = info[ROW_SPEED : ROW_SPEED + 3] + time_step * info[ROW_MASS : ROW_MASS + 1] * total[0:3]
        next_ref[u, 0:3, :] = info[0:3] + time_step * speed
        next_ref[u, 4:7, :] = speed

    if width <= 4:
        for u in range(width):
            unit(u)
    else:
        lax.fori_loop(0, width, lambda u, carry: (unit(u), carry)[1], 0)

    own = next_ref[me]
    state_ref[...] = own
    table = [table_ref[g * patches : (g + 1) * patches, :] for g in range(6)]
    nodes, landing, target, from_nodes, to_device, from_device = table
    first, second = [], []
    for c in (0, 1, 2, 4, 5, 6):
        rows = [next_ref[u, c : c + 1, :] for u in range(width)]
        home = jnp.broadcast_to(own[c : c + 1], (patches, LANES))
        first.append(jnp.concatenate([pick(home, nodes), pick(choose(rows, from_device), from_nodes)], axis=0))
        second.append(jnp.concatenate([pick(choose(rows, to_device), target), pick(home, landing)], axis=0))
    forces = pair_forces(first, second)
    sign = jnp.where(lax.broadcasted_iota(jnp.int32, (2 * patches, LANES), 0) < patches, 1.0, -1.0)
    put_parts(parts_ref, [sign * f for f in forces], 2 * patches)
    elastic_terms(
        own[0:3], rest_ref[...], connect_ref[...], modulus_ref[...], stiff_ref[...], fparts_ref, hot_ref, weight_ref
    )
    base = connect_ref.shape[0] * connect_ref.shape[1]
    for s in range(2 * patches):
        span = pl.ds(base + s * LANES, LANES)
        hot_ref[:, span] = spots(table_ref[s : s + 1, :])
        weight_ref[:, span] = parts_ref[pl.ds(s, TILE, stride=2 * patches), :].astype(jnp.bfloat16)
    total = scatter(hot_ref[...], weight_ref[...])
    near_ref[...] = total
    lists = row_ref[0, ROW_ELASTIC : ROW_ELASTIC + TILE, :].astype(jnp.int32)
    sides = [pick(total, jnp.broadcast_to(lists[4 + k : 5 + k], (TILE, LANES))) for k in range(4)]
    even = lax.rem(me, 2) == 0
    send_ref[0] = jnp.where(side == 0, sides[1], sides[0])
    send_ref[1] = jnp.where(side == 0, sides[0], sides[1])
    send_ref[2] = jnp.where(even, sides[3], sides[2])
    send_ref[3] = jnp.where(even, sides[2], sides[3])


def end_kernel(row_ref, state_ref, near_ref, *refs):
    in_refs, (place_ref, speed_ref, hot_ref, weight_ref) = refs[:4], refs[4:]
    side = lax.rem(lax.axis_index("mx"), 2)
    even = lax.rem(lax.axis_index("my"), 2)
    lists = row_ref[0, ROW_ELASTIC : ROW_ELASTIC + TILE, :].astype(jnp.int32)
    order = [
        jnp.where(side == 0, lists[5:6], lists[4:5]),
        jnp.where(side == 0, lists[4:5], lists[5:6]),
        jnp.where(even == 0, lists[7:8], lists[6:7]),
        jnp.where(even == 0, lists[6:7], lists[7:8]),
    ]
    total = near_ref[...] + faces([ref[...] for ref in in_refs], order, hot_ref, weight_ref)
    mass = row_ref[0, ROW_MASS : ROW_MASS + 1, :]
    speed = state_ref[4:7, :] + time_step * mass * total[0:3]
    speed_ref[...] = speed
    place_ref[...] = state_ref[0:3, :] + time_step * speed


def call(kernel, name, outs, scratch, *args):
    return pl.pallas_call(
        kernel,
        name=name,
        out_shape=[jax.ShapeDtypeStruct(shape, jnp.dtype(kind)) for shape, kind in outs],
        in_specs=[pl.BlockSpec(memory_space=pltpu.VMEM)] * len(args),
        out_specs=[pl.BlockSpec(memory_space=pltpu.VMEM)] * len(outs),
        scratch_shapes=[pltpu.VMEM(shape, kind) for shape, kind in scratch],
    )(*args)


def swap(value, axis, first):
    size = lax.axis_size(axis)
    pairs = [(i, i + 1) for i in range(first, size - 1, 2)]
    return lax.ppermute(value, axis, pairs + [(j, i) for i, j in pairs])


def gather_row(record, axis):
    size = lax.axis_size(axis)
    held = record[None]
    step = size // 2
    while step:
        other = lax.ppermute(held, axis, [(i, i ^ step) for i in range(size)])
        held = jnp.stack([held, other], axis=1).reshape((-1,) + record.shape)
        step //= 2
    return held


def body(
    positions, velocities, rest_positions, inverse_mass, element_nodes, modulus, stiffness, shared_lists, patch_nodes,
    patch_owner, pair_map,
):
    width = lax.axis_size("my")
    patches = patch_owner.shape[0]
    corners, elements = element_nodes.shape
    count = width * patches
    spread = corners * elements
    f32, i32, bf16 = jnp.float32, jnp.int32, jnp.bfloat16
    modulus, mass = modulus[None], inverse_mass[None]
    (record,) = call(
        pack_kernel,
        "pack",
        [((ROW_PATCH + 2 * patches, LANES), f32)],
        [((TILE * corners * elements // LANES, LANES), f32), ((LANES, spread), bf16), ((TILE, spread), bf16)],
        positions, velocities, rest_positions, mass, element_nodes, modulus, stiffness, shared_lists, patch_nodes,
        patch_owner[None], pair_map,
    )
    row = gather_row(record, "my")
    total, pair, other, table = call(
        functools.partial(row_kernel, width, patches),
        "row",
        [((width, TILE, LANES), f32), ((width, 4, LANES), f32), ((width, 4, LANES), f32), ((6 * patches, LANES), i32)],
        [
            ((TILE * count, LANES), f32),
            ((TILE * count, LANES), f32),
            ((6 * count, LANES), i32),
            ((LANES, 2 * patches * LANES), bf16),
            ((TILE, 2 * patches * LANES), bf16),
        ],
        row,
    )
    pair, other = swap(pair, "mx", 0), swap(other, "mx", 1)
    deep = spread + 2 * patches * LANES
    state, near, send = call(
        functools.partial(step_kernel, width, patches),
        "step",
        [((TILE, LANES), f32), ((TILE, LANES), f32), ((4, TILE, LANES), f32)],
        [
            ((width, TILE, LANES), f32),
            ((TILE * corners * elements // LANES, LANES), f32),
            ((TILE * 2 * patches, LANES), f32),
            ((LANES, deep), bf16),
            ((TILE, deep), bf16),
        ],
        row, total, pair, other, table, rest_positions, element_nodes, modulus, stiffness,
    )
    arrived = [swap(send[k], axis, first) for k, (axis, first) in enumerate((("mx", 0), ("mx", 1), ("my", 0), ("my", 1)))]
    return tuple(
        call(
            end_kernel,
            "end",
            [((3, LANES), f32), ((3, LANES), f32)],
            [((LANES, 4 * LANES), bf16), ((TILE, 4 * LANES), bf16)],
            row, state, near, *arrived,
        )
    )


def solution(mesh):
    in_specs = (
        P(None, ("mx", "my")),
        P(None, ("mx", "my")),
        P(None, ("mx", "my")),
        P(("mx", "my")),
        P(None, ("mx", "my")),
        P(("mx", "my")),
        P(),
        P(None, ("mx", "my")),
        P(("mx", "my"), None),
        P(("mx", "my")),
        P(("mx", "my"), None),
    )
    out_specs = (P(None, ("mx", "my")), P(None, ("mx", "my")))
    return jax.shard_map(body, mesh=mesh, in_specs=in_specs, out_specs=out_specs, check_vma=False)
```

time: 113 us -> 42.3 us (0.37)
  starting transfers between devices: 44.5 us -> 15.4 us
  waiting for transfers between devices: 32.8 us -> 10.6 us
  matrix products: 17 us -> 0 us
  Pallas kernels: 0 us -> 11.9 us
  other arithmetic: 7.28 us -> 0.75 us
  local copies, waits for them, and re-layouts: 8.75 us -> 2.52 us
    all_to_all x6 -> x0, waiting for transfers between devices: 24.5 us -> none  [the longest x2 10.9 us: send_full(): lax.all_to_all(packed, 'my', split_axis=0, concat_axis=0, tiled=True)]
    all_to_all x6 -> x0, starting transfers between devices: 23.3 us -> none  [the longest x2 6.78 us: send_full(): lax.all_to_all(packed, 'my', split_axis=0, concat_axis=0, tiled=True)]
    dot_general x22 -> x0, matrix products: 17 us -> none  [the longest x2 4.75 us: owner_contact(): jnp.einsum('scm,skm->sck', partner_rows, pair_hot, precision=exact)]
    pallas_call x0 -> x4, Pallas kernels: none -> 11.9 us  [call(): pl.pallas_call(kernel, name=name, out_shape=[jax.ShapeDtypeStruct(shape,...]
    ppermute x8, starting transfers between devices: 21.2 us -> 15.4 us  [the longest x6 11.4 us: swap(): return lax.ppermute(value, axis, pairs + [(j, i) for i, j in pairs])]
    scatter x3 -> x0, local copies, waits for them, and re-layouts: 4.66 us -> none  [the longest x2 4.04 us: send_full(): jnp.zeros((slots, 6, members.shape[2]), jnp.float32).at[target_slot]]
    ppermute x8, waiting for transfers between devices: 8.29 us -> 10.6 us  [the longest x6 5.42 us: swap(): return lax.ppermute(value, axis, pairs + [(j, i) for i, j in pairs])]
    reduce_sum x4 -> x0, other arithmetic: 2.21 us -> none  [the longest x1 1.25 us: owner_contact(): total_live = jnp.maximum(jnp.sum(live_flags), 1.0)]
  transfers between devices with their start and end apart: 14 -> 8, of which waited for: 7 -> 4; matrix products, arithmetic and copies ran while one was open for 10% -> 0% of each run, Pallas kernels for 0% -> 0%
where the time goes in v1:
time: 42.3 us; the launch traced here: 41.8 us
  starting transfers between devices  15.4 us (36%)
  Pallas kernels  11.9 us (28%)
  waiting for transfers between devices  10.6 us (25%)
  local copies, waits for them, and re-layouts  2.52 us (6%)
  other arithmetic  0.75 us (2%)
  between operations  0.74 us (2%)
    pallas_call x4, Pallas kernels, call(): pl.pallas_call(kernel, name=name, out_shape=[jax.ShapeDtypeStruct(shape,...  11.9 us
    ppermute x6, starting transfers between devices, swap(): return lax.ppermute(value, axis, pairs + [(j, i) for i, j in pairs])  11.4 us
    ppermute x6, waiting for transfers between devices, swap(): return lax.ppermute(value, axis, pairs + [(j, i) for i, j in pairs])  5.42 us
    ppermute x2, waiting for transfers between devices, gather_row(): other = lax.ppermute(held, axis, [(i, i ^ step) for i in range(size)])  5.14 us
    ppermute x2, starting transfers between devices, gather_row(): other = lax.ppermute(held, axis, [(i, i ^ step) for i in range(size)])  4.02 us
    unnamed x12, local copies, waits for them, and re-layouts  1.17 us
  transfers between devices with their start and end apart: 8, of which 4 were waited for; matrix products, arithmetic and copies ran while one was open for 0% of the time, Pallas kernels for 0%

profile of v1, /device:TPU:4, one launch (start us, length us, event | category | flops | bytes accessed | tf_op | source)
XLA Modules:
  0.0 41.8 jit_solution(18285638687532498594)
XLA Ops:
  0.6 2.0 %pack.1 = f32[48,128]{1,0:T(8,128)} custom-call(f32[3,128]{1,0:T(4,128)} %place_ref.1, f32[3,128]{1,0:T(4,128)} %speed_ref.1, f32[3,128]{1,0:T(4,128)} %rest_ref.3, f32[1,128]{1,0:T(1,128)} %bitcast.29, s32[8,256]{1,0:T(8,128)} %connect_ref.3, f32[1,256]{1,0:T(1,128)} %bitcast.27, f32[24,24]{1,0:T(8,128)} %stiff_ref.3, s32[4,128]{1,0:T(4,128)} %lists_ref.1, ...), custom_call_target="tpu_custom_call" | custom-call | tf_op jit(solution)/shard_map/pack/pallas_call | solution.py:305
  2.7 2.6 %collective-permute-start = (f32[1,48,128]{2,1,0:T(8,128)}, f32[1,48,128]{2,1,0:T(8,128)S(1)}, u32[]{:S(2)}, u32[]{:S(2)}) collective-permute-start(f32[1,48,128]{2,1,0:T(8,128)} %bitcast.23), channel_id=1, source_target_pairs={{0,2},{1,3},{2,0},{3,1},{4,6},{5,7},{6,4},{7,5},{8,10},{9,11},{10,... | collective-permute-start | bytes 73736 | tf_op jit(solution)/shard_map/ppermute | solution.py:326
  5.3 2.5 %collective-permute-done = f32[1,48,128]{2,1,0:T(8,128)S(1)} collective-permute-done((f32[1,48,128]{2,1,0:T(8,128)}, f32[1,48,128]{2,1,0:T(8,128)S(1)}, u32[]{:S(2)}, u32[]{:S(2)}) %collective-permute-start) | collective-permute-done | bytes 24608 | tf_op jit(solution)/shard_map/ppermute | solution.py:326
  7.8 0.7 %fusion.1 = (f32[2,1,48,128]{3,2,0,1:T(8,128)S(1)}, f32[2,48,128]{2,1,0:T(8,128)S(1)}) fusion(f32[1,1,48,128]{3,2,1,0:T(8,128)S(1)} %bitcast.26, f32[1,1,48,128]{3,2,1,0:T(8,128)} %bitcast.24), kind=kLoop, calls=%fused_computation.3 | loop fusion | flops 12288 | bytes 147456 | tf_op jit(solution)/shard_map/stack;reshape | solution.py:327
  8.5 1.4 %collective-permute-start.1 = (f32[2,48,128]{2,1,0:T(8,128)S(1)}, f32[2,48,128]{2,1,0:T(8,128)S(1)}, u32[]{:S(2)}, u32[]{:S(2)}) collective-permute-start(f32[2,48,128]{2,1,0:T(8,128)S(1)} %get-tuple-element.17), channel_id=1, source_target_pairs={{0,1},{1,0},{2,3},{3,2},{4,5},{5,4},{6,7},{7,6},{8,9},{9,8},{10,11... | collective-permute-start | bytes 147464 | tf_op jit(solution)/shard_map/ppermute | solution.py:326
  9.9 2.7 %collective-permute-done.1 = f32[2,48,128]{2,1,0:T(8,128)S(1)} collective-permute-done((f32[2,48,128]{2,1,0:T(8,128)S(1)}, f32[2,48,128]{2,1,0:T(8,128)S(1)}, u32[]{:S(2)}, u32[]{:S(2)}) %collective-permute-start.1) | collective-permute-done | bytes 49184 | tf_op jit(solution)/shard_map/ppermute | solution.py:326
  12.6 0.7 %copy.13 = f32[2,2,48,128]{3,2,1,0:T(8,128)} copy(f32[2,2,48,128]{3,2,0,1:T(8,128)S(1)} %pad_maximum_fusion) | data formatting | bytes 196608 | tf_op jit(solution)/shard_map/stack | solution.py:327
  13.3 4.8 %row.1 = (f32[4,8,128]{2,1,0:T(8,128)}, f32[4,4,128]{2,1,0:T(4,128)}, f32[4,4,128]{2,1,0:T(4,128)}, s32[96,128]{1,0:T(8,128)}) custom-call(f32[4,48,128]{2,1,0:T(8,128)} %bitcast.20), custom_call_target="tpu_custom_call" | custom-call | tf_op jit(solution)/shard_map/row/pallas_call | solution.py:305
  18.1 0.0 collective-permute-start.2
  18.1 3.4 %collective-permute-start.3 = (f32[4,4,128]{2,1,0:T(4,128)}, f32[4,4,128]{2,1,0:T(4,128)S(1)}, u32[]{:S(2)}, u32[]{:S(2)}) collective-permute-start(f32[4,4,128]{2,1,0:T(4,128)} %get-tuple-element.11), channel_id=1, source_target_pairs={{4,8},{12,16},{20,24},{8,4},{16,12},{24,20},{5,9},{13,17},{21,25},... | collective-permute-start | bytes 24584 | tf_op jit(solution)/shard_map/ppermute | solution.py:318
  21.5 0.0 collective-permute-done.2.pair_ref
  21.6 2.6 %collective-permute-done.3.other_ref = f32[4,4,128]{2,1,0:T(4,128)S(1)} collective-permute-done((f32[4,4,128]{2,1,0:T(4,128)}, f32[4,4,128]{2,1,0:T(4,128)S(1)}, u32[]{:S(2)}, u32[]{:S(2)}) %collective-permute-start.3) | collective-permute-done | bytes 8224 | tf_op jit(solution)/shard_map/ppermute | solution.py:318
  24.2 0.6 %copy-done.1 = f32[4,4,128]{2,1,0:T(4,128)} copy-done((f32[4,4,128]{2,1,0:T(4,128)}, f32[4,4,128]{2,1,0:T(4,128)S(1)}, u32[]{:S(2)}) %copy-start.1) | copy-done | bytes 8216
  24.7 3.3 %step.1 = (f32[8,128]{1,0:T(8,128)}, f32[8,128]{1,0:T(8,128)}, f32[4,8,128]{2,1,0:T(8,128)}) custom-call(f32[4,48,128]{2,1,0:T(8,128)} %bitcast.21, f32[4,8,128]{2,1,0:T(8,128)} %get-tuple-element.9.total_ref, f32[4,4,128]{2,1,0:T(4,128)} %copy-done, f32[4,4,128]{2,1,0:T(4,128)} %copy-done.1, s32[96,128]{1,0:T(8,128)} %get-tuple-element.12.table_ref, ...), custom_call_target="tpu_custom_call" | custom-call | tf_op jit(solution)/shard_map/step/pallas_call | solution.py:305
  28.0 0.7 %slice_bitcast_fusion = (f32[8,128]{1,0:T(8,128)S(1)}, f32[8,128]{1,0:T(8,128)S(1)}, f32[8,128]{1,0:T(8,128)S(1)}, f32[8,128]{1,0:T(8,128)S(1)}) fusion(f32[4,8,128]{2,1,0:T(8,128)} %get-tuple-element.15), kind=kLoop, calls=%fused_computation.4 | loop fusion | bytes 32768 | tf_op jit(solution)/shard_map/squeeze | solution.py:380
  28.7 0.7 %collective-permute-start.7 = (f32[8,128]{1,0:T(8,128)S(1)}, f32[8,128]{1,0:T(8,128)S(1)}, u32[]{:S(2)}, u32[]{:S(2)}) collective-permute-start(f32[8,128]{1,0:T(8,128)S(1)} %get-tuple-element.18), channel_id=1, source_target_pairs={{1,2},{2,1},{5,6},{6,5},{9,10},{10,9},{13,14},{14,13},{17,18},{18,... | collective-permute-start | bytes 12296 | tf_op jit(solution)/shard_map/ppermute | solution.py:318
  29.4 4.3 %collective-permute-start.6 = (f32[8,128]{1,0:T(8,128)S(1)}, f32[8,128]{1,0:T(8,128)S(1)}, u32[]{:S(2)}, u32[]{:S(2)}) collective-permute-start(f32[8,128]{1,0:T(8,128)S(1)} %get-tuple-element.19), channel_id=1, source_target_pairs={{0,1},{2,3},{1,0},{3,2},{4,5},{6,7},{5,4},{7,6},{8,9},{10,11},{9,8... | collective-permute-start | bytes 12296 | tf_op jit(solution)/shard_map/ppermute | solution.py:318
  33.7 2.9 %collective-permute-start.5 = (f32[8,128]{1,0:T(8,128)S(1)}, f32[8,128]{1,0:T(8,128)S(1)}, u32[]{:S(2)}, u32[]{:S(2)}) collective-permute-start(f32[8,128]{1,0:T(8,128)S(1)} %get-tuple-element.20), channel_id=1, source_target_pairs={{4,8},{12,16},{20,24},{8,4},{16,12},{24,20},{5,9},{13,17},{21,25},... | collective-permute-start | bytes 12296 | tf_op jit(solution)/shard_map/ppermute | solution.py:318
  36.6 0.1 collective-permute-start.4
  36.7 0.0 collective-permute-done.7.refs_3_
  36.7 0.0 collective-permute-done.6.refs_2_
  36.7 2.8 %collective-permute-done.5.refs_1_ = f32[8,128]{1,0:T(8,128)S(1)} collective-permute-done((f32[8,128]{1,0:T(8,128)S(1)}, f32[8,128]{1,0:T(8,128)S(1)}, u32[]{:S(2)}, u32[]{:S(2)}) %collective-permute-start.5) | collective-permute-done | bytes 4128 | tf_op jit(solution)/shard_map/ppermute | solution.py:318
  39.5 0.6 %copy-done.4 = f32[8,128]{1,0:T(8,128)} copy-done((f32[8,128]{1,0:T(8,128)}, f32[8,128]{1,0:T(8,128)S(1)}, u32[]{:S(2)}) %copy-start.4) | copy-done | bytes 4120
  40.1 1.7 %end.1 = (f32[3,128]{1,0:T(4,128)}, f32[3,128]{1,0:T(4,128)}) custom-call(f32[4,48,128]{2,1,0:T(8,128)} %bitcast.22, f32[8,128]{1,0:T(8,128)} %get-tuple-element.13.state_ref, f32[8,128]{1,0:T(8,128)} %get-tuple-element.14.near_ref, f32[8,128]{1,0:T(8,128)} %copy-done.5, f32[8,128]{1,0:T(8,128)} %copy-done.4, f32[8,128]{1,0:T(8,128)} %copy-done.3, ...), custom_call_target="tpu_custom_call" | custom-call | tf_op jit(solution)/shard_map/end/pallas_call | solution.py:305
  (12 shorter events, 0.0 us)
Async XLA Ops:
  2.7 5.1 %collective-permute-start = (f32[1,48,128]{2,1,0:T(8,128)}, f32[1,48,128]{2,1,0:T(8,128)S(1)}, u32[]{:S(2)}, u32[]{:S(2)}) collective-permute-start(f32[1,48,128]{2,1,0:T(8,128)} %bitcast.23), channel_id=1, source_target_pairs={{0,2},{1,3},{2,0},{3,1},{4,6},{5,7},{6,4},{7,5},{8,10},{9,11},{10,... | collective-permute-start | bytes 73736 | tf_op jit(solution)/shard_map/ppermute | solution.py:326
  8.5 4.1 %collective-permute-start.1 = (f32[2,48,128]{2,1,0:T(8,128)S(1)}, f32[2,48,128]{2,1,0:T(8,128)S(1)}, u32[]{:S(2)}, u32[]{:S(2)}) collective-permute-start(f32[2,48,128]{2,1,0:T(8,128)S(1)} %get-tuple-element.17), channel_id=1, source_target_pairs={{0,1},{1,0},{2,3},{3,2},{4,5},{5,4},{6,7},{7,6},{8,9},{9,8},{10,11... | collective-permute-start | bytes 147464 | tf_op jit(solution)/shard_map/ppermute | solution.py:326
  18.1 3.5 %collective-permute-start.2 = (f32[4,4,128]{2,1,0:T(4,128)}, f32[4,4,128]{2,1,0:T(4,128)S(1)}, u32[]{:S(2)}, u32[]{:S(2)}) collective-permute-start(f32[4,4,128]{2,1,0:T(4,128)} %get-tuple-element.10), channel_id=1, source_target_pairs={{0,4},{8,12},{16,20},{24,28},{4,0},{12,8},{20,16},{28,24},{1,5},{9... | collective-permute-start | bytes 24584 | tf_op jit(solution)/shard_map/ppermute | solution.py:318
  18.1 6.1 %collective-permute-start.3 = (f32[4,4,128]{2,1,0:T(4,128)}, f32[4,4,128]{2,1,0:T(4,128)S(1)}, u32[]{:S(2)}, u32[]{:S(2)}) collective-permute-start(f32[4,4,128]{2,1,0:T(4,128)} %get-tuple-element.11), channel_id=1, source_target_pairs={{4,8},{12,16},{20,24},{8,4},{16,12},{24,20},{5,9},{13,17},{21,25},... | collective-permute-start | bytes 24584 | tf_op jit(solution)/shard_map/ppermute | solution.py:318
  21.5 2.6 %copy-start = (f32[4,4,128]{2,1,0:T(4,128)}, f32[4,4,128]{2,1,0:T(4,128)S(1)}, u32[]{:S(2)}) copy-start(f32[4,4,128]{2,1,0:T(4,128)S(1)} %collective-permute-done.2.pair_ref) | copy-start | bytes 24580
  24.2 0.6 %copy-start.1 = (f32[4,4,128]{2,1,0:T(4,128)}, f32[4,4,128]{2,1,0:T(4,128)S(1)}, u32[]{:S(2)}) copy-start(f32[4,4,128]{2,1,0:T(4,128)S(1)} %collective-permute-done.3.other_ref) | copy-start | bytes 24580
  28.7 8.0 %collective-permute-start.7 = (f32[8,128]{1,0:T(8,128)S(1)}, f32[8,128]{1,0:T(8,128)S(1)}, u32[]{:S(2)}, u32[]{:S(2)}) collective-permute-start(f32[8,128]{1,0:T(8,128)S(1)} %get-tuple-element.18), channel_id=1, source_target_pairs={{1,2},{2,1},{5,6},{6,5},{9,10},{10,9},{13,14},{14,13},{17,18},{18,... | collective-permute-start | bytes 12296 | tf_op jit(solution)/shard_map/ppermute | solution.py:318
  29.4 7.3 %collective-permute-start.6 = (f32[8,128]{1,0:T(8,128)S(1)}, f32[8,128]{1,0:T(8,128)S(1)}, u32[]{:S(2)}, u32[]{:S(2)}) collective-permute-start(f32[8,128]{1,0:T(8,128)S(1)} %get-tuple-element.19), channel_id=1, source_target_pairs={{0,1},{2,3},{1,0},{3,2},{4,5},{6,7},{5,4},{7,6},{8,9},{10,11},{9,8... | collective-permute-start | bytes 12296 | tf_op jit(solution)/shard_map/ppermute | solution.py:318
  33.7 5.8 %collective-permute-start.5 = (f32[8,128]{1,0:T(8,128)S(1)}, f32[8,128]{1,0:T(8,128)S(1)}, u32[]{:S(2)}, u32[]{:S(2)}) collective-permute-start(f32[8,128]{1,0:T(8,128)S(1)} %get-tuple-element.20), channel_id=1, source_target_pairs={{4,8},{12,16},{20,24},{8,4},{16,12},{24,20},{5,9},{13,17},{21,25},... | collective-permute-start | bytes 12296 | tf_op jit(solution)/shard_map/ppermute | solution.py:318
  36.6 2.9 %collective-permute-start.4 = (f32[8,128]{1,0:T(8,128)S(1)}, f32[8,128]{1,0:T(8,128)S(1)}, u32[]{:S(2)}, u32[]{:S(2)}) collective-permute-start(f32[8,128]{1,0:T(8,128)S(1)} %get-tuple-element.21), channel_id=1, source_target_pairs={{0,4},{8,12},{16,20},{24,28},{4,0},{12,8},{20,16},{28,24},{1,5},{9... | collective-permute-start | bytes 12296 | tf_op jit(solution)/shard_map/ppermute | solution.py:318
  36.7 2.9 %copy-start.2 = (f32[8,128]{1,0:T(8,128)}, f32[8,128]{1,0:T(8,128)S(1)}, u32[]{:S(2)}) copy-start(f32[8,128]{1,0:T(8,128)S(1)} %collective-permute-done.7.refs_3_) | copy-start | bytes 12292
  36.7 2.8 %copy-start.3 = (f32[8,128]{1,0:T(8,128)}, f32[8,128]{1,0:T(8,128)S(1)}, u32[]{:S(2)}) copy-start(f32[8,128]{1,0:T(8,128)S(1)} %collective-permute-done.6.refs_2_) | copy-start | bytes 12292
  39.5 0.6 %copy-start.4 = (f32[8,128]{1,0:T(8,128)}, f32[8,128]{1,0:T(8,128)S(1)}, u32[]{:S(2)}) copy-start(f32[8,128]{1,0:T(8,128)S(1)} %collective-permute-done.5.refs_1_) | copy-start | bytes 12292
  39.5 0.6 %copy-start.5 = (f32[8,128]{1,0:T(8,128)}, f32[8,128]{1,0:T(8,128)S(1)}, u32[]{:S(2)}) copy-start(f32[8,128]{1,0:T(8,128)S(1)} %collective-permute-done.4.refs_0_) | copy-start | bytes 12292

commit v2 on v1

v2 whole, which is shorter than its diff:
```python
import functools

import jax
import jax.numpy as jnp
from jax import lax
from jax.experimental import pallas as pl
from jax.experimental.pallas import tpu as pltpu
from jax.sharding import PartitionSpec as P

STEPS = 2

time_step = 0.1
penalty = 4.0
damping = 0.5
contact_reach = 4.0
LANES = 128
TILE = 8
FINE = 32
ROW_MASS, ROW_SPEED, ROW_OWNER, ROW_ELASTIC, ROW_LISTS, ROW_PATCH = 3, 4, 7, 8, 12, 16


def pick(rows, indices):
    return jnp.take_along_axis(rows, indices, axis=1)


def parted(indices):
    coarse = jnp.floor(indices * (1.0 / FINE))
    return coarse, indices - FINE * coarse


def put_parts(parts_ref, values, base=0):
    for c, value in enumerate(values):
        high = value.astype(jnp.bfloat16).astype(jnp.float32)
        rest = value - high
        for b in range(value.shape[0] // TILE):
            at = base + b * TILE * TILE
            parts_ref[at + c * TILE : at + (c + 1) * TILE, :] = high[b * TILE : (b + 1) * TILE]
            parts_ref[at + (4 + c) * TILE : at + (5 + c) * TILE, :] = rest[b * TILE : (b + 1) * TILE]


def get_parts(parts_ref, row):
    if isinstance(row, int):
        start = row // TILE * TILE * TILE + row % TILE
    else:
        start = lax.div(row, TILE) * (TILE * TILE) + lax.rem(row, TILE)
    return parts_ref[pl.ds(start, TILE, stride=TILE), :]


def scatter(entries):
    blocks = LANES // FINE
    total = jnp.zeros((blocks * TILE, FINE), jnp.float32)
    for coarse, fine, weights in entries:
        wide = weights.shape[1]
        shape = (blocks * TILE, wide)
        block = (lax.broadcasted_iota(jnp.int32, shape, 0) // TILE).astype(jnp.float32).astype(jnp.bfloat16)
        placed = jnp.where(
            jnp.broadcast_to(coarse, shape).astype(jnp.bfloat16) == block,
            jnp.concatenate([weights] * blocks, axis=0).astype(jnp.bfloat16),
            jnp.zeros(shape, jnp.bfloat16),
        )
        shape = (FINE, wide)
        node = lax.broadcasted_iota(jnp.int32, shape, 0).astype(jnp.float32).astype(jnp.bfloat16)
        hot = jnp.where(
            jnp.broadcast_to(fine, shape).astype(jnp.bfloat16) == node,
            jnp.ones(shape, jnp.bfloat16),
            jnp.zeros(shape, jnp.bfloat16),
        )
        total += lax.dot_general(placed, hot, (((1,), (1,)), ((), ())), preferred_element_type=jnp.float32)
    tile = jnp.concatenate([total[b * TILE : (b + 1) * TILE] for b in range(blocks)], axis=1)
    return tile + pltpu.roll(tile, 4, 0)


def joined(entries):
    return [
        tuple(jnp.concatenate([a, b], axis=1) for a, b in zip(*two)) for two in zip(entries[0::2], entries[1::2])
    ]


def tile_parts(tile):
    high = tile.astype(jnp.bfloat16).astype(jnp.float32)
    rest = pltpu.roll(tile - high, 4, 0)
    row = lax.broadcasted_iota(jnp.int32, tile.shape, 0)
    return jnp.where(row < 4, high, rest)


def product(left, right):
    def parts(x):
        high = x.astype(jnp.bfloat16)
        return high, (x - high.astype(jnp.float32)).astype(jnp.bfloat16)

    (lh, lr), (rh, rr) = parts(left), parts(right)
    return sum(jnp.dot(a, b, preferred_element_type=jnp.float32) for a, b in ((lh, rh), (lr, rh), (lh, rr)))


def elastic_terms(place, rest, connect, modulus, stiffness, parts_ref):
    corners, count = connect.shape
    moved = place - rest
    local = jnp.concatenate(
        [
            jnp.concatenate(
                [
                    pick(
                        jnp.broadcast_to(moved[c : c + 1], (corners, LANES)),
                        connect[:, k * LANES : (k + 1) * LANES],
                    )
                    for k in range(count // LANES)
                ],
                axis=1,
            )
            for c in range(3)
        ],
        axis=0,
    )
    forces = -modulus * product(stiffness, local)
    for k in range(count // LANES):
        put_parts(
            parts_ref,
            [forces[c * corners : (c + 1) * corners, k * LANES : (k + 1) * LANES] for c in range(3)],
            k * corners * TILE,
        )
    coarse, fine = parted(connect.astype(jnp.float32))
    return [
        (
            coarse[a : a + 1],
            fine[a : a + 1],
            jnp.concatenate([get_parts(parts_ref, k * corners + a) for k in range(count // LANES)], axis=1),
        )
        for a in range(corners)
    ]


def pair_forces(mine, partner):
    offset = [b - a for a, b in zip(mine[:3], partner[:3])]
    distance = offset[0] * offset[0] + offset[1] * offset[1] + offset[2] * offset[2]
    weight = jnp.exp(-distance / contact_reach)
    return [
        -penalty * weight * o + damping * weight * (b - a)
        for o, a, b in zip(offset, mine[3:], partner[3:])
    ]


def choose(rows, device):
    chosen = jnp.broadcast_to(rows[0], device.shape)
    for d, row in enumerate(rows[1:], 1):
        chosen = jnp.where(device == d, row, chosen)
    return chosen


def pack_kernel(
    place_ref, speed_ref, rest_ref, mass_ref, connect_ref, modulus_ref, stiff_ref, lists_ref, patch_ref, owner_ref,
    map_ref, out_ref, *refs,
):
    patches = patch_ref.shape[0]
    keep_refs, (parts_ref,) = refs[:-1], refs[-1:]
    for keep_ref, ref in zip(keep_refs, (rest_ref, connect_ref, modulus_ref, stiff_ref)):
        keep_ref[...] = ref[...].astype(jnp.float32)
    out_ref[ROW_ELASTIC : ROW_ELASTIC + TILE, :] = scatter(
        elastic_terms(place_ref[...], rest_ref[...], connect_ref[...], modulus_ref[...], stiff_ref[...], parts_ref)
    )
    out_ref[0:3, :] = place_ref[...]
    out_ref[ROW_MASS : ROW_MASS + 1, :] = mass_ref[...]
    out_ref[ROW_SPEED : ROW_SPEED + 3, :] = speed_ref[...]
    out_ref[ROW_OWNER : ROW_OWNER + 1, :] = jnp.zeros((1, LANES), jnp.float32)
    out_ref[ROW_OWNER : ROW_OWNER + 1, 0:patches] = owner_ref[...].astype(jnp.float32)
    out_ref[ROW_LISTS : ROW_LISTS + 4, :] = lists_ref[...].astype(jnp.float32)
    out_ref[ROW_PATCH : ROW_PATCH + patches, :] = patch_ref[...].astype(jnp.float32)
    out_ref[ROW_PATCH + patches :, :] = map_ref[...].astype(jnp.float32)


def row_kernel(width, patches, row_ref, total_ref, pair_ref, other_ref, table_ref, parts_ref, back_ref, idx_ref, coarse_ref, fine_ref):
    me = lax.axis_index("my")
    side = lax.rem(lax.axis_index("mx"), 2)
    count = width * patches
    slot = [slot_of(me, u, width) for u in range(width)]
    state = [row_ref[slot[u], 0:TILE, :] for u in range(width)]
    nodes = jnp.concatenate([row_ref[slot[u], ROW_PATCH : ROW_PATCH + patches, :] for u in range(width)], axis=0)
    pairs = jnp.concatenate([row_ref[slot[u], ROW_PATCH + patches :, :] for u in range(width)], axis=0)
    lane = lax.broadcasted_iota(jnp.int32, (patches, LANES), 1)
    line = lax.broadcasted_iota(jnp.int32, (patches, LANES), 0)
    owner_col = jnp.concatenate(
        [
            jnp.sum(jnp.where(lane == line, state[u][ROW_OWNER : ROW_OWNER + 1], 0.0), axis=1, keepdims=True)
            for u in range(width)
        ],
        axis=0,
    )
    p = lax.broadcasted_iota(jnp.int32, (count, count), 0).astype(jnp.float32)
    q = lax.broadcasted_iota(jnp.int32, (count, count), 1).astype(jnp.float32)
    owner_row = jnp.sum(jnp.where(p == q, owner_col, 0.0), axis=0, keepdims=True)
    same = owner_col == owner_row
    after = jnp.min(jnp.where(same, jnp.where(q > p, q, q + count), 3.0 * count), axis=1, keepdims=True)
    after = jnp.where(after >= count, after - count, after)
    before = jnp.max(jnp.where(same, jnp.where(q < p, q + count, q), -1.0), axis=1, keepdims=True)
    before = jnp.where(before >= count, before - count, before)
    link = jnp.where(q == after, 1.0, 0.0).astype(jnp.bfloat16)
    back = jnp.where(q == before, 1.0, 0.0).astype(jnp.bfloat16)

    def route(table, rows):
        return jnp.dot(table, rows.astype(jnp.bfloat16), preferred_element_type=jnp.float32)

    target = pick(route(link, nodes), pairs.astype(jnp.int32))
    device = jnp.broadcast_to(jnp.floor(after / patches), (count, LANES))
    node_ids, target_ids = nodes.astype(jnp.int32), target.astype(jnp.int32)
    device_ids = device.astype(jnp.int32)
    mine, partner = [], []
    for c in (0, 1, 2, 4, 5, 6):
        rows = [state[u][c : c + 1] for u in range(width)]
        own = jnp.concatenate([jnp.broadcast_to(row, (patches, LANES)) for row in rows], axis=0)
        mine.append(pick(own, node_ids))
        partner.append(pick(choose(rows, device_ids), target_ids))
    forces = pair_forces(mine, partner)
    put_parts(parts_ref, forces)
    for c, force in enumerate(forces):
        high = force.astype(jnp.bfloat16).astype(jnp.float32)
        for g, part in ((c, high), (4 + c, force - high)):
            routed = -route(back, part)
            for b in range(count // TILE):
                at = b * TILE * TILE + g * TILE
                back_ref[at : at + TILE, :] = routed[b * TILE : (b + 1) * TILE]
    landing = route(back, target)
    from_nodes = route(back, nodes)
    idx_ref[0:count, :] = nodes
    idx_ref[count : 2 * count, :] = landing
    idx_ref[2 * count : 3 * count, :] = target
    idx_ref[3 * count : 4 * count, :] = from_nodes
    idx_ref[4 * count : 5 * count, :] = device
    idx_ref[5 * count : 6 * count, :] = jnp.broadcast_to(jnp.floor(before / patches), (count, LANES))
    for g in range(6):
        table_ref[g * patches : (g + 1) * patches, :] = idx_ref[pl.ds(g * count + me * patches, patches), :]
    coarse, fine = parted(idx_ref[0 : 2 * count, :])
    coarse_ref[...] = coarse
    fine_ref[...] = fine

    def unit(u):
        entries = []
        for base, ref in ((0, parts_ref), (count, back_ref)):
            for s in range(patches):
                at = u * patches + s
                entries.append(
                    (
                        coarse_ref[pl.ds(base + at, 1), :],
                        fine_ref[pl.ds(base + at, 1), :],
                        get_parts(ref, at),
                    )
                )
        info = row_ref[slot_of(me, u, width), ROW_ELASTIC : ROW_ELASTIC + TILE, :]
        total = scatter(joined(entries)) + info
        total_ref[u] = total
        lists = info.astype(jnp.int32)
        low = pick(total, jnp.broadcast_to(lists[4:5], (TILE, LANES)))
        high = pick(total, jnp.broadcast_to(lists[5:6], (TILE, LANES)))
        pair_ref[u] = jnp.where(side == 0, high, low)[0:4]
        other_ref[u] = jnp.where(side == 0, low, high)[0:4]

    if width <= 4:
        for u in range(width):
            unit(u)
    else:
        lax.fori_loop(0, width, lambda u, carry: (unit(u), carry)[1], 0)


def faces(tiles, lists):
    return scatter(joined([(*parted(row), tile_parts(tile)) for row, tile in zip(lists, tiles)]))


def step_kernel(
    width, patches, row_ref, total_ref, pair_ref, other_ref, table_ref, rest_ref, connect_ref, modulus_ref, stiff_ref,
    state_ref, near_ref, *refs,
):
    send_refs, (next_ref, fparts_ref, parts_ref) = refs[:4], refs[4:]
    me = lax.axis_index("my")
    side = lax.rem(lax.axis_index("mx"), 2)
    blank = jnp.zeros((4, LANES), jnp.float32)

    def unit(u):
        info = row_ref[slot_of(me, u, width), 0 : 2 * TILE, :]
        lists = info[TILE:]
        lower, upper = lists[4:5], lists[5:6]
        down, up = jnp.maximum(u - 1, 0), jnp.minimum(u + 1, width - 1)
        down_list = row_ref[slot_of(me, down, width), ROW_LISTS + 3 : ROW_LISTS + 4, :].astype(jnp.int32)
        up_list = row_ref[slot_of(me, up, width), ROW_LISTS + 2 : ROW_LISTS + 3, :].astype(jnp.int32)
        low = pick(total_ref[down], jnp.broadcast_to(down_list, (TILE, LANES)))
        high = pick(total_ref[up], jnp.broadcast_to(up_list, (TILE, LANES)))
        low = jnp.where(u > 0, low, 0.0)
        high = jnp.where(u < width - 1, high, 0.0)
        tiles = [
            jnp.concatenate([pair_ref[u], blank], axis=0),
            jnp.concatenate([other_ref[u], blank], axis=0),
            low,
            high,
        ]
        near, far = jnp.where(side == 0, upper, lower), jnp.where(side == 0, lower, upper)
        total = total_ref[u] + faces(tiles, [near, far, lists[6:7], lists[7:8]])
        speed = info[ROW_SPEED : ROW_SPEED + 3] + time_step * info[ROW_MASS : ROW_MASS + 1] * total[0:3]
        next_ref[u, 0:3, :] = info[0:3] + time_step * speed
        next_ref[u, 4:7, :] = speed

    if width <= 4:
        for u in range(width):
            unit(u)
    else:
        lax.fori_loop(0, width, lambda u, carry: (unit(u), carry)[1], 0)

    own = next_ref[me]
    state_ref[...] = own
    table = [table_ref[g * patches : (g + 1) * patches, :].astype(jnp.int32) for g in range(6)]
    nodes, landing, target, from_nodes, to_device, from_device = table
    first, second = [], []
    for c in (0, 1, 2, 4, 5, 6):
        rows = [next_ref[u, c : c + 1, :] for u in range(width)]
        home = jnp.broadcast_to(own[c : c + 1], (patches, LANES))
        first.append(jnp.concatenate([pick(home, nodes), pick(choose(rows, from_device), from_nodes)], axis=0))
        second.append(jnp.concatenate([pick(choose(rows, to_device), target), pick(home, landing)], axis=0))
    forces = pair_forces(first, second)
    sign = jnp.where(lax.broadcasted_iota(jnp.int32, (2 * patches, LANES), 0) < patches, 1.0, -1.0)
    put_parts(parts_ref, [sign * f for f in forces])
    coarse, fine = parted(table_ref[0 : 2 * patches, :])
    entries = [
        (coarse[s : s + 1], fine[s : s + 1], get_parts(parts_ref, s))
        for s in range(2 * patches)
    ]
    total = scatter(
        elastic_terms(own[0:3], rest_ref[...], connect_ref[...].astype(jnp.int32), modulus_ref[...], stiff_ref[...], fparts_ref)
        + joined(entries)
    )
    near_ref[...] = total
    lists = row_ref[0, ROW_ELASTIC : ROW_ELASTIC + TILE, :].astype(jnp.int32)
    sides = [pick(total, jnp.broadcast_to(lists[4 + k : 5 + k], (TILE, LANES))) for k in range(4)]
    even = lax.rem(me, 2) == 0
    send_refs[0][...] = jnp.where(side == 0, sides[1], sides[0])
    send_refs[1][...] = jnp.where(side == 0, sides[0], sides[1])
    send_refs[2][...] = jnp.where(even, sides[3], sides[2])
    send_refs[3][...] = jnp.where(even, sides[2], sides[3])


def end_kernel(row_ref, state_ref, near_ref, *refs):
    in_refs, (place_ref, speed_ref) = refs[:4], refs[4:]
    side = lax.rem(lax.axis_index("mx"), 2)
    even = lax.rem(lax.axis_index("my"), 2)
    lists = row_ref[0, ROW_ELASTIC : ROW_ELASTIC + TILE, :]
    order = [
        jnp.where(side == 0, lists[5:6], lists[4:5]),
        jnp.where(side == 0, lists[4:5], lists[5:6]),
        jnp.where(even == 0, lists[7:8], lists[6:7]),
        jnp.where(even == 0, lists[6:7], lists[7:8]),
    ]
    total = near_ref[...] + faces([ref[...] for ref in in_refs], order)
    mass = row_ref[0, ROW_MASS : ROW_MASS + 1, :]
    speed = state_ref[4:7, :] + time_step * mass * total[0:3]
    speed_ref[...] = speed
    place_ref[...] = state_ref[0:3, :] + time_step * speed


def call(kernel, name, outs, scratch, *args, result=pltpu.VMEM, keep=True):
    return pl.pallas_call(
        kernel,
        name=name,
        out_shape=[result(shape, jnp.float32) for shape in outs],
        in_specs=[pl.BlockSpec(memory_space=pltpu.VMEM)] * len(args),
        out_specs=[pl.BlockSpec(memory_space=pltpu.VMEM)] * len(outs),
        scratch_shapes=[pltpu.VMEM(shape, jnp.float32) for shape in scratch],
    )(*[pltpu.with_memory_space_constraint(arg, pltpu.VMEM) if keep else arg for arg in args])


def swap(value, axis, first):
    size = lax.axis_size(axis)
    pairs = [(i, i + 1) for i in range(first, size - 1, 2)]
    return lax.ppermute(value, axis, pairs + [(j, i) for i, j in pairs])


def gather_row(record, axis):
    size = lax.axis_size(axis)
    held = record[None]
    step = size // 2
    while step:
        other = lax.ppermute(held, axis, [(i, i ^ step) for i in range(size)])
        held = jnp.concatenate([held, other], axis=0)
        step //= 2
    return held


def slot_of(me, device, size):
    apart = jnp.bitwise_xor(me, device)
    slot, step, place = 0, size // 2, 1
    while step:
        slot = slot + place * (lax.div(apart, step) & 1)
        step, place = step // 2, place * 2
    return slot


def body(
    positions, velocities, rest_positions, inverse_mass, element_nodes, modulus, stiffness, shared_lists, patch_nodes,
    patch_owner, pair_map,
):
    width = lax.axis_size("my")
    patches = patch_owner.shape[0]
    corners, elements = element_nodes.shape
    count = width * patches
    modulus, mass = modulus[None], inverse_mass[None]
    element_parts = (TILE * corners * elements // LANES, LANES)
    tile = (TILE, LANES)
    record, *held = call(
        pack_kernel,
        "pack",
        [(ROW_PATCH + 2 * patches, LANES), (3, LANES), (corners, elements), (1, elements), stiffness.shape],
        [element_parts],
        positions, velocities, rest_positions, mass, element_nodes, modulus, stiffness, shared_lists, patch_nodes,
        patch_owner[None], pair_map, keep=False,
    )
    row = gather_row(record, "my")
    total, pair, other, table = call(
        functools.partial(row_kernel, width, patches),
        "row",
        [(width, TILE, LANES), (width, 4, LANES), (width, 4, LANES), (6 * patches, LANES)],
        [(TILE * count, LANES)] * 2 + [(6 * count, LANES)] + [(2 * count, LANES)] * 2,
        row,
    )
    pair, other = swap(pair, "mx", 0), swap(other, "mx", 1)
    state, near, *sends = call(
        functools.partial(step_kernel, width, patches),
        "step",
        [tile] * 6,
        [(width, TILE, LANES), element_parts, (TILE * 2 * patches, LANES)],
        row, total, pair, other, table, *held,
    )
    ways = (("mx", 0), ("mx", 1), ("my", 0), ("my", 1))
    arrived = [swap(send, axis, first) for send, (axis, first) in zip(sends, ways)]
    return tuple(
        call(end_kernel, "end", [(3, LANES), (3, LANES)], [], row, state, near, *arrived, result=jax.ShapeDtypeStruct)
    )


def solution(mesh):
    in_specs = (
        P(None, ("mx", "my")),
        P(None, ("mx", "my")),
        P(None, ("mx", "my")),
        P(("mx", "my")),
        P(None, ("mx", "my")),
        P(("mx", "my")),
        P(),
        P(None, ("mx", "my")),
        P(("mx", "my"), None),
        P(("mx", "my")),
        P(("mx", "my"), None),
    )
    out_specs = (P(None, ("mx", "my")), P(None, ("mx", "my")))
    return jax.shard_map(body, mesh=mesh, in_specs=in_specs, out_specs=out_specs, check_vma=False)
```

time: 42.3 us -> 30.9 us (0.73)
  the two profiles are of different devices: /device:TPU:4 before, /device:TPU:20 now
where the time goes in v2:
time: 30.9 us; the launch traced here: 30.6 us
  starting transfers between devices  12.7 us (41%)
  waiting for transfers between devices  12.7 us (41%)
  Pallas kernels  4.42 us (14%)
  between operations  0.71 us (2%)
    ppermute x6, starting transfers between devices, swap(): return lax.ppermute(value, axis, pairs + [(j, i) for i, j in pairs])  10.6 us
    ppermute x2, waiting for transfers between devices, gather_row(): other = lax.ppermute(held, axis, [(i, i ^ step) for i in range(size)])  6.78 us
    ppermute x6, waiting for transfers between devices, swap(): return lax.ppermute(value, axis, pairs + [(j, i) for i, j in pairs])  5.97 us
    pallas_call x4, Pallas kernels, call(): pl.pallas_call(kernel, name=name, out_shape=[result(shape, jnp.float32) f...  4.42 us
    ppermute x2, starting transfers between devices, gather_row(): other = lax.ppermute(held, axis, [(i, i ^ step) for i in range(size)])  2.13 us
  transfers between devices with their start and end apart: 8, of which 4 were waited for; matrix products, arithmetic and copies ran while one was open for 0% of the time, Pallas kernels for 0%

profile of v2, /device:TPU:20, one launch (start us, length us, event | category | flops | bytes accessed | tf_op | source)
XLA Modules:
  0.0 30.6 jit_solution(4652225667104854806)
XLA Ops:
  0.6 1.3 %pack.1 = (f32[48,128]{1,0:T(8,128)S(1)}, f32[3,128]{1,0:T(4,128)S(1)}, f32[8,256]{1,0:T(8,128)S(1)}, f32[1,256]{1,0:T(1,128)S(1)}, f32[24,24]{1,0:T(8,128)S(1)}) custom-call(f32[3,128]{1,0:T(4,128)} %place_ref.1, f32[3,128]{1,0:T(4,128)} %speed_ref.1, f32[3,128]{1,0:T(4,128)} %rest_ref.1, f32[1,128]{1,0:T(1,128)} %bitcast.8, s32[8,256]{1,0:T(8,128)} %connect_ref.1, ...), custom_call_target="tpu_custom_call" | custom-call | tf_op jit(solution)/shard_map/pack/pallas_call | solution.py:355
  1.9 0.4 %collective-permute-start = (f32[1,48,128]{2,1,0:T(8,128)S(1)}, f32[1,48,128]{2,1,0:T(8,128)S(1)}, u32[]{:S(2)}, u32[]{:S(2)}) collective-permute-start(f32[1,48,128]{2,1,0:T(8,128)S(1)} %bitcast.4), channel_id=1, source_target_pairs={{0,2},{1,3},{2,0},{3,1},{4,6},{5,7},{6,4},{7,5},{8,10},{9,11},{10,... | collective-permute-start | bytes 73736 | tf_op jit(solution)/shard_map/ppermute | solution.py:376
  2.3 4.4 %collective-permute-done = f32[1,48,128]{2,1,0:T(8,128)S(1)} collective-permute-done((f32[1,48,128]{2,1,0:T(8,128)S(1)}, f32[1,48,128]{2,1,0:T(8,128)S(1)}, u32[]{:S(2)}, u32[]{:S(2)}) %collective-permute-start) | collective-permute-done | bytes 24608 | tf_op jit(solution)/shard_map/ppermute | solution.py:376
  6.7 1.7 %collective-permute-start.1 = (f32[2,48,128]{2,1,0:T(8,128)S(1)}, f32[2,48,128]{2,1,0:T(8,128)S(1)}, u32[]{:S(2)}, u32[]{:S(2)}) collective-permute-start(f32[2,48,128]{2,1,0:T(8,128)S(1)} %pad_maximum_fusion.1), channel_id=1, source_target_pairs={{0,1},{1,0},{2,3},{3,2},{4,5},{5,4},{6,7},{7,6},{8,9},{9,8},{10,11... | collective-permute-start | bytes 147464 | tf_op jit(solution)/shard_map/ppermute | solution.py:376
  8.4 2.4 %collective-permute-done.1 = f32[2,48,128]{2,1,0:T(8,128)S(1)} collective-permute-done((f32[2,48,128]{2,1,0:T(8,128)S(1)}, f32[2,48,128]{2,1,0:T(8,128)S(1)}, u32[]{:S(2)}, u32[]{:S(2)}) %collective-permute-start.1) | collective-permute-done | bytes 49184 | tf_op jit(solution)/shard_map/ppermute | solution.py:376
  10.8 1.3 %row.1 = (f32[4,8,128]{2,1,0:T(8,128)S(1)}, f32[4,4,128]{2,1,0:T(4,128)S(1)}, f32[4,4,128]{2,1,0:T(4,128)S(1)}, f32[96,128]{1,0:T(8,128)S(1)}) custom-call(f32[4,48,128]{2,1,0:T(8,128)S(1)} %pad_maximum_fusion.row_ref), custom_call_target="tpu_custom_call" | custom-call | tf_op jit(solution)/shard_map/row/pallas_call | solution.py:355
  12.2 0.0 collective-permute-start.2
  12.2 3.4 %collective-permute-start.3 = (f32[4,4,128]{2,1,0:T(4,128)S(1)}, f32[4,4,128]{2,1,0:T(4,128)S(1)}, u32[]{:S(2)}, u32[]{:S(2)}) collective-permute-start(f32[4,4,128]{2,1,0:T(4,128)S(1)} %get-tuple-element.20), channel_id=1, source_target_pairs={{4,8},{12,16},{20,24},{8,4},{16,12},{24,20},{5,9},{13,17},{21,25},... | collective-permute-start | bytes 24584 | tf_op jit(solution)/shard_map/ppermute | solution.py:368
  15.6 0.0 collective-permute-done.2.pair_ref
  15.6 2.4 %collective-permute-done.3.other_ref = f32[4,4,128]{2,1,0:T(4,128)S(1)} collective-permute-done((f32[4,4,128]{2,1,0:T(4,128)S(1)}, f32[4,4,128]{2,1,0:T(4,128)S(1)}, u32[]{:S(2)}, u32[]{:S(2)}) %collective-permute-start.3) | collective-permute-done | bytes 8224 | tf_op jit(solution)/shard_map/ppermute | solution.py:368
  18.1 1.0 %step.1 = (f32[8,128]{1,0:T(8,128)S(1)}, f32[8,128]{1,0:T(8,128)S(1)}, f32[8,128]{1,0:T(8,128)S(1)}, f32[8,128]{1,0:T(8,128)S(1)}, f32[8,128]{1,0:T(8,128)S(1)}, /*index=5*/f32[8,128]{1,0:T(8,128)S(1)}) custom-call(f32[4,48,128]{2,1,0:T(8,128)S(1)} %pad_maximum_fusion.row_ref, f32[4,8,128]{2,1,0:T(8,128)S(1)} %get-tuple-element.18.total_ref, ...), custom_call_target="tpu_custom_call" | custom-call | tf_op jit(solution)/shard_map/step/pallas_call | solution.py:355
  19.1 0.0 collective-permute-start.4
  19.1 3.4 %collective-permute-start.5 = (f32[8,128]{1,0:T(8,128)S(1)}, f32[8,128]{1,0:T(8,128)S(1)}, u32[]{:S(2)}, u32[]{:S(2)}) collective-permute-start(f32[8,128]{1,0:T(8,128)S(1)} %get-tuple-element.29), channel_id=1, source_target_pairs={{4,8},{12,16},{20,24},{8,4},{16,12},{24,20},{5,9},{13,17},{21,25},... | collective-permute-start | bytes 12296 | tf_op jit(solution)/shard_map/ppermute | solution.py:368
  22.5 1.8 %collective-permute-start.6 = (f32[8,128]{1,0:T(8,128)S(1)}, f32[8,128]{1,0:T(8,128)S(1)}, u32[]{:S(2)}, u32[]{:S(2)}) collective-permute-start(f32[8,128]{1,0:T(8,128)S(1)} %get-tuple-element.30), channel_id=1, source_target_pairs={{0,1},{2,3},{1,0},{3,2},{4,5},{6,7},{5,4},{7,6},{8,9},{10,11},{9,8... | collective-permute-start | bytes 12296 | tf_op jit(solution)/shard_map/ppermute | solution.py:368
  24.3 1.9 %collective-permute-start.7 = (f32[8,128]{1,0:T(8,128)S(1)}, f32[8,128]{1,0:T(8,128)S(1)}, u32[]{:S(2)}, u32[]{:S(2)}) collective-permute-start(f32[8,128]{1,0:T(8,128)S(1)} %get-tuple-element.31), channel_id=1, source_target_pairs={{1,2},{2,1},{5,6},{6,5},{9,10},{10,9},{13,14},{14,13},{17,18},{18,... | collective-permute-start | bytes 12296 | tf_op jit(solution)/shard_map/ppermute | solution.py:368
  26.2 0.0 collective-permute-done.4.refs_0_
  26.3 0.0 collective-permute-done.5.refs_1_
  26.3 0.0 collective-permute-done.6.refs_2_
  26.3 3.5 %collective-permute-done.7.refs_3_ = f32[8,128]{1,0:T(8,128)S(1)} collective-permute-done((f32[8,128]{1,0:T(8,128)S(1)}, f32[8,128]{1,0:T(8,128)S(1)}, u32[]{:S(2)}, u32[]{:S(2)}) %collective-permute-start.7) | collective-permute-done | bytes 4128 | tf_op jit(solution)/shard_map/ppermute | solution.py:368
  29.8 0.8 %end.1 = (f32[3,128]{1,0:T(4,128)}, f32[3,128]{1,0:T(4,128)}) custom-call(f32[4,48,128]{2,1,0:T(8,128)S(1)} %pad_maximum_fusion.row_ref, f32[8,128]{1,0:T(8,128)S(1)} %get-tuple-element.26.state_ref, f32[8,128]{1,0:T(8,128)S(1)} %get-tuple-element.27.near_ref, f32[8,128]{1,0:T(8,128)S(1)} %collective-permute-done.4.refs_0_, ...), custom_call_target="tpu_custom_call" | custom-call | tf_op jit(solution)/shard_map/end/pallas_call | solution.py:355
  (2 shorter events, 0.0 us)
Async XLA Ops:
  1.9 4.8 %collective-permute-start = (f32[1,48,128]{2,1,0:T(8,128)S(1)}, f32[1,48,128]{2,1,0:T(8,128)S(1)}, u32[]{:S(2)}, u32[]{:S(2)}) collective-permute-start(f32[1,48,128]{2,1,0:T(8,128)S(1)} %bitcast.4), channel_id=1, source_target_pairs={{0,2},{1,3},{2,0},{3,1},{4,6},{5,7},{6,4},{7,5},{8,10},{9,11},{10,... | collective-permute-start | bytes 73736 | tf_op jit(solution)/shard_map/ppermute | solution.py:376
  6.7 4.1 %collective-permute-start.1 = (f32[2,48,128]{2,1,0:T(8,128)S(1)}, f32[2,48,128]{2,1,0:T(8,128)S(1)}, u32[]{:S(2)}, u32[]{:S(2)}) collective-permute-start(f32[2,48,128]{2,1,0:T(8,128)S(1)} %pad_maximum_fusion.1), channel_id=1, source_target_pairs={{0,1},{1,0},{2,3},{3,2},{4,5},{5,4},{6,7},{7,6},{8,9},{9,8},{10,11... | collective-permute-start | bytes 147464 | tf_op jit(solution)/shard_map/ppermute | solution.py:376
  12.2 3.5 %collective-permute-start.2 = (f32[4,4,128]{2,1,0:T(4,128)S(1)}, f32[4,4,128]{2,1,0:T(4,128)S(1)}, u32[]{:S(2)}, u32[]{:S(2)}) collective-permute-start(f32[4,4,128]{2,1,0:T(4,128)S(1)} %get-tuple-element.19), channel_id=1, source_target_pairs={{0,4},{8,12},{16,20},{24,28},{4,0},{12,8},{20,16},{28,24},{1,5},{9... | collective-permute-start | bytes 24584 | tf_op jit(solution)/shard_map/ppermute | solution.py:368
  12.2 5.9 %collective-permute-start.3 = (f32[4,4,128]{2,1,0:T(4,128)S(1)}, f32[4,4,128]{2,1,0:T(4,128)S(1)}, u32[]{:S(2)}, u32[]{:S(2)}) collective-permute-start(f32[4,4,128]{2,1,0:T(4,128)S(1)} %get-tuple-element.20), channel_id=1, source_target_pairs={{4,8},{12,16},{20,24},{8,4},{16,12},{24,20},{5,9},{13,17},{21,25},... | collective-permute-start | bytes 24584 | tf_op jit(solution)/shard_map/ppermute | solution.py:368
  19.1 7.2 %collective-permute-start.4 = (f32[8,128]{1,0:T(8,128)S(1)}, f32[8,128]{1,0:T(8,128)S(1)}, u32[]{:S(2)}, u32[]{:S(2)}) collective-permute-start(f32[8,128]{1,0:T(8,128)S(1)} %get-tuple-element.28), channel_id=1, source_target_pairs={{0,4},{8,12},{16,20},{24,28},{4,0},{12,8},{20,16},{28,24},{1,5},{9... | collective-permute-start | bytes 12296 | tf_op jit(solution)/shard_map/ppermute | solution.py:368
  19.1 7.2 %collective-permute-start.5 = (f32[8,128]{1,0:T(8,128)S(1)}, f32[8,128]{1,0:T(8,128)S(1)}, u32[]{:S(2)}, u32[]{:S(2)}) collective-permute-start(f32[8,128]{1,0:T(8,128)S(1)} %get-tuple-element.29), channel_id=1, source_target_pairs={{4,8},{12,16},{20,24},{8,4},{16,12},{24,20},{5,9},{13,17},{21,25},... | collective-permute-start | bytes 12296 | tf_op jit(solution)/shard_map/ppermute | solution.py:368
  22.5 3.7 %collective-permute-start.6 = (f32[8,128]{1,0:T(8,128)S(1)}, f32[8,128]{1,0:T(8,128)S(1)}, u32[]{:S(2)}, u32[]{:S(2)}) collective-permute-start(f32[8,128]{1,0:T(8,128)S(1)} %get-tuple-element.30), channel_id=1, source_target_pairs={{0,1},{2,3},{1,0},{3,2},{4,5},{6,7},{5,4},{7,6},{8,9},{10,11},{9,8... | collective-permute-start | bytes 12296 | tf_op jit(solution)/shard_map/ppermute | solution.py:368
  24.3 5.5 %collective-permute-start.7 = (f32[8,128]{1,0:T(8,128)S(1)}, f32[8,128]{1,0:T(8,128)S(1)}, u32[]{:S(2)}, u32[]{:S(2)}) collective-permute-start(f32[8,128]{1,0:T(8,128)S(1)} %get-tuple-element.31), channel_id=1, source_target_pairs={{1,2},{2,1},{5,6},{6,5},{9,10},{10,9},{13,14},{14,13},{17,18},{18,... | collective-permute-start | bytes 12296 | tf_op jit(solution)/shard_map/ppermute | solution.py:368

commit v3 on v2

v3 whole, which is shorter than its diff:
```python
import functools

import jax
import jax.numpy as jnp
from jax import lax
from jax.experimental import pallas as pl
from jax.experimental.pallas import tpu as pltpu
from jax.sharding import PartitionSpec as P

STEPS = 2

time_step = 0.1
penalty = 4.0
damping = 0.5
contact_reach = 4.0
LANES = 128
TILE = 8
FINE = 32
VMEM_GRANT = 16 << 20
ROW_MASS, ROW_SPEED, ROW_OWNER, ROW_ELASTIC, ROW_LISTS, ROW_PATCH = 3, 4, 7, 8, 12, 16


def pick(rows, indices):
    return jnp.take_along_axis(rows, indices, axis=1)


def parted(indices):
    coarse = jnp.floor(indices * (1.0 / FINE))
    return coarse, indices - FINE * coarse


def put_parts(parts_ref, values, base=0):
    for c, value in enumerate(values):
        high = value.astype(jnp.bfloat16).astype(jnp.float32)
        rest = value - high
        for b in range(value.shape[0] // TILE):
            at = base + b * TILE * TILE
            parts_ref[at + c * TILE : at + (c + 1) * TILE, :] = high[b * TILE : (b + 1) * TILE]
            parts_ref[at + (4 + c) * TILE : at + (5 + c) * TILE, :] = rest[b * TILE : (b + 1) * TILE]


def get_parts(parts_ref, row):
    if isinstance(row, int):
        start = row // TILE * TILE * TILE + row % TILE
    else:
        start = lax.div(row, TILE) * (TILE * TILE) + lax.rem(row, TILE)
    return parts_ref[pl.ds(start, TILE, stride=TILE), :]


def scatter(entries):
    blocks = LANES // FINE
    total = jnp.zeros((blocks * TILE, FINE), jnp.float32)
    for coarse, fine, weights in entries:
        wide = weights.shape[1]
        shape = (blocks * TILE, wide)
        block = (lax.broadcasted_iota(jnp.int32, shape, 0) // TILE).astype(jnp.float32).astype(jnp.bfloat16)
        placed = jnp.where(
            jnp.broadcast_to(coarse, shape).astype(jnp.bfloat16) == block,
            jnp.concatenate([weights] * blocks, axis=0).astype(jnp.bfloat16),
            jnp.zeros(shape, jnp.bfloat16),
        )
        shape = (FINE, wide)
        node = lax.broadcasted_iota(jnp.int32, shape, 0).astype(jnp.float32).astype(jnp.bfloat16)
        hot = jnp.where(
            jnp.broadcast_to(fine, shape).astype(jnp.bfloat16) == node,
            jnp.ones(shape, jnp.bfloat16),
            jnp.zeros(shape, jnp.bfloat16),
        )
        total += lax.dot_general(placed, hot, (((1,), (1,)), ((), ())), preferred_element_type=jnp.float32)
    tile = jnp.concatenate([total[b * TILE : (b + 1) * TILE] for b in range(blocks)], axis=1)
    return tile + pltpu.roll(tile, 4, 0)


def joined(entries):
    return [
        tuple(jnp.concatenate([a, b], axis=1) for a, b in zip(*two)) for two in zip(entries[0::2], entries[1::2])
    ]


def tile_parts(tile):
    high = tile.astype(jnp.bfloat16).astype(jnp.float32)
    rest = pltpu.roll(tile - high, 4, 0)
    row = lax.broadcasted_iota(jnp.int32, tile.shape, 0)
    return jnp.where(row < 4, high, rest)


def product(left, right):
    def parts(x):
        high = x.astype(jnp.bfloat16)
        return high, (x - high.astype(jnp.float32)).astype(jnp.bfloat16)

    (lh, lr), (rh, rr) = parts(left), parts(right)
    return sum(jnp.dot(a, b, preferred_element_type=jnp.float32) for a, b in ((lh, rh), (lr, rh), (lh, rr)))


def elastic_entries(units, stiffness, parts_ref):
    local, moduli = [], []
    for place, rest, connect, modulus in units:
        moved = place - rest
        for corners, scale in zip(connect, modulus):
            local.append(
                jnp.concatenate(
                    [
                        pick(jnp.broadcast_to(moved[c : c + 1], corners.shape), corners.astype(jnp.int32))
                        for c in range(3)
                    ],
                    axis=0,
                )
            )
            moduli.append(scale)
    forces = -jnp.concatenate(moduli, axis=1) * product(stiffness, jnp.concatenate(local, axis=1))
    lists, at = [], 0
    for _, _, connect, _ in units:
        base, count = at, connect[0].shape[0]
        for k in range(len(connect)):
            span = slice((at + k) * LANES, (at + k + 1) * LANES)
            put_parts(
                parts_ref, [forces[c * count : (c + 1) * count, span] for c in range(3)], (at + k) * count * TILE
            )
        split = [parted(corners) for corners in connect]
        lists.append(
            [
                (
                    jnp.concatenate([coarse[a : a + 1] for coarse, _ in split], axis=1),
                    jnp.concatenate([fine[a : a + 1] for _, fine in split], axis=1),
                    jnp.concatenate([get_parts(parts_ref, (base + k) * count + a) for k in range(len(connect))], axis=1),
                )
                for a in range(count)
            ]
        )
        at += len(connect)
    return lists


def pair_forces(mine, partner):
    offset = [b - a for a, b in zip(mine[:3], partner[:3])]
    distance = offset[0] * offset[0] + offset[1] * offset[1] + offset[2] * offset[2]
    weight = jnp.exp(-distance / contact_reach)
    return [
        -penalty * weight * o + damping * weight * (b - a)
        for o, a, b in zip(offset, mine[3:], partner[3:])
    ]


def choose(rows, device):
    chosen = jnp.broadcast_to(rows[0], device.shape)
    for d, row in enumerate(rows[1:], 1):
        chosen = jnp.where(device == d, row, chosen)
    return chosen


def pack_kernel(
    place_ref, speed_ref, rest_ref, mass_ref, connect_ref, modulus_ref, stiff_ref, lists_ref, patch_ref, owner_ref,
    map_ref, out_ref, keep_ref, parts_ref,
):
    patches = patch_ref.shape[0]
    corners, elements = connect_ref.shape
    runs = [slice(k * LANES, (k + 1) * LANES) for k in range(elements // LANES)]
    connect = [connect_ref[:, run].astype(jnp.float32) for run in runs]
    modulus = [modulus_ref[:, run] for run in runs]
    (entries,) = elastic_entries([(place_ref[...], rest_ref[...], connect, modulus)], stiff_ref[...], parts_ref)
    keep_ref[...] = stiff_ref[...]
    out_ref[0:3, :] = place_ref[...]
    out_ref[ROW_MASS : ROW_MASS + 1, :] = mass_ref[...]
    out_ref[ROW_SPEED : ROW_SPEED + 3, :] = speed_ref[...]
    out_ref[ROW_OWNER : ROW_OWNER + 1, :] = jnp.zeros((1, LANES), jnp.float32)
    out_ref[ROW_OWNER : ROW_OWNER + 1, 0:patches] = owner_ref[...].astype(jnp.float32)
    out_ref[ROW_PATCH : ROW_PATCH + patches, :] = patch_ref[...].astype(jnp.float32)
    out_ref[ROW_PATCH + patches : ROW_PATCH + 2 * patches, :] = map_ref[...].astype(jnp.float32)
    base = ROW_PATCH + 2 * patches
    for k, run in enumerate(runs):
        out_ref[base + k * corners : base + (k + 1) * corners, :] = connect[k]
    last = base + len(runs) * corners
    out_ref[last : last + TILE, :] = jnp.zeros((TILE, LANES), jnp.float32)
    out_ref[last : last + 3, :] = rest_ref[...]
    for k, scale in enumerate(modulus):
        out_ref[last + 4 + k : last + 5 + k, :] = scale
    out_ref[ROW_ELASTIC : ROW_ELASTIC + TILE, :] = scatter(entries)
    out_ref[ROW_LISTS : ROW_LISTS + 4, :] = lists_ref[...].astype(jnp.float32)


def route(table, rows):
    return jnp.dot(table, rows.astype(jnp.bfloat16), preferred_element_type=jnp.float32)


def put_contact(width, patches, state, indices, back, parts_ref, back_ref):
    count = width * patches
    nodes, target, device = [part.astype(jnp.int32) for part in indices]
    mine, partner = [], []
    for c in (0, 1, 2, 4, 5, 6):
        rows = [tile[c : c + 1] for tile in state]
        own = jnp.concatenate([jnp.broadcast_to(row, (patches, LANES)) for row in rows], axis=0)
        mine.append(pick(own, nodes))
        partner.append(pick(choose(rows, device), target))
    forces = pair_forces(mine, partner)
    put_parts(parts_ref, forces)
    for c, force in enumerate(forces):
        high = force.astype(jnp.bfloat16).astype(jnp.float32)
        for g, part in ((c, high), (4 + c, force - high)):
            routed = -route(back, part)
            for b in range(count // TILE):
                at = b * TILE * TILE + g * TILE
                back_ref[at : at + TILE, :] = routed[b * TILE : (b + 1) * TILE]


def contact_entries(width, patches, u, coarse_ref, fine_ref, parts_ref, back_ref):
    entries = []
    for base, ref in ((0, parts_ref), (width * patches, back_ref)):
        for s in range(patches):
            at = u * patches + s
            entries.append((coarse_ref[pl.ds(base + at, 1), :], fine_ref[pl.ds(base + at, 1), :], get_parts(ref, at)))
    return joined(entries)


def each_unit(width, unit):
    if width <= 4:
        for u in range(width):
            unit(u)
    else:
        lax.fori_loop(0, width, lambda u, carry: (unit(u), carry)[1], 0)


def face_values(tile, row):
    return pick(tile, jnp.broadcast_to(row.astype(jnp.int32), tile.shape))


def row_kernel(
    width, patches, row_ref, total_ref, pair_ref, other_ref, idx_ref, link_ref, coarse_ref, fine_ref, parts_ref, back_ref
):
    me = lax.axis_index("my")
    side = lax.rem(lax.axis_index("mx"), 2)
    count = width * patches
    slot = [slot_of(me, u, width) for u in range(width)]
    state = [row_ref[slot[u], 0:TILE, :] for u in range(width)]
    nodes = jnp.concatenate([row_ref[slot[u], ROW_PATCH : ROW_PATCH + patches, :] for u in range(width)], axis=0)
    pairs = jnp.concatenate(
        [row_ref[slot[u], ROW_PATCH + patches : ROW_PATCH + 2 * patches, :] for u in range(width)], axis=0
    )
    lane = lax.broadcasted_iota(jnp.int32, (patches, LANES), 1)
    line = lax.broadcasted_iota(jnp.int32, (patches, LANES), 0)
    owner_col = jnp.concatenate(
        [
            jnp.sum(jnp.where(lane == line, state[u][ROW_OWNER : ROW_OWNER + 1], 0.0), axis=1, keepdims=True)
            for u in range(width)
        ],
        axis=0,
    )
    p = lax.broadcasted_iota(jnp.int32, (count, count), 0).astype(jnp.float32)
    q = lax.broadcasted_iota(jnp.int32, (count, count), 1).astype(jnp.float32)
    owner_row = jnp.sum(jnp.where(p == q, owner_col, 0.0), axis=0, keepdims=True)
    same = owner_col == owner_row
    after = jnp.min(jnp.where(same, jnp.where(q > p, q, q + count), 3.0 * count), axis=1, keepdims=True)
    after = jnp.where(after >= count, after - count, after)
    before = jnp.max(jnp.where(same, jnp.where(q < p, q + count, q), -1.0), axis=1, keepdims=True)
    before = jnp.where(before >= count, before - count, before)
    link = jnp.where(q == after, 1.0, 0.0).astype(jnp.bfloat16)
    back = jnp.where(q == before, 1.0, 0.0)
    link_ref[...] = back
    back = back.astype(jnp.bfloat16)
    target = pick(route(link, nodes), pairs.astype(jnp.int32))
    device = jnp.broadcast_to(jnp.floor(after / patches), (count, LANES))
    idx_ref[0:count, :] = nodes
    idx_ref[count : 2 * count, :] = target
    idx_ref[2 * count : 3 * count, :] = device
    coarse, fine = parted(jnp.concatenate([nodes, route(back, target)], axis=0))
    coarse_ref[...] = coarse
    fine_ref[...] = fine
    put_contact(width, patches, state, (nodes, target, device), back, parts_ref, back_ref)

    def unit(u):
        info = row_ref[slot_of(me, u, width), ROW_ELASTIC : ROW_ELASTIC + TILE, :]
        total = scatter(contact_entries(width, patches, u, coarse_ref, fine_ref, parts_ref, back_ref)) + info
        total_ref[u] = total
        low, high = face_values(total, info[4:5]), face_values(total, info[5:6])
        pair_ref[u] = jnp.where(side == 0, high, low)[0:4]
        other_ref[u] = jnp.where(side == 0, low, high)[0:4]

    each_unit(width, unit)


def faces(tiles, lists):
    return scatter(joined([(*parted(row), tile_parts(tile)) for row, tile in zip(lists, tiles)]))


def inside(axis):
    at, size = lax.axis_index(axis), lax.axis_size(axis)
    partner = at - 1 + 2 * lax.rem(at, 2)
    return jnp.logical_and(partner >= 0, partner < size)


def step_kernel(
    width, patches, corners, row_ref, total_ref, pair_ref, other_ref, idx_ref, link_ref, coarse_ref, fine_ref, stiff_ref,
    state_ref, near_ref, low_ref, high_ref, send_ref, far_ref, next_ref, element_ref, parts_ref, back_ref,
):
    me = lax.axis_index("my")
    side = lax.rem(lax.axis_index("mx"), 2)
    joins = inside("mx")
    count = width * patches
    blank = jnp.zeros((4, LANES), jnp.float32)

    def unit(u):
        info = row_ref[slot_of(me, u, width), 0 : 2 * TILE, :]
        lists = info[ROW_LISTS : ROW_LISTS + 4]
        down, up = jnp.maximum(u - 1, 0), jnp.minimum(u + 1, width - 1)
        low = face_values(total_ref[down], row_ref[slot_of(me, down, width), ROW_LISTS + 3 : ROW_LISTS + 4, :])
        high = face_values(total_ref[up], row_ref[slot_of(me, up, width), ROW_LISTS + 2 : ROW_LISTS + 3, :])
        tiles = [
            jnp.concatenate([pair_ref[u], blank], axis=0),
            jnp.where(joins, jnp.concatenate([other_ref[u], blank], axis=0), 0.0),
            jnp.where(u > 0, low, 0.0),
            jnp.where(u < width - 1, high, 0.0),
        ]
        near, far = jnp.where(side == 0, lists[1:2], lists[0:1]), jnp.where(side == 0, lists[0:1], lists[1:2])
        total = total_ref[u] + faces(tiles, [near, far, lists[2:3], lists[3:4]])
        speed = info[ROW_SPEED : ROW_SPEED + 3] + time_step * info[ROW_MASS : ROW_MASS + 1] * total[0:3]
        next_ref[u, 0:3, :] = info[0:3] + time_step * speed
        next_ref[u, 4:7, :] = speed

    each_unit(width, unit)
    state_ref[...] = next_ref[me]
    state = [next_ref[u] for u in range(width)]
    indices = [idx_ref[g * count : (g + 1) * count, :] for g in range(3)]
    put_contact(width, patches, state, indices, link_ref[...].astype(jnp.bfloat16), parts_ref, back_ref)
    around = [me, jnp.maximum(me - 1, 0), jnp.minimum(me + 1, width - 1)]
    base = ROW_PATCH + 2 * patches
    last = row_ref.shape[1] - TILE
    units = []
    for u in around:
        slot = slot_of(me, u, width)
        runs = (last - base) // corners
        connect = [row_ref[slot, base + k * corners : base + (k + 1) * corners, :] for k in range(runs)]
        tail = row_ref[slot, last : last + TILE, :]
        units.append((next_ref[u][0:3], tail[0:3], connect, [tail[4 + k : 5 + k] for k in range(runs)]))
    elastic = elastic_entries(units, stiff_ref[...], element_ref)
    totals = [
        scatter(entries + contact_entries(width, patches, u, coarse_ref, fine_ref, parts_ref, back_ref))
        for u, entries in zip(around, elastic)
    ]
    near_ref[...] = totals[0]
    low = face_values(totals[1], row_ref[slot_of(me, around[1], width), ROW_LISTS + 3 : ROW_LISTS + 4, :])
    high = face_values(totals[2], row_ref[slot_of(me, around[2], width), ROW_LISTS + 2 : ROW_LISTS + 3, :])
    low_ref[...] = jnp.where(me > 0, low, 0.0)
    high_ref[...] = jnp.where(me < width - 1, high, 0.0)
    lists = row_ref[0, ROW_LISTS : ROW_LISTS + 4, :]
    low, high = face_values(totals[0], lists[0:1]), face_values(totals[0], lists[1:2])
    send_ref[...] = jnp.where(side == 0, high, low)
    far_ref[...] = jnp.where(side == 0, low, high)


def end_kernel(row_ref, state_ref, near_ref, low_ref, high_ref, pair_ref, other_ref, place_ref, speed_ref):
    side = lax.rem(lax.axis_index("mx"), 2)
    info = row_ref[0, 0 : 2 * TILE, :]
    lists = info[ROW_LISTS : ROW_LISTS + 4]
    near, far = jnp.where(side == 0, lists[1:2], lists[0:1]), jnp.where(side == 0, lists[0:1], lists[1:2])
    tiles = [pair_ref[...], jnp.where(inside("mx"), other_ref[...], 0.0), low_ref[...], high_ref[...]]
    total = near_ref[...] + faces(tiles, [near, far, lists[2:3], lists[3:4]])
    speed = state_ref[4:7, :] + time_step * info[ROW_MASS : ROW_MASS + 1] * total[0:3]
    speed_ref[...] = speed
    place_ref[...] = state_ref[0:3, :] + time_step * speed


def call(kernel, name, outs, scratch, *args, result=pltpu.VMEM, keep=True):
    return pl.pallas_call(
        kernel,
        name=name,
        out_shape=[result(shape, jnp.float32) for shape in outs],
        in_specs=[pl.BlockSpec(memory_space=pltpu.VMEM)] * len(args),
        out_specs=[pl.BlockSpec(memory_space=pltpu.VMEM)] * len(outs),
        scratch_shapes=[pltpu.VMEM(shape, jnp.float32) for shape in scratch],
        compiler_params=pltpu.CompilerParams(vmem_limit_bytes=VMEM_GRANT),
    )(*[pltpu.with_memory_space_constraint(arg, pltpu.VMEM) if keep else arg for arg in args])


def swap(value, axis, first):
    size = lax.axis_size(axis)
    pairs = [(i, i + 1) for i in range(first, size - 1, 2)]
    if first and size % 2 == 0:
        pairs.append((0, size - 1))
    return lax.ppermute(value, axis, pairs + [(j, i) for i, j in pairs])


def gather_row(record, axis):
    size = lax.axis_size(axis)
    held = record[None]
    step = size // 2
    while step:
        other = lax.ppermute(held, axis, [(i, i ^ step) for i in range(size)])
        held = jnp.concatenate([held, other], axis=0)
        step //= 2
    return held


def slot_of(me, device, size):
    apart = jnp.bitwise_xor(me, device)
    slot, step, place = 0, size // 2, 1
    while step:
        slot = slot + place * (lax.div(apart, step) & 1)
        step, place = step // 2, place * 2
    return slot


def body(
    positions, velocities, rest_positions, inverse_mass, element_nodes, modulus, stiffness, shared_lists, patch_nodes,
    patch_owner, pair_map,
):
    width = lax.axis_size("my")
    patches = patch_owner.shape[0]
    corners, elements = element_nodes.shape
    count = width * patches
    modulus, mass = modulus[None], inverse_mass[None]
    runs = elements // LANES
    element_parts = (TILE * corners * runs, LANES)
    tile = (TILE, LANES)
    parts = (TILE * count, LANES)
    record, stiff = call(
        pack_kernel,
        "pack",
        [(ROW_PATCH + 2 * patches + runs * corners + TILE, LANES), stiffness.shape],
        [element_parts],
        positions, velocities, rest_positions, mass, element_nodes, modulus, stiffness, shared_lists, patch_nodes,
        patch_owner[None], pair_map, keep=False,
    )
    row = gather_row(record, "my")
    total, pair, other, *tables = call(
        functools.partial(row_kernel, width, patches),
        "row",
        [(width, TILE, LANES), (width, 4, LANES), (width, 4, LANES), (3 * count, LANES), (count, count)]
        + [(2 * count, LANES)] * 2,
        [parts, parts],
        row,
    )
    pair, other = swap(pair, "mx", 0), swap(other, "mx", 1)
    state, near, low, high, pair, other = call(
        functools.partial(step_kernel, width, patches, corners),
        "step",
        [tile] * 6,
        [(width, TILE, LANES), (3 * element_parts[0], LANES), parts, parts],
        row, total, pair, other, *tables, stiff,
    )
    pair, other = swap(pair, "mx", 0), swap(other, "mx", 1)
    outs = [(3, LANES), (3, LANES)]
    return tuple(
        call(end_kernel, "end", outs, [], row, state, near, low, high, pair, other, result=jax.ShapeDtypeStruct)
    )


def solution(mesh):
    in_specs = (
        P(None, ("mx", "my")),
        P(None, ("mx", "my")),
        P(None, ("mx", "my")),
        P(("mx", "my")),
        P(None, ("mx", "my")),
        P(("mx", "my")),
        P(),
        P(None, ("mx", "my")),
        P(("mx", "my"), None),
        P(("mx", "my")),
        P(("mx", "my"), None),
    )
    out_specs = (P(None, ("mx", "my")), P(None, ("mx", "my")))
    return jax.shard_map(body, mesh=mesh, in_specs=in_specs, out_specs=out_specs, check_vma=False)
```

time: 30.9 us -> 29.7 us (0.961)
  the two profiles are of different devices: /device:TPU:20 before, /device:TPU:0 now
where the time goes in v3:
time: 29.7 us; the launch traced here: 29.3 us
  starting transfers between devices  11.1 us (37%)
  waiting for transfers between devices  7.87 us (26%)
  local copies, waits for them, and re-layouts  5.49 us (18%)
  Pallas kernels  4.02 us (14%)
  between operations  0.71 us (2%)
    ppermute x2, starting transfers between devices, gather_row(): other = lax.ppermute(held, axis, [(i, i ^ step) for i in range(size)])  5.62 us
    ppermute x4, starting transfers between devices, swap(): return lax.ppermute(value, axis, pairs + [(j, i) for i, j in pairs])  5.52 us
    unnamed x22, local copies, waits for them, and re-layouts  5.49 us
    ppermute x2, waiting for transfers between devices, gather_row(): other = lax.ppermute(held, axis, [(i, i ^ step) for i in range(size)])  5.18 us
    pallas_call x4, Pallas kernels, call(): pl.pallas_call(kernel, name=name, out_shape=[result(shape, jnp.float32) f...  4.02 us
    ppermute x4, waiting for transfers between devices, swap(): return lax.ppermute(value, axis, pairs + [(j, i) for i, j in pairs])  2.69 us
  transfers between devices with their start and end apart: 6, of which 4 were waited for; matrix products, arithmetic and copies ran while one was open for 0% of the time, Pallas kernels for 0%

profile of v3, /device:TPU:0, one launch (start us, length us, event | category | flops | bytes accessed | tf_op | source)
XLA Modules:
  0.0 29.3 jit_solution(12425585085533413008)
XLA Ops:
  0.7 0.6 %copy-done.5 = f32[3,128]{1,0:T(4,128)S(1)} copy-done((f32[3,128]{1,0:T(4,128)S(1)}, f32[3,128]{1,0:T(4,128)}, u32[]{:S(2)}) %copy-start.5) | copy-done | bytes 1560
  1.3 0.0 copy-done.4
  1.3 0.0 copy-done.8
  1.4 0.7 %copy-done = f32[24,24]{1,0:T(8,128)S(1)} copy-done((f32[24,24]{1,0:T(8,128)S(1)}, f32[24,24]{1,0:T(8,128)}, u32[]{:S(2)}) %copy-start) | copy-done | bytes 2328
  2.1 0.7 %copy-done.1 = s32[8,256]{1,0:T(8,128)S(1)} copy-done((s32[8,256]{1,0:T(8,128)S(1)}, s32[8,256]{1,0:T(8,128)}, u32[]{:S(2)}) %copy-start.1) | copy-done | bytes 8216
  2.8 0.7 %copy-done.2 = s32[16,128]{1,0:T(8,128)S(1)} copy-done((s32[16,128]{1,0:T(8,128)S(1)}, s32[16,128]{1,0:T(8,128)}, u32[]{:S(2)}) %copy-start.2) | copy-done | bytes 8216
  3.5 0.7 %copy-done.3 = s32[16,128]{1,0:T(8,128)S(1)} copy-done((s32[16,128]{1,0:T(8,128)S(1)}, s32[16,128]{1,0:T(8,128)}, u32[]{:S(2)}) %copy-start.3) | copy-done | bytes 8216
  4.2 0.7 %copy-done.6 = f32[3,128]{1,0:T(4,128)S(1)} copy-done((f32[3,128]{1,0:T(4,128)S(1)}, f32[3,128]{1,0:T(4,128)}, u32[]{:S(2)}) %copy-start.6) | copy-done | bytes 1560
  4.8 0.7 %copy-done.7 = s32[4,128]{1,0:T(4,128)S(1)} copy-done((s32[4,128]{1,0:T(4,128)S(1)}, s32[4,128]{1,0:T(4,128)}, u32[]{:S(2)}) %copy-start.7) | copy-done | bytes 2072
  5.5 0.7 %copy-done.10 = s32[16]{0:T(128)S(1)} copy-done((s32[16]{0:T(128)S(1)}, s32[16]{0:T(128)}, u32[]{:S(2)}) %copy-start.10) | copy-done | bytes 88
  6.2 0.4 %pack.1 = (f32[72,128]{1,0:T(8,128)S(1)}, f32[24,24]{1,0:T(8,128)S(1)}) custom-call(f32[3,128]{1,0:T(4,128)S(1)} %copy-done.4, f32[3,128]{1,0:T(4,128)S(1)} %copy-done.5, f32[3,128]{1,0:T(4,128)S(1)} %copy-done.6, f32[1,128]{1,0:T(1,128)S(1)} %bitcast.8, s32[8,256]{1,0:T(8,128)S(1)} %copy-done.1, f32[1,256]{1,0:T(1,128)S(1)} %bitcast.7, ...), custom_call_target="tpu_custom_call" | custom-call | tf_op jit(solution)/shard_map/pack/pallas_call | solution.py:363
  6.6 4.1 %collective-permute-start = (f32[1,72,128]{2,1,0:T(8,128)S(1)}, f32[1,72,128]{2,1,0:T(8,128)S(1)}, u32[]{:S(2)}, u32[]{:S(2)}) collective-permute-start(f32[1,72,128]{2,1,0:T(8,128)S(1)} %bitcast.4), channel_id=1, source_target_pairs={{0,2},{1,3},{2,0},{3,1},{4,6},{5,7},{6,4},{7,5},{8,10},{9,11},{10,... | collective-permute-start | bytes 110600 | tf_op jit(solution)/shard_map/ppermute | solution.py:387
  10.7 2.3 %collective-permute-done = f32[1,72,128]{2,1,0:T(8,128)S(1)} collective-permute-done((f32[1,72,128]{2,1,0:T(8,128)S(1)}, f32[1,72,128]{2,1,0:T(8,128)S(1)}, u32[]{:S(2)}, u32[]{:S(2)}) %collective-permute-start) | collective-permute-done | bytes 36896 | tf_op jit(solution)/shard_map/ppermute | solution.py:387
  13.1 1.5 %collective-permute-start.1 = (f32[2,72,128]{2,1,0:T(8,128)S(1)}, f32[2,72,128]{2,1,0:T(8,128)S(1)}, u32[]{:S(2)}, u32[]{:S(2)}) collective-permute-start(f32[2,72,128]{2,1,0:T(8,128)S(1)} %pad_maximum_fusion.1), channel_id=1, source_target_pairs={{0,1},{1,0},{2,3},{3,2},{4,5},{5,4},{6,7},{7,6},{8,9},{9,8},{10,11... | collective-permute-start | bytes 221192 | tf_op jit(solution)/shard_map/ppermute | solution.py:387
  14.6 2.8 %collective-permute-done.1 = f32[2,72,128]{2,1,0:T(8,128)S(1)} collective-permute-done((f32[2,72,128]{2,1,0:T(8,128)S(1)}, f32[2,72,128]{2,1,0:T(8,128)S(1)}, u32[]{:S(2)}, u32[]{:S(2)}) %collective-permute-start.1) | collective-permute-done | bytes 73760 | tf_op jit(solution)/shard_map/ppermute | solution.py:387
  17.4 1.3 %row.1 = (f32[4,8,128]{2,1,0:T(8,128)S(1)}, f32[4,4,128]{2,1,0:T(4,128)S(1)}, f32[4,4,128]{2,1,0:T(4,128)S(1)}, f32[192,128]{1,0:T(8,128)S(1)}, f32[64,64]{1,0:T...) custom-call(f32[4,72,128]{2,1,0:T(8,128)S(1)} %pad_maximum_fusion.row_ref), custom_call_target="tpu_custom_call" | custom-call | tf_op jit(solution)/shard_map/row/pallas_call | solution.py:363
  18.7 0.0 collective-permute-start.2
  18.7 2.8 %collective-permute-start.3 = (f32[4,4,128]{2,1,0:T(4,128)S(1)}, f32[4,4,128]{2,1,0:T(4,128)S(1)}, u32[]{:S(2)}, u32[]{:S(2)}) collective-permute-start(f32[4,4,128]{2,1,0:T(4,128)S(1)} %get-tuple-element.20), channel_id=1, source_target_pairs={{4,8},{12,16},{20,24},{0,28},{8,4},{16,12},{24,20},{28,0},{5,9},{1... | collective-permute-start | bytes 24584 | tf_op jit(solution)/shard_map/ppermute | solution.py:379
  21.5 1.4 %collective-permute-done.3.other_ref = f32[4,4,128]{2,1,0:T(4,128)S(1)} collective-permute-done((f32[4,4,128]{2,1,0:T(4,128)S(1)}, f32[4,4,128]{2,1,0:T(4,128)S(1)}, u32[]{:S(2)}, u32[]{:S(2)}) %collective-permute-start.3) | collective-permute-done | bytes 8224 | tf_op jit(solution)/shard_map/ppermute | solution.py:379
  22.9 1.5 %step.1 = (f32[8,128]{1,0:T(8,128)S(1)}, f32[8,128]{1,0:T(8,128)S(1)}, f32[8,128]{1,0:T(8,128)S(1)}, f32[8,128]{1,0:T(8,128)S(1)}, f32[8,128]{1,0:T(8,128)S(1)}, /*index=5*/f32[8,128]{1,0:T(8,128)S(1)}) custom-call(f32[4,72,128]{2,1,0:T(8,128)S(1)} %pad_maximum_fusion.row_ref, f32[4,8,128]{2,1,0:T(8,128)S(1)} %get-tuple-element.18.total_ref, ...), custom_call_target="tpu_custom_call" | custom-call | tf_op jit(solution)/shard_map/step/pallas_call | solution.py:363
  24.4 0.1 collective-permute-start.4
  24.4 2.7 %collective-permute-start.5 = (f32[8,128]{1,0:T(8,128)S(1)}, f32[8,128]{1,0:T(8,128)S(1)}, u32[]{:S(2)}, u32[]{:S(2)}) collective-permute-start(f32[8,128]{1,0:T(8,128)S(1)} %get-tuple-element.31), channel_id=1, source_target_pairs={{4,8},{12,16},{20,24},{0,28},{8,4},{16,12},{24,20},{28,0},{5,9},{1... | collective-permute-start | bytes 12296 | tf_op jit(solution)/shard_map/ppermute | solution.py:379
  27.1 1.3 %collective-permute-done.5.other_ref = f32[8,128]{1,0:T(8,128)S(1)} collective-permute-done((f32[8,128]{1,0:T(8,128)S(1)}, f32[8,128]{1,0:T(8,128)S(1)}, u32[]{:S(2)}, u32[]{:S(2)}) %collective-permute-start.5) | collective-permute-done | bytes 4128 | tf_op jit(solution)/shard_map/ppermute | solution.py:379
  28.4 0.8 %end.1 = (f32[3,128]{1,0:T(4,128)}, f32[3,128]{1,0:T(4,128)}) custom-call(f32[4,72,128]{2,1,0:T(8,128)S(1)} %pad_maximum_fusion.row_ref, f32[8,128]{1,0:T(8,128)S(1)} %get-tuple-element.26.state_ref, f32[8,128]{1,0:T(8,128)S(1)} %get-tuple-element.27.near_ref, f32[8,128]{1,0:T(8,128)S(1)} %get-tuple-element.28.low_ref, ...), custom_call_target="tpu_custom_call" | custom-call | tf_op jit(solution)/shard_map/end/pallas_call | solution.py:363
  (16 shorter events, 0.0 us)
Async XLA Ops:
  0.6 0.7 %copy-start.5 = (f32[3,128]{1,0:T(4,128)S(1)}, f32[3,128]{1,0:T(4,128)}, u32[]{:S(2)}) copy-start(f32[3,128]{1,0:T(4,128)} %speed_ref.1) | copy-start | bytes 4612
  0.6 0.7 %copy-start.4 = (f32[3,128]{1,0:T(4,128)S(1)}, f32[3,128]{1,0:T(4,128)}, u32[]{:S(2)}) copy-start(f32[3,128]{1,0:T(4,128)} %place_ref.1) | copy-start | bytes 4612
  0.7 0.7 %copy-start.8 = (f32[256]{0:T(256)S(1)}, f32[256]{0:T(256)}, u32[]{:S(2)}) copy-start(f32[256]{0:T(256)} %param.16) | copy-start | bytes 3076
  0.7 0.7 %copy-start.9 = (f32[128]{0:T(128)S(1)}, f32[128]{0:T(128)}, u32[]{:S(2)}) copy-start(f32[128]{0:T(128)} %param.14) | copy-start | bytes 1540
  1.3 0.7 %copy-start = (f32[24,24]{1,0:T(8,128)S(1)}, f32[24,24]{1,0:T(8,128)}, u32[]{:S(2)}) copy-start(f32[24,24]{1,0:T(8,128)} %stiff_ref.1) | copy-start | bytes 6916
  2.1 0.7 %copy-start.1 = (s32[8,256]{1,0:T(8,128)S(1)}, s32[8,256]{1,0:T(8,128)}, u32[]{:S(2)}) copy-start(s32[8,256]{1,0:T(8,128)} %connect_ref.1) | copy-start | bytes 24580
  2.8 0.7 %copy-start.2 = (s32[16,128]{1,0:T(8,128)S(1)}, s32[16,128]{1,0:T(8,128)}, u32[]{:S(2)}) copy-start(s32[16,128]{1,0:T(8,128)} %patch_ref.1) | copy-start | bytes 24580
  3.5 0.7 %copy-start.3 = (s32[16,128]{1,0:T(8,128)S(1)}, s32[16,128]{1,0:T(8,128)}, u32[]{:S(2)}) copy-start(s32[16,128]{1,0:T(8,128)} %map_ref.1) | copy-start | bytes 24580
  4.1 0.7 %copy-start.6 = (f32[3,128]{1,0:T(4,128)S(1)}, f32[3,128]{1,0:T(4,128)}, u32[]{:S(2)}) copy-start(f32[3,128]{1,0:T(4,128)} %rest_ref.1) | copy-start | bytes 4612
  4.8 0.7 %copy-start.7 = (s32[4,128]{1,0:T(4,128)S(1)}, s32[4,128]{1,0:T(4,128)}, u32[]{:S(2)}) copy-start(s32[4,128]{1,0:T(4,128)} %lists_ref.1) | copy-start | bytes 6148
  5.5 0.7 %copy-start.10 = (s32[16]{0:T(128)S(1)}, s32[16]{0:T(128)}, u32[]{:S(2)}) copy-start(s32[16]{0:T(128)} %param.20) | copy-start | bytes 196
  6.6 6.4 %collective-permute-start = (f32[1,72,128]{2,1,0:T(8,128)S(1)}, f32[1,72,128]{2,1,0:T(8,128)S(1)}, u32[]{:S(2)}, u32[]{:S(2)}) collective-permute-start(f32[1,72,128]{2,1,0:T(8,128)S(1)} %bitcast.4), channel_id=1, source_target_pairs={{0,2},{1,3},{2,0},{3,1},{4,6},{5,7},{6,4},{7,5},{8,10},{9,11},{10,... | collective-permute-start | bytes 110600 | tf_op jit(solution)/shard_map/ppermute | solution.py:387
  13.1 4.4 %collective-permute-start.1 = (f32[2,72,128]{2,1,0:T(8,128)S(1)}, f32[2,72,128]{2,1,0:T(8,128)S(1)}, u32[]{:S(2)}, u32[]{:S(2)}) collective-permute-start(f32[2,72,128]{2,1,0:T(8,128)S(1)} %pad_maximum_fusion.1), channel_id=1, source_target_pairs={{0,1},{1,0},{2,3},{3,2},{4,5},{5,4},{6,7},{7,6},{8,9},{9,8},{10,11... | collective-permute-start | bytes 221192 | tf_op jit(solution)/shard_map/ppermute | solution.py:387
  18.7 2.8 %collective-permute-start.2 = (f32[4,4,128]{2,1,0:T(4,128)S(1)}, f32[4,4,128]{2,1,0:T(4,128)S(1)}, u32[]{:S(2)}, u32[]{:S(2)}) collective-permute-start(f32[4,4,128]{2,1,0:T(4,128)S(1)} %get-tuple-element.19), channel_id=1, source_target_pairs={{0,4},{8,12},{16,20},{24,28},{4,0},{12,8},{20,16},{28,24},{1,5},{9... | collective-permute-start | bytes 24584 | tf_op jit(solution)/shard_map/ppermute | solution.py:379
  18.7 4.1 %collective-permute-start.3 = (f32[4,4,128]{2,1,0:T(4,128)S(1)}, f32[4,4,128]{2,1,0:T(4,128)S(1)}, u32[]{:S(2)}, u32[]{:S(2)}) collective-permute-start(f32[4,4,128]{2,1,0:T(4,128)S(1)} %get-tuple-element.20), channel_id=1, source_target_pairs={{4,8},{12,16},{20,24},{0,28},{8,4},{16,12},{24,20},{28,0},{5,9},{1... | collective-permute-start | bytes 24584 | tf_op jit(solution)/shard_map/ppermute | solution.py:379
  24.4 2.8 %collective-permute-start.4 = (f32[8,128]{1,0:T(8,128)S(1)}, f32[8,128]{1,0:T(8,128)S(1)}, u32[]{:S(2)}, u32[]{:S(2)}) collective-permute-start(f32[8,128]{1,0:T(8,128)S(1)} %get-tuple-element.30), channel_id=1, source_target_pairs={{0,4},{8,12},{16,20},{24,28},{4,0},{12,8},{20,16},{28,24},{1,5},{9... | collective-permute-start | bytes 12296 | tf_op jit(solution)/shard_map/ppermute | solution.py:379
  24.4 4.0 %collective-permute-start.5 = (f32[8,128]{1,0:T(8,128)S(1)}, f32[8,128]{1,0:T(8,128)S(1)}, u32[]{:S(2)}, u32[]{:S(2)}) collective-permute-start(f32[8,128]{1,0:T(8,128)S(1)} %get-tuple-element.31), channel_id=1, source_target_pairs={{4,8},{12,16},{20,24},{0,28},{8,4},{16,12},{24,20},{28,0},{5,9},{1... | collective-permute-start | bytes 12296 | tf_op jit(solution)/shard_map/ppermute | solution.py:379

commit v4 on v3

--- a/solution.py
+++ b/solution.py
@@ -7,7 +7,6 @@
 from jax.experimental.pallas import tpu as pltpu
 from jax.sharding import PartitionSpec as P
 
-STEPS = 2
 
 time_step = 0.1
 penalty = 4.0
@@ -47,28 +46,31 @@
     return parts_ref[pl.ds(start, TILE, stride=TILE), :]
 
 
-def scatter(entries):
+def scatter(entries, chains=2):
     blocks = LANES // FINE
-    total = jnp.zeros((blocks * TILE, FINE), jnp.float32)
-    for coarse, fine, weights in entries:
-        wide = weights.shape[1]
-        shape = (blocks * TILE, wide)
-        block = (lax.broadcasted_iota(jnp.int32, shape, 0) // TILE).astype(jnp.float32).astype(jnp.bfloat16)
-        placed = jnp.where(
-            jnp.broadcast_to(coarse, shape).astype(jnp.bfloat16) == block,
-            jnp.concatenate([weights] * blocks, axis=0).astype(jnp.bfloat16),
-            jnp.zeros(shape, jnp.bfloat16),
-        )
-        shape = (FINE, wide)
-        node = lax.broadcasted_iota(jnp.int32, shape, 0).astype(jnp.float32).astype(jnp.bfloat16)
-        hot = jnp.where(
-            jnp.broadcast_to(fine, shape).astype(jnp.bfloat16) == node,
-            jnp.ones(shape, jnp.bfloat16),
-            jnp.zeros(shape, jnp.bfloat16),
-        )
-        total += lax.dot_general(placed, hot, (((1,), (1,)), ((), ())), preferred_element_type=jnp.float32)
-    tile = jnp.concatenate([total[b * TILE : (b + 1) * TILE] for b in range(blocks)], axis=1)
-    return tile + pltpu.roll(tile, 4, 0)
+    tiles = []
+    for first in range(min(chains, len(entries))):
+        total = jnp.zeros((blocks * TILE, FINE), jnp.float32)
+        for coarse, fine, weights in entries[first::chains]:
+            wide = weights.shape[1]
+            shape = (blocks * TILE, wide)
+            block = (lax.broadcasted_iota(jnp.int32, shape, 0) // TILE).astype(jnp.float32).astype(jnp.bfloat16)
+            placed = jnp.where(
+                jnp.broadcast_to(coarse, shape).astype(jnp.bfloat16) == block,
+                jnp.concatenate([weights] * blocks, axis=0).astype(jnp.bfloat16),
+                jnp.zeros(shape, jnp.bfloat16),
+            )
+            shape = (FINE, wide)
+            node = lax.broadcasted_iota(jnp.int32, shape, 0).astype(jnp.float32).astype(jnp.bfloat16)
+            hot = jnp.where(
+                jnp.broadcast_to(fine, shape).astype(jnp.bfloat16) == node,
+                jnp.ones(shape, jnp.bfloat16),
+                jnp.zeros(shape, jnp.bfloat16),
+            )
+            total += lax.dot_general(placed, hot, (((1,), (1,)), ((), ())), preferred_element_type=jnp.float32)
+        tile = jnp.concatenate([total[b * TILE : (b + 1) * TILE] for b in range(blocks)], axis=1)
+        tiles.append(tile + pltpu.roll(tile, 4, 0))
+    return sum(tiles[1:], tiles[0])
 
 
 def joined(entries):
@@ -269,7 +271,7 @@
 
     def unit(u):
         info = row_ref[slot_of(me, u, width), ROW_ELASTIC : ROW_ELASTIC + TILE, :]
-        total = scatter(contact_entries(width, patches, u, coarse_ref, fine_ref, parts_ref, back_ref)) + info
+        total = scatter(contact_entries(width, patches, u, coarse_ref, fine_ref, parts_ref, back_ref), 1) + info
         total_ref[u] = total
         low, high = face_values(total, info[4:5]), face_values(total, info[5:6])
         pair_ref[u] = jnp.where(side == 0, high, low)[0:4]
@@ -319,8 +321,6 @@
     each_unit(width, unit)
     state_ref[...] = next_ref[me]
     state = [next_ref[u] for u in range(width)]
-    indices = [idx_ref[g * count : (g + 1) * count, :] for g in range(3)]
-    put_contact(width, patches, state, indices, link_ref[...].astype(jnp.bfloat16), parts_ref, back_ref)
     around = [me, jnp.maximum(me - 1, 0), jnp.minimum(me + 1, width - 1)]
     base = ROW_PATCH + 2 * patches
     last = row_ref.shape[1] - TILE
@@ -332,6 +332,8 @@
         tail = row_ref[slot, last : last + TILE, :]
         units.append((next_ref[u][0:3], tail[0:3], connect, [tail[4 + k : 5 + k] for k in range(runs)]))
     elastic = elastic_entries(units, stiff_ref[...], element_ref)
+    indices = [idx_ref[g * count : (g + 1) * count, :] for g in range(3)]
+    put_contact(width, patches, state, indices, link_ref[...].astype(jnp.bfloat16), parts_ref, back_ref)
     totals = [
         scatter(entries + contact_entries(width, patches, u, coarse_ref, fine_ref, parts_ref, back_ref))
         for u, entries in zip(around, elastic)
@@ -359,24 +361,34 @@
     place_ref[...] = state_ref[0:3, :] + time_step * speed
 
 
-def call(kernel, name, outs, scratch, *args, result=pltpu.VMEM, keep=True):
+def call(kernel, outs, scratch, *args, result=pltpu.VMEM, keep=True):
     return pl.pallas_call(
         kernel,
-        name=name,
         out_shape=[result(shape, jnp.float32) for shape in outs],
         in_specs=[pl.BlockSpec(memory_space=pltpu.VMEM)] * len(args),
         out_specs=[pl.BlockSpec(memory_space=pltpu.VMEM)] * len(outs),
         scratch_shapes=[pltpu.VMEM(shape, jnp.float32) for shape in scratch],
-        compiler_params=pltpu.CompilerParams(vmem_limit_bytes=VMEM_GRANT),
+        compiler_params=pltpu.CompilerParams(vmem_limit_bytes=VMEM_GRANT if keep else None),
     )(*[pltpu.with_memory_space_constraint(arg, pltpu.VMEM) if keep else arg for arg in args])
 
 
-def swap(value, axis, first):
-    size = lax.axis_size(axis)
-    pairs = [(i, i + 1) for i in range(first, size - 1, 2)]
-    if first and size % 2 == 0:
-        pairs.append((0, size - 1))
-    return lax.ppermute(value, axis, pairs + [(j, i) for i, j in pairs])
+def swap(value, axis, first, other):
+    size, depth = lax.axis_size(axis), lax.axis_size(other)
+    pairs = []
+    for i in range(size):
+        partner = i + 1 - 2 * ((i - first) % 2)
+        for k in range(depth):
+            if 0 <= partner < size:
+                pairs.append((i * depth + k, partner * depth + k))
+            elif depth % 2 == 0:
+                pairs.append((i * depth + k, i * depth + (k ^ 1)))
+    return lax.ppermute(value, (axis, other), pairs)
+
+
+def both(pair, other):
+    other = swap(other, "mx", 1, "my")
+    pair = swap(pair, "mx", 0, "my")
+    return pair, other
 
 
 def gather_row(record, axis):
@@ -414,7 +426,6 @@
     parts = (TILE * count, LANES)
     record, stiff = call(
         pack_kernel,
-        "pack",
         [(ROW_PATCH + 2 * patches + runs * corners + TILE, LANES), stiffness.shape],
         [element_parts],
         positions, velocities, rest_positions, mass, element_nodes, modulus, stiffness, shared_lists, patch_nodes,
@@ -423,25 +434,21 @@
     row = gather_row(record, "my")
     total, pair, other, *tables = call(
         functools.partial(row_kernel, width, patches),
-        "row",
         [(width, TILE, LANES), (width, 4, LANES), (width, 4, LANES), (3 * count, LANES), (count, count)]
         + [(2 * count, LANES)] * 2,
         [parts, parts],
         row,
     )
-    pair, other = swap(pair, "mx", 0), swap(other, "mx", 1)
+    pair, other = both(pair, other)
     state, near, low, high, pair, other = call(
         functools.partial(step_kernel, width, patches, corners),
-        "step",
         [tile] * 6,
         [(width, TILE, LANES), (3 * element_parts[0], LANES), parts, parts],
         row, total, pair, other, *tables, stiff,
     )
-    pair, other = swap(pair, "mx", 0), swap(other, "mx", 1)
+    pair, other = both(pair, other)
     outs = [(3, LANES), (3, LANES)]
-    return tuple(
-        call(end_kernel, "end", outs, [], row, state, near, low, high, pair, other, result=jax.ShapeDtypeStruct)
-    )
+    return tuple(call(end_kernel, outs, [], row, state, near, low, high, pair, other, result=jax.ShapeDtypeStruct))
 
 
 def solution(mesh):

time: 29.7 us -> 23.9 us (0.80)
  local copies, waits for them, and re-layouts: 5.49 us -> 0 us
  starting transfers between devices: 11.1 us -> 8.88 us
  waiting for transfers between devices: 7.87 us -> 9.41 us
  Pallas kernels: 4.02 us -> 4.76 us
    unnamed x22 -> x0, local copies, waits for them, and re-layouts: 5.49 us -> none
    ppermute x4, starting transfers between devices: 5.52 us -> 3.24 us  [swap(): return lax.ppermute(value, (axis, other), pairs)]
    ppermute x4, waiting for transfers between devices: 2.69 us -> 4.23 us  [swap(): return lax.ppermute(value, (axis, other), pairs)]
    pallas_call x4, Pallas kernels: 4.02 us -> 4.76 us  [call(): pl.pallas_call(kernel, out_shape=[result(shape, jnp.float32) for shape in...]
where the time goes in v4:
time: 23.9 us; the launch traced here: 23.7 us
  waiting for transfers between devices  9.41 us (39%)
  starting transfers between devices  8.88 us (37%)
  Pallas kernels  4.76 us (20%)
  between operations  0.66 us (3%)
    ppermute x2, starting transfers between devices, gather_row(): other = lax.ppermute(held, axis, [(i, i ^ step) for i in range(size)])  5.64 us
    ppermute x2, waiting for transfers between devices, gather_row(): other = lax.ppermute(held, axis, [(i, i ^ step) for i in range(size)])  5.17 us
    pallas_call x4, Pallas kernels, call(): pl.pallas_call(kernel, out_shape=[result(shape, jnp.float32) for shape in...  4.76 us
    ppermute x4, waiting for transfers between devices, swap(): return lax.ppermute(value, (axis, other), pairs)  4.23 us
    ppermute x4, starting transfers between devices, swap(): return lax.ppermute(value, (axis, other), pairs)  3.24 us
  transfers between devices with their start and end apart: 6, of which 4 were waited for; matrix products, arithmetic and copies ran while one was open for 0% of the time, Pallas kernels for 0%

profile of v4, /device:TPU:0, one launch (start us, length us, event | category | flops | bytes accessed | tf_op | source)
XLA Modules:
  0.0 23.7 jit_solution(6663182446704472525)
XLA Ops:
  0.6 1.3 %shard_map.122 = (f32[72,128]{1,0:T(8,128)S(1)}, f32[24,24]{1,0:T(8,128)S(1)}) custom-call(f32[3,128]{1,0:T(4,128)} %place_ref.1, f32[3,128]{1,0:T(4,128)} %speed_ref.1, f32[3,128]{1,0:T(4,128)} %rest_ref.1, f32[1,128]{1,0:T(1,128)} %bitcast.8, s32[8,256]{1,0:T(8,128)} %connect_ref.1, f32[1,256]{1,0:T(1,128)} %bitcast.7, f32[24,24]{1,0:T(8,128)} %stiff_ref.1, ...), custom_call_target="tpu_custom_call" | custom-call | tf_op jit(solution)/shard_map/pallas_call | solution.py:365
  1.9 4.1 %collective-permute-start = (f32[1,72,128]{2,1,0:T(8,128)S(1)}, f32[1,72,128]{2,1,0:T(8,128)S(1)}, u32[]{:S(2)}, u32[]{:S(2)}) collective-permute-start(f32[1,72,128]{2,1,0:T(8,128)S(1)} %bitcast.4), channel_id=1, source_target_pairs={{0,2},{1,3},{2,0},{3,1},{4,6},{5,7},{6,4},{7,5},{8,10},{9,11},{10,... | collective-permute-start | bytes 110600 | tf_op jit(solution)/shard_map/ppermute | solution.py:399
  6.1 2.3 %collective-permute-done = f32[1,72,128]{2,1,0:T(8,128)S(1)} collective-permute-done((f32[1,72,128]{2,1,0:T(8,128)S(1)}, f32[1,72,128]{2,1,0:T(8,128)S(1)}, u32[]{:S(2)}, u32[]{:S(2)}) %collective-permute-start) | collective-permute-done | bytes 36896 | tf_op jit(solution)/shard_map/ppermute | solution.py:399
  8.4 1.5 %collective-permute-start.1 = (f32[2,72,128]{2,1,0:T(8,128)S(1)}, f32[2,72,128]{2,1,0:T(8,128)S(1)}, u32[]{:S(2)}, u32[]{:S(2)}) collective-permute-start(f32[2,72,128]{2,1,0:T(8,128)S(1)} %pad_maximum_fusion.1), channel_id=1, source_target_pairs={{0,1},{1,0},{2,3},{3,2},{4,5},{5,4},{6,7},{7,6},{8,9},{9,8},{10,11... | collective-permute-start | bytes 221192 | tf_op jit(solution)/shard_map/ppermute | solution.py:399
  9.9 2.8 %collective-permute-done.1 = f32[2,72,128]{2,1,0:T(8,128)S(1)} collective-permute-done((f32[2,72,128]{2,1,0:T(8,128)S(1)}, f32[2,72,128]{2,1,0:T(8,128)S(1)}, u32[]{:S(2)}, u32[]{:S(2)}) %collective-permute-start.1) | collective-permute-done | bytes 73760 | tf_op jit(solution)/shard_map/ppermute | solution.py:399
  12.8 1.3 %shard_map.123 = (f32[4,8,128]{2,1,0:T(8,128)S(1)}, f32[4,4,128]{2,1,0:T(4,128)S(1)}, f32[4,4,128]{2,1,0:T(4,128)S(1)}, f32[192,128]{1,0:T(8,128)S(1)}, f32[64,6...) custom-call(f32[4,72,128]{2,1,0:T(8,128)S(1)} %pad_maximum_fusion.row_ref), custom_call_target="tpu_custom_call" | custom-call | tf_op jit(solution)/shard_map/pallas_call | solution.py:365
  14.1 0.0 collective-permute-start.2
  14.1 1.6 %collective-permute-start.3 = (f32[4,4,128]{2,1,0:T(4,128)S(1)}, f32[4,4,128]{2,1,0:T(4,128)S(1)}, u32[]{:S(2)}, u32[]{:S(2)}) collective-permute-start(f32[4,4,128]{2,1,0:T(4,128)S(1)} %get-tuple-element.20), channel_id=1, source_target_pairs={{0,1},{1,0},{2,3},{3,2},{4,8},{5,9},{6,10},{7,11},{8,4},{9,5},{10,... | collective-permute-start | bytes 24584 | tf_op jit(solution)/shard_map/ppermute | solution.py:385
  15.7 0.0 collective-permute-done.2.pair_ref
  15.7 2.1 %collective-permute-done.3.other_ref = f32[4,4,128]{2,1,0:T(4,128)S(1)} collective-permute-done((f32[4,4,128]{2,1,0:T(4,128)S(1)}, f32[4,4,128]{2,1,0:T(4,128)S(1)}, u32[]{:S(2)}, u32[]{:S(2)}) %collective-permute-start.3) | collective-permute-done | bytes 8224 | tf_op jit(solution)/shard_map/ppermute | solution.py:385
  17.8 1.4 %shard_map.124 = (f32[8,128]{1,0:T(8,128)S(1)}, f32[8,128]{1,0:T(8,128)S(1)}, f32[8,128]{1,0:T(8,128)S(1)}, f32[8,128]{1,0:T(8,128)S(1)}, f32[8,128]{1,0:T(8,128)S(1)}, /*index=5*/f32[8,128]{1,0:T(8,128)S(1)}) custom-call(f32[4,72,128]{2,1,0:T(8,128)S(1)} %pad_maximum_fusion.row_ref, f32[4,8,128]{2,1,0:T(8,128)S(1)} %get-tuple-element.18.total_ref, ...), custom_call_target="tpu_custom_call" | custom-call | tf_op jit(solution)/shard_map/pallas_call | solution.py:365
  19.2 0.1 collective-permute-start.4
  19.3 1.5 %collective-permute-start.5 = (f32[8,128]{1,0:T(8,128)S(1)}, f32[8,128]{1,0:T(8,128)S(1)}, u32[]{:S(2)}, u32[]{:S(2)}) collective-permute-start(f32[8,128]{1,0:T(8,128)S(1)} %get-tuple-element.31), channel_id=1, source_target_pairs={{0,1},{1,0},{2,3},{3,2},{4,8},{5,9},{6,10},{7,11},{8,4},{9,5},{10,... | collective-permute-start | bytes 12296 | tf_op jit(solution)/shard_map/ppermute | solution.py:385
  20.8 0.0 collective-permute-done.4.pair_ref
  20.8 2.1 %collective-permute-done.5.other_ref = f32[8,128]{1,0:T(8,128)S(1)} collective-permute-done((f32[8,128]{1,0:T(8,128)S(1)}, f32[8,128]{1,0:T(8,128)S(1)}, u32[]{:S(2)}, u32[]{:S(2)}) %collective-permute-start.5) | collective-permute-done | bytes 4128 | tf_op jit(solution)/shard_map/ppermute | solution.py:385
  22.9 0.8 %shard_map.125 = (f32[3,128]{1,0:T(4,128)}, f32[3,128]{1,0:T(4,128)}) custom-call(f32[4,72,128]{2,1,0:T(8,128)S(1)} %pad_maximum_fusion.row_ref, f32[8,128]{1,0:T(8,128)S(1)} %get-tuple-element.26.state_ref, f32[8,128]{1,0:T(8,128)S(1)} %get-tuple-element.27.near_ref, f32[8,128]{1,0:T(8,128)S(1)} %get-tuple-element.28.low_ref, ...), custom_call_target="tpu_custom_call" | custom-call | tf_op jit(solution)/shard_map/pallas_call | solution.py:365
  (2 shorter events, 0.0 us)
Async XLA Ops:
  1.9 6.5 %collective-permute-start = (f32[1,72,128]{2,1,0:T(8,128)S(1)}, f32[1,72,128]{2,1,0:T(8,128)S(1)}, u32[]{:S(2)}, u32[]{:S(2)}) collective-permute-start(f32[1,72,128]{2,1,0:T(8,128)S(1)} %bitcast.4), channel_id=1, source_target_pairs={{0,2},{1,3},{2,0},{3,1},{4,6},{5,7},{6,4},{7,5},{8,10},{9,11},{10,... | collective-permute-start | bytes 110600 | tf_op jit(solution)/shard_map/ppermute | solution.py:399
  8.4 4.4 %collective-permute-start.1 = (f32[2,72,128]{2,1,0:T(8,128)S(1)}, f32[2,72,128]{2,1,0:T(8,128)S(1)}, u32[]{:S(2)}, u32[]{:S(2)}) collective-permute-start(f32[2,72,128]{2,1,0:T(8,128)S(1)} %pad_maximum_fusion.1), channel_id=1, source_target_pairs={{0,1},{1,0},{2,3},{3,2},{4,5},{5,4},{6,7},{7,6},{8,9},{9,8},{10,11... | collective-permute-start | bytes 221192 | tf_op jit(solution)/shard_map/ppermute | solution.py:399
  14.1 1.6 %collective-permute-start.2 = (f32[4,4,128]{2,1,0:T(4,128)S(1)}, f32[4,4,128]{2,1,0:T(4,128)S(1)}, u32[]{:S(2)}, u32[]{:S(2)}) collective-permute-start(f32[4,4,128]{2,1,0:T(4,128)S(1)} %get-tuple-element.19), channel_id=1, source_target_pairs={{0,4},{1,5},{2,6},{3,7},{4,0},{5,1},{6,2},{7,3},{8,12},{9,13},{10,... | collective-permute-start | bytes 24584 | tf_op jit(solution)/shard_map/ppermute | solution.py:385
  14.1 3.7 %collective-permute-start.3 = (f32[4,4,128]{2,1,0:T(4,128)S(1)}, f32[4,4,128]{2,1,0:T(4,128)S(1)}, u32[]{:S(2)}, u32[]{:S(2)}) collective-permute-start(f32[4,4,128]{2,1,0:T(4,128)S(1)} %get-tuple-element.20), channel_id=1, source_target_pairs={{0,1},{1,0},{2,3},{3,2},{4,8},{5,9},{6,10},{7,11},{8,4},{9,5},{10,... | collective-permute-start | bytes 24584 | tf_op jit(solution)/shard_map/ppermute | solution.py:385
  19.2 1.6 %collective-permute-start.4 = (f32[8,128]{1,0:T(8,128)S(1)}, f32[8,128]{1,0:T(8,128)S(1)}, u32[]{:S(2)}, u32[]{:S(2)}) collective-permute-start(f32[8,128]{1,0:T(8,128)S(1)} %get-tuple-element.30), channel_id=1, source_target_pairs={{0,4},{1,5},{2,6},{3,7},{4,0},{5,1},{6,2},{7,3},{8,12},{9,13},{10,... | collective-permute-start | bytes 12296 | tf_op jit(solution)/shard_map/ppermute | solution.py:385
  19.3 3.6 %collective-permute-start.5 = (f32[8,128]{1,0:T(8,128)S(1)}, f32[8,128]{1,0:T(8,128)S(1)}, u32[]{:S(2)}, u32[]{:S(2)}) collective-permute-start(f32[8,128]{1,0:T(8,128)S(1)} %get-tuple-element.31), channel_id=1, source_target_pairs={{0,1},{1,0},{2,3},{3,2},{4,8},{5,9},{6,10},{7,11},{8,4},{9,5},{10,... | collective-permute-start | bytes 12296 | tf_op jit(solution)/shard_map/ppermute | solution.py:385

commit v5 on v4

--- a/solution.py
+++ b/solution.py
@@ -226,18 +226,18 @@
     return pick(tile, jnp.broadcast_to(row.astype(jnp.int32), tile.shape))
 
 
-def row_kernel(
-    width, patches, row_ref, total_ref, pair_ref, other_ref, idx_ref, link_ref, coarse_ref, fine_ref, parts_ref, back_ref
-):
+def row_kernel(width, patches, where, *refs):
+    total_ref, pair_ref, other_ref, keep_ref, idx_ref, link_ref, coarse_ref, fine_ref, parts_ref, back_ref = refs[-10:]
     me = lax.axis_index("my")
     side = lax.rem(lax.axis_index("mx"), 2)
     count = width * patches
-    slot = [slot_of(me, u, width) for u in range(width)]
-    state = [row_ref[slot[u], 0:TILE, :] for u in range(width)]
-    nodes = jnp.concatenate([row_ref[slot[u], ROW_PATCH : ROW_PATCH + patches, :] for u in range(width)], axis=0)
-    pairs = jnp.concatenate(
-        [row_ref[slot[u], ROW_PATCH + patches : ROW_PATCH + 2 * patches, :] for u in range(width)], axis=0
-    )
+    record = [refs[piece].at[place] for piece, place in where]
+    state = [ref[0:TILE, :] for ref in record]
+    nodes = jnp.concatenate([ref[ROW_PATCH : ROW_PATCH + patches, :] for ref in record], axis=0)
+    pairs = jnp.concatenate([ref[ROW_PATCH + patches : ROW_PATCH + 2 * patches, :] for ref in record], axis=0)
+    for s, ref in enumerate(record):
+        keep_ref[s, 0:ROW_PATCH, :] = ref[0:ROW_PATCH, :]
+        keep_ref[s, ROW_PATCH:, :] = ref[ROW_PATCH + 2 * patches :, :]
     lane = lax.broadcasted_iota(jnp.int32, (patches, LANES), 1)
     line = lax.broadcasted_iota(jnp.int32, (patches, LANES), 0)
     owner_col = jnp.concatenate(
@@ -247,9 +247,9 @@
         ],
         axis=0,
     )
-    p = lax.broadcasted_iota(jnp.int32, (count, count), 0).astype(jnp.float32)
-    q = lax.broadcasted_iota(jnp.int32, (count, count), 1).astype(jnp.float32)
-    owner_row = jnp.sum(jnp.where(p == q, owner_col, 0.0), axis=0, keepdims=True)
+    row, col = [lax.broadcasted_iota(jnp.int32, (count, count), axis) for axis in (0, 1)]
+    owner_row = jnp.sum(jnp.where(row == col, owner_col, 0.0), axis=0, keepdims=True)
+    p, q = [(((at // patches) ^ me) * patches + at % patches).astype(jnp.float32) for at in (row, col)]
     same = owner_col == owner_row
     after = jnp.min(jnp.where(same, jnp.where(q > p, q, q + count), 3.0 * count), axis=1, keepdims=True)
     after = jnp.where(after >= count, after - count, after)
@@ -260,7 +260,7 @@
     link_ref[...] = back
     back = back.astype(jnp.bfloat16)
     target = pick(route(link, nodes), pairs.astype(jnp.int32))
-    device = jnp.broadcast_to(jnp.floor(after / patches), (count, LANES))
+    device = jnp.broadcast_to(jnp.floor(after / patches).astype(jnp.int32) ^ me, (count, LANES)).astype(jnp.float32)
     idx_ref[0:count, :] = nodes
     idx_ref[count : 2 * count, :] = target
     idx_ref[2 * count : 3 * count, :] = device
@@ -270,7 +270,7 @@
     put_contact(width, patches, state, (nodes, target, device), back, parts_ref, back_ref)
 
     def unit(u):
-        info = row_ref[slot_of(me, u, width), ROW_ELASTIC : ROW_ELASTIC + TILE, :]
+        info = keep_ref[u, ROW_ELASTIC : ROW_ELASTIC + TILE, :]
         total = scatter(contact_entries(width, patches, u, coarse_ref, fine_ref, parts_ref, back_ref), 1) + info
         total_ref[u] = total
         low, high = face_values(total, info[4:5]), face_values(total, info[5:6])
@@ -290,86 +290,102 @@
     return jnp.logical_and(partner >= 0, partner < size)
 
 
+def mid_kernel(width, keep_ref, total_ref, base_ref):
+    me = lax.axis_index("my")
+
+    def unit(s):
+        info = keep_ref[s, 0 : 2 * TILE, :]
+        u = me ^ s
+        down, up = jnp.maximum(u - 1, 0) ^ me, jnp.minimum(u + 1, width - 1) ^ me
+        low = face_values(total_ref[down], keep_ref[down, ROW_LISTS + 3 : ROW_LISTS + 4, :])
+        high = face_values(total_ref[up], keep_ref[up, ROW_LISTS + 2 : ROW_LISTS + 3, :])
+        tiles = [jnp.where(u > 0, low, 0.0), jnp.where(u < width - 1, high, 0.0)]
+        total = total_ref[s] + faces(tiles, [info[ROW_LISTS + 2 : ROW_LISTS + 3], info[ROW_LISTS + 3 : ROW_LISTS + 4]])
+        mass = info[ROW_MASS : ROW_MASS + 1]
+        base_ref[s, 0:4, :] = info[0:4]
+        base_ref[s, 4:7, :] = info[ROW_SPEED : ROW_SPEED + 3] + time_step * mass * total[0:3]
+
+    each_unit(width, unit)
+
+
+def mx_faces(lists, pair, other):
+    side = lax.rem(lax.axis_index("mx"), 2)
+    near, far = jnp.where(side == 0, lists[1:2], lists[0:1]), jnp.where(side == 0, lists[0:1], lists[1:2])
+    return faces([pair, jnp.where(inside("mx"), other, 0.0)], [near, far])
+
+
+def elements_of(keep_ref, next_ref, s, corners):
+    last = keep_ref.shape[1] - TILE
+    runs = (last - ROW_PATCH) // corners
+    connect = [keep_ref[s, ROW_PATCH + k * corners : ROW_PATCH + (k + 1) * corners, :] for k in range(runs)]
+    tail = keep_ref[s, last : last + TILE, :]
+    return next_ref[s][0:3], tail[0:3], connect, [tail[4 + k : 5 + k] for k in range(runs)]
+
+
 def step_kernel(
-    width, patches, corners, row_ref, total_ref, pair_ref, other_ref, idx_ref, link_ref, coarse_ref, fine_ref, stiff_ref,
-    state_ref, near_ref, low_ref, high_ref, send_ref, far_ref, next_ref, element_ref, parts_ref, back_ref,
+    width, patches, corners, keep_ref, base_ref, pair_ref, other_ref, idx_ref, link_ref, coarse_ref, fine_ref, stiff_ref,
+    next_ref, near_ref, send_ref, far_ref, parts_ref, back_ref, element_ref,
+):
+    side = lax.rem(lax.axis_index("mx"), 2)
+    count = width * patches
+    blank = jnp.zeros((4, LANES), jnp.float32)
+
+    def unit(s):
+        base = base_ref[s]
+        lists = keep_ref[s, ROW_LISTS : ROW_LISTS + 4, :]
+        pair, other = [jnp.concatenate([ref[s], blank], axis=0) for ref in (pair_ref, other_ref)]
+        speed = base[4:7] + time_step * base[3:4] * mx_faces(lists, pair, other)[0:3]
+        next_ref[s, 0:3, :] = base[0:3] + time_step * speed
+        next_ref[s, 4:7, :] = speed
+
+    each_unit(width, unit)
+    (elastic,) = elastic_entries([elements_of(keep_ref, next_ref, 0, corners)], stiff_ref[...], element_ref)
+    state = [next_ref[s] for s in range(width)]
+    indices = [idx_ref[g * count : (g + 1) * count, :] for g in range(3)]
+    put_contact(width, patches, state, indices, link_ref[...].astype(jnp.bfloat16), parts_ref, back_ref)
+    total = scatter(elastic + contact_entries(width, patches, 0, coarse_ref, fine_ref, parts_ref, back_ref))
+    near_ref[...] = total
+    lists = keep_ref[0, ROW_LISTS : ROW_LISTS + 4, :]
+    low, high = face_values(total, lists[0:1]), face_values(total, lists[1:2])
+    send_ref[...] = jnp.where(side == 0, high, low)
+    far_ref[...] = jnp.where(side == 0, low, high)
+
+
+def spare_kernel(
+    width, patches, corners, keep_ref, next_ref, near_ref, coarse_ref, fine_ref, parts_ref, back_ref, stiff_ref,
+    total_ref, element_ref,
 ):
     me = lax.axis_index("my")
-    side = lax.rem(lax.axis_index("mx"), 2)
-    joins = inside("mx")
-    count = width * patches
-    blank = jnp.zeros((4, LANES), jnp.float32)
-
-    def unit(u):
-        info = row_ref[slot_of(me, u, width), 0 : 2 * TILE, :]
-        lists = info[ROW_LISTS : ROW_LISTS + 4]
-        down, up = jnp.maximum(u - 1, 0), jnp.minimum(u + 1, width - 1)
-        low = face_values(total_ref[down], row_ref[slot_of(me, down, width), ROW_LISTS + 3 : ROW_LISTS + 4, :])
-        high = face_values(total_ref[up], row_ref[slot_of(me, up, width), ROW_LISTS + 2 : ROW_LISTS + 3, :])
-        tiles = [
-            jnp.concatenate([pair_ref[u], blank], axis=0),
-            jnp.where(joins, jnp.concatenate([other_ref[u], blank], axis=0), 0.0),
-            jnp.where(u > 0, low, 0.0),
-            jnp.where(u < width - 1, high, 0.0),
-        ]
-        near, far = jnp.where(side == 0, lists[1:2], lists[0:1]), jnp.where(side == 0, lists[0:1], lists[1:2])
-        total = total_ref[u] + faces(tiles, [near, far, lists[2:3], lists[3:4]])
-        speed = info[ROW_SPEED : ROW_SPEED + 3] + time_step * info[ROW_MASS : ROW_MASS + 1] * total[0:3]
-        next_ref[u, 0:3, :] = info[0:3] + time_step * speed
-        next_ref[u, 4:7, :] = speed
-
-    each_unit(width, unit)
-    state_ref[...] = next_ref[me]
-    state = [next_ref[u] for u in range(width)]
-    around = [me, jnp.maximum(me - 1, 0), jnp.minimum(me + 1, width - 1)]
-    base = ROW_PATCH + 2 * patches
-    last = row_ref.shape[1] - TILE
-    units = []
-    for u in around:
-        slot = slot_of(me, u, width)
-        runs = (last - base) // corners
-        connect = [row_ref[slot, base + k * corners : base + (k + 1) * corners, :] for k in range(runs)]
-        tail = row_ref[slot, last : last + TILE, :]
-        units.append((next_ref[u][0:3], tail[0:3], connect, [tail[4 + k : 5 + k] for k in range(runs)]))
-    elastic = elastic_entries(units, stiff_ref[...], element_ref)
-    indices = [idx_ref[g * count : (g + 1) * count, :] for g in range(3)]
-    put_contact(width, patches, state, indices, link_ref[...].astype(jnp.bfloat16), parts_ref, back_ref)
-    totals = [
-        scatter(entries + contact_entries(width, patches, u, coarse_ref, fine_ref, parts_ref, back_ref))
-        for u, entries in zip(around, elastic)
+    around = [jnp.maximum(me - 1, 0) ^ me, jnp.minimum(me + 1, width - 1) ^ me]
+    elastic = elastic_entries([elements_of(keep_ref, next_ref, s, corners) for s in around], stiff_ref[...], element_ref)
+    below, above = [
+        scatter(entries + contact_entries(width, patches, s, coarse_ref, fine_ref, parts_ref, back_ref), 1)
+        for s, entries in zip(around, elastic)
     ]
-    near_ref[...] = totals[0]
-    low = face_values(totals[1], row_ref[slot_of(me, around[1], width), ROW_LISTS + 3 : ROW_LISTS + 4, :])
-    high = face_values(totals[2], row_ref[slot_of(me, around[2], width), ROW_LISTS + 2 : ROW_LISTS + 3, :])
-    low_ref[...] = jnp.where(me > 0, low, 0.0)
-    high_ref[...] = jnp.where(me < width - 1, high, 0.0)
-    lists = row_ref[0, ROW_LISTS : ROW_LISTS + 4, :]
-    low, high = face_values(totals[0], lists[0:1]), face_values(totals[0], lists[1:2])
-    send_ref[...] = jnp.where(side == 0, high, low)
-    far_ref[...] = jnp.where(side == 0, low, high)
-
-
-def end_kernel(row_ref, state_ref, near_ref, low_ref, high_ref, pair_ref, other_ref, place_ref, speed_ref):
-    side = lax.rem(lax.axis_index("mx"), 2)
-    info = row_ref[0, 0 : 2 * TILE, :]
-    lists = info[ROW_LISTS : ROW_LISTS + 4]
-    near, far = jnp.where(side == 0, lists[1:2], lists[0:1]), jnp.where(side == 0, lists[0:1], lists[1:2])
-    tiles = [pair_ref[...], jnp.where(inside("mx"), other_ref[...], 0.0), low_ref[...], high_ref[...]]
-    total = near_ref[...] + faces(tiles, [near, far, lists[2:3], lists[3:4]])
-    speed = state_ref[4:7, :] + time_step * info[ROW_MASS : ROW_MASS + 1] * total[0:3]
+    low = face_values(below, keep_ref[around[0], ROW_LISTS + 3 : ROW_LISTS + 4, :])
+    high = face_values(above, keep_ref[around[1], ROW_LISTS + 2 : ROW_LISTS + 3, :])
+    lists = keep_ref[0, ROW_LISTS : ROW_LISTS + 4, :]
+    tiles = [jnp.where(me > 0, low, 0.0), jnp.where(me < width - 1, high, 0.0)]
+    total_ref[...] = near_ref[...] + faces(tiles, [lists[2:3], lists[3:4]])
+
+
+def end_kernel(keep_ref, next_ref, total_ref, pair_ref, other_ref, place_ref, speed_ref):
+    lists = keep_ref[0, ROW_LISTS : ROW_LISTS + 4, :]
+    total = total_ref[...] + mx_faces(lists, pair_ref[...], other_ref[...])
+    speed = next_ref[0, 4:7, :] + time_step * keep_ref[0, ROW_MASS : ROW_MASS + 1, :] * total[0:3]
     speed_ref[...] = speed
-    place_ref[...] = state_ref[0:3, :] + time_step * speed
-
-
-def call(kernel, outs, scratch, *args, result=pltpu.VMEM, keep=True):
+    place_ref[...] = next_ref[0, 0:3, :] + time_step * speed
+
+
+def call(kernel, outs, scratch, *args, result=pltpu.VMEM, placed=True):
     return pl.pallas_call(
         kernel,
         out_shape=[result(shape, jnp.float32) for shape in outs],
         in_specs=[pl.BlockSpec(memory_space=pltpu.VMEM)] * len(args),
         out_specs=[pl.BlockSpec(memory_space=pltpu.VMEM)] * len(outs),
         scratch_shapes=[pltpu.VMEM(shape, jnp.float32) for shape in scratch],
-        compiler_params=pltpu.CompilerParams(vmem_limit_bytes=VMEM_GRANT if keep else None),
-    )(*[pltpu.with_memory_space_constraint(arg, pltpu.VMEM) if keep else arg for arg in args])
+        compiler_params=pltpu.CompilerParams(vmem_limit_bytes=VMEM_GRANT if placed else None),
+    )(*[pltpu.with_memory_space_constraint(arg, pltpu.VMEM) if placed else arg for arg in args])
 
 
 def swap(value, axis, first, other):
@@ -393,22 +409,23 @@
 
 def gather_row(record, axis):
     size = lax.axis_size(axis)
-    held = record[None]
-    step = size // 2
-    while step:
-        other = lax.ppermute(held, axis, [(i, i ^ step) for i in range(size)])
-        held = jnp.concatenate([held, other], axis=0)
-        step //= 2
-    return held
-
-
-def slot_of(me, device, size):
-    apart = jnp.bitwise_xor(me, device)
-    slot, step, place = 0, size // 2, 1
-    while step:
-        slot = slot + place * (lax.div(apart, step) & 1)
-        step, place = step // 2, place * 2
-    return slot
+    steps = [size >> k for k in range(1, size.bit_length())]
+
+    def exchange(value, step):
+        return lax.ppermute(value, axis, [(i, i ^ step) for i in range(size)])
+
+    direct = []
+    for step in steps:
+        direct.append(exchange(record[None], step))
+    pieces, slots = [record[None]], [[0]]
+    for step, near in zip(steps, direct):
+        far, far_slots = pieces[1:], [s ^ step for held in slots[1:] for s in held]
+        pieces, slots = pieces + [near], slots + [[step]]
+        if far:
+            pieces.append(exchange(far[0] if len(far) == 1 else jnp.concatenate(far, axis=0), step))
+            slots.append(far_slots)
+    where = {s: (n, k) for n, held in enumerate(slots) for k, s in enumerate(held)}
+    return pieces, [where[s] for s in range(size)]
 
 
 def body(
@@ -429,26 +446,34 @@
         [(ROW_PATCH + 2 * patches + runs * corners + TILE, LANES), stiffness.shape],
         [element_parts],
         positions, velocities, rest_positions, mass, element_nodes, modulus, stiffness, shared_lists, patch_nodes,
-        patch_owner[None], pair_map, keep=False,
-    )
-    row = gather_row(record, "my")
-    total, pair, other, *tables = call(
-        functools.partial(row_kernel, width, patches),
-        [(width, TILE, LANES), (width, 4, LANES), (width, 4, LANES), (3 * count, LANES), (count, count)]
+        patch_owner[None], pair_map, placed=False,
+    )
+    pieces, where = gather_row(record, "my")
+    kept = (width, record.shape[0] - 2 * patches, LANES)
+    total, pair, other, keep, indices, link, *spots = call(
+        functools.partial(row_kernel, width, patches, where),
+        [(width, TILE, LANES), (width, 4, LANES), (width, 4, LANES), kept, (3 * count, LANES), (count, count)]
         + [(2 * count, LANES)] * 2,
         [parts, parts],
-        row,
-    )
+        *pieces,
+    )
+    states = (width, TILE, LANES)
     pair, other = both(pair, other)
-    state, near, low, high, pair, other = call(
-        functools.partial(step_kernel, width, patches, corners),
-        [tile] * 6,
-        [(width, TILE, LANES), (3 * element_parts[0], LANES), parts, parts],
-        row, total, pair, other, *tables, stiff,
+    (base,) = call(functools.partial(mid_kernel, width), [states], [], keep, total)
+    contact = functools.partial(step_kernel, width, patches, corners)
+    outs = [states, tile, tile, tile, parts, parts]
+    state, near, pair, other, *forces = call(
+        contact, outs, [element_parts], keep, base, pair, other, indices, link, *spots, stiff
     )
     pair, other = both(pair, other)
+    (total,) = call(
+        functools.partial(spare_kernel, width, patches, corners),
+        [tile],
+        [(2 * element_parts[0], LANES)],
+        keep, state, near, *spots, *forces, stiff,
+    )
     outs = [(3, LANES), (3, LANES)]
-    return tuple(call(end_kernel, outs, [], row, state, near, low, high, pair, other, result=jax.ShapeDtypeStruct))
+    return tuple(call(end_kernel, outs, [], keep, state, total, pair, other, result=jax.ShapeDtypeStruct))
 
 
 def solution(mesh):

time: 23.9 us -> 23.2 us (0.971)
  waiting for transfers between devices: 9.41 us -> 6.67 us
  starting transfers between devices: 8.88 us -> 10.2 us
  Pallas kernels: 4.76 us -> 5.53 us
    ppermute x2 -> x3, waiting for transfers between devices: 5.17 us -> 3.41 us  [exchange(): return lax.ppermute(value, axis, [(i, i ^ step) for i in range(size)])]
    ppermute x2 -> x3, starting transfers between devices: 5.64 us -> 7.12 us  [exchange(): return lax.ppermute(value, axis, [(i, i ^ step) for i in range(size)])]
    ppermute x4, waiting for transfers between devices: 4.23 us -> 3.27 us  [swap(): return lax.ppermute(value, (axis, other), pairs)]
    pallas_call x4 -> x6, Pallas kernels: 4.76 us -> 5.53 us  [call(): pl.pallas_call(kernel, out_shape=[result(shape, jnp.float32) for shape in...]
  transfers between devices with their start and end apart: 6 -> 7, of which waited for: 4 -> 5; matrix products, arithmetic and copies ran while one was open for 0% -> 0% of each run, Pallas kernels for 0% -> 5%
where the time goes in v5:
time: 23.2 us; the launch traced here: 23.1 us
  starting transfers between devices  10.2 us (44%)
  waiting for transfers between devices  6.67 us (29%)
  Pallas kernels  5.53 us (24%)
  between operations  0.69 us (3%)
    ppermute x3, starting transfers between devices, exchange(): return lax.ppermute(value, axis, [(i, i ^ step) for i in range(size)])  7.12 us
    pallas_call x6, Pallas kernels, call(): pl.pallas_call(kernel, out_shape=[result(shape, jnp.float32) for shape in...  5.53 us
    ppermute x3, waiting for transfers between devices, exchange(): return lax.ppermute(value, axis, [(i, i ^ step) for i in range(size)])  3.41 us
    ppermute x4, waiting for transfers between devices, swap(): return lax.ppermute(value, (axis, other), pairs)  3.27 us
    ppermute x4, starting transfers between devices, swap(): return lax.ppermute(value, (axis, other), pairs)  3.04 us
  transfers between devices with their start and end apart: 7, of which 5 were waited for; matrix products, arithmetic and copies ran while one was open for 0% of the time, Pallas kernels for 5%

profile of v5, /device:TPU:0, one launch (start us, length us, event | category | flops | bytes accessed | tf_op | source)
XLA Modules:
  0.0 23.1 jit_solution(14937275470201297801)
XLA Ops:
  0.6 1.3 %shard_map.122 = (f32[72,128]{1,0:T(8,128)S(1)}, f32[24,24]{1,0:T(8,128)S(1)}) custom-call(f32[3,128]{1,0:T(4,128)} %place_ref.1, f32[3,128]{1,0:T(4,128)} %speed_ref.1, f32[3,128]{1,0:T(4,128)} %rest_ref.1, f32[1,128]{1,0:T(1,128)} %bitcast.8, s32[8,256]{1,0:T(8,128)} %connect_ref.1, f32[1,256]{1,0:T(1,128)} %bitcast.7, f32[24,24]{1,0:T(8,128)} %stiff_ref.1, ...), custom_call_target="tpu_custom_call" | custom-call | tf_op jit(solution)/shard_map/pallas_call | solution.py:381
  1.9 4.1 %collective-permute-start = (f32[1,72,128]{2,1,0:T(8,128)S(1)}, f32[1,72,128]{2,1,0:T(8,128)S(1)}, u32[]{:S(2)}, u32[]{:S(2)}) collective-permute-start(f32[1,72,128]{2,1,0:T(8,128)S(1)} %bitcast.4), channel_id=1, source_target_pairs={{0,2},{1,3},{2,0},{3,1},{4,6},{5,7},{6,4},{7,5},{8,10},{9,11},{10,... | collective-permute-start | bytes 110600 | tf_op jit(solution)/shard_map/ppermute | solution.py:415
  6.1 1.6 %collective-permute-start.1 = (f32[1,72,128]{2,1,0:T(8,128)S(1)}, f32[1,72,128]{2,1,0:T(8,128)S(1)}, u32[]{:S(2)}, u32[]{:S(2)}) collective-permute-start(f32[1,72,128]{2,1,0:T(8,128)S(1)} %bitcast.5), channel_id=1, source_target_pairs={{0,1},{1,0},{2,3},{3,2},{4,5},{5,4},{6,7},{7,6},{8,9},{9,8},{10,11... | collective-permute-start | bytes 110600 | tf_op jit(solution)/shard_map/ppermute | solution.py:415
  7.7 0.9 %collective-permute-done.refs_1_ = f32[1,72,128]{2,1,0:T(8,128)S(1)} collective-permute-done((f32[1,72,128]{2,1,0:T(8,128)S(1)}, f32[1,72,128]{2,1,0:T(8,128)S(1)}, u32[]{:S(2)}, u32[]{:S(2)}) %collective-permute-start) | collective-permute-done | bytes 36896 | tf_op jit(solution)/shard_map/ppermute | solution.py:415
  8.5 1.4 %collective-permute-start.2 = (f32[1,72,128]{2,1,0:T(8,128)S(1)}, f32[1,72,128]{2,1,0:T(8,128)S(1)}, u32[]{:S(2)}, u32[]{:S(2)}) collective-permute-start(f32[1,72,128]{2,1,0:T(8,128)S(1)} %collective-permute-done.refs_1_), channel_id=1, source_target_pairs={{0,1},{1,0},{2,3},{3,2},{4,5},{5,4},{6,7},{7,6},{8,9},{9,8},{10,11... | collective-permute-start | bytes 110600 | tf_op jit(solution)/shard_map/ppermute | solution.py:415
  9.9 0.4 %collective-permute-done.1.refs_2_ = f32[1,72,128]{2,1,0:T(8,128)S(1)} collective-permute-done((f32[1,72,128]{2,1,0:T(8,128)S(1)}, f32[1,72,128]{2,1,0:T(8,128)S(1)}, u32[]{:S(2)}, u32[]{:S(2)}) %collective-permute-start.1) | collective-permute-done | bytes 36896 | tf_op jit(solution)/shard_map/ppermute | solution.py:415
  10.4 2.1 %collective-permute-done.2.refs_3_ = f32[1,72,128]{2,1,0:T(8,128)S(1)} collective-permute-done((f32[1,72,128]{2,1,0:T(8,128)S(1)}, f32[1,72,128]{2,1,0:T(8,128)S(1)}, u32[]{:S(2)}, u32[]{:S(2)}) %collective-permute-start.2) | collective-permute-done | bytes 36896 | tf_op jit(solution)/shard_map/ppermute | solution.py:415
  12.5 1.3 %shard_map.123 = (f32[4,8,128]{2,1,0:T(8,128)S(1)}, f32[4,4,128]{2,1,0:T(4,128)S(1)}, f32[4,4,128]{2,1,0:T(4,128)S(1)}, f32[4,40,128]{2,1,0:T(8,128)S(1)}, f32[1...) custom-call(f32[1,72,128]{2,1,0:T(8,128)S(1)} %bitcast.6, ...), custom_call_target="tpu_custom_call" | custom-call | tf_op jit(solution)/shard_map/pallas_call | solution.py:381
  13.8 0.0 collective-permute-start.3
  13.8 1.5 %collective-permute-start.4 = (f32[4,4,128]{2,1,0:T(4,128)S(1)}, f32[4,4,128]{2,1,0:T(4,128)S(1)}, u32[]{:S(2)}, u32[]{:S(2)}) collective-permute-start(f32[4,4,128]{2,1,0:T(4,128)S(1)} %get-tuple-element.22), channel_id=1, source_target_pairs={{0,1},{1,0},{2,3},{3,2},{4,8},{5,9},{6,10},{7,11},{8,4},{9,5},{10,... | collective-permute-start | bytes 24584 | tf_op jit(solution)/shard_map/ppermute | solution.py:401
  15.3 0.3 %shard_map.124.base_ref = f32[4,8,128]{2,1,0:T(8,128)S(1)} custom-call(f32[4,40,128]{2,1,0:T(8,128)S(1)} %get-tuple-element.19.keep_ref, f32[4,8,128]{2,1,0:T(8,128)S(1)} %get-tuple-element.20.total_ref), custom_call_target="tpu_custom_call" | custom-call | tf_op jit(solution)/shard_map/pallas_call | solution.py:381
  15.6 0.0 collective-permute-done.3.pair_ref
  15.6 1.9 %collective-permute-done.4.other_ref = f32[4,4,128]{2,1,0:T(4,128)S(1)} collective-permute-done((f32[4,4,128]{2,1,0:T(4,128)S(1)}, f32[4,4,128]{2,1,0:T(4,128)S(1)}, u32[]{:S(2)}, u32[]{:S(2)}) %collective-permute-start.4) | collective-permute-done | bytes 8224 | tf_op jit(solution)/shard_map/ppermute | solution.py:401
  17.5 1.0 %shard_map.125 = (f32[4,8,128]{2,1,0:T(8,128)S(1)}, f32[8,128]{1,0:T(8,128)S(1)}, f32[8,128]{1,0:T(8,128)S(1)}, f32[8,128]{1,0:T(8,128)S(1)}, f32[512,128]{1,0:T(8,128)S(1)}, /*index=5*/f32[512,128]{1,0:T(8,128)S(1)}) custom-call(f32[4,40,128]{2,1,0:T(8,128)S(1)} %get-tuple-element.19.keep_ref, f32[4,8,128]{2,1,0:T(8,128)S(1)} %shard_map.124.base_ref, ...), custom_call_target="tpu_custom_call" | custom-call | tf_op jit(solution)/shard_map/pallas_call | solution.py:381
  18.5 0.1 collective-permute-start.5
  18.7 1.4 %collective-permute-start.6 = (f32[8,128]{1,0:T(8,128)S(1)}, f32[8,128]{1,0:T(8,128)S(1)}, u32[]{:S(2)}, u32[]{:S(2)}) collective-permute-start(f32[8,128]{1,0:T(8,128)S(1)} %get-tuple-element.33), channel_id=1, source_target_pairs={{0,1},{1,0},{2,3},{3,2},{4,8},{5,9},{6,10},{7,11},{8,4},{9,5},{10,... | collective-permute-start | bytes 12296 | tf_op jit(solution)/shard_map/ppermute | solution.py:401
  20.1 0.8 %shard_map.126.total_ref = f32[8,128]{1,0:T(8,128)S(1)} custom-call(f32[4,40,128]{2,1,0:T(8,128)S(1)} %get-tuple-element.19.keep_ref, f32[4,8,128]{2,1,0:T(8,128)S(1)} %get-tuple-element.28.next_ref, f32[8,128]{1,0:T(8,128)S(1)} %get-tuple-element.29.near_ref, f32[128,128]{1,0:T(8,128)S(1)} %get-tuple-element.25.coarse_ref, ...), custom_call_target="tpu_custom_call" | custom-call | tf_op jit(solution)/shard_map/pallas_call | solution.py:381
  20.9 0.0 collective-permute-done.5.pair_ref
  20.9 1.3 %collective-permute-done.6.other_ref = f32[8,128]{1,0:T(8,128)S(1)} collective-permute-done((f32[8,128]{1,0:T(8,128)S(1)}, f32[8,128]{1,0:T(8,128)S(1)}, u32[]{:S(2)}, u32[]{:S(2)}) %collective-permute-start.6) | collective-permute-done | bytes 4128 | tf_op jit(solution)/shard_map/ppermute | solution.py:401
  22.3 0.8 %shard_map.127 = (f32[3,128]{1,0:T(4,128)}, f32[3,128]{1,0:T(4,128)}) custom-call(f32[4,40,128]{2,1,0:T(8,128)S(1)} %get-tuple-element.19.keep_ref, f32[4,8,128]{2,1,0:T(8,128)S(1)} %get-tuple-element.28.next_ref, f32[8,128]{1,0:T(8,128)S(1)} %shard_map.126.total_ref, f32[8,128]{1,0:T(8,128)S(1)} %collective-permute-done.5.pair_ref, ...), custom_call_target="tpu_custom_call" | custom-call | tf_op jit(solution)/shard_map/pallas_call | solution.py:381
Async XLA Ops:
  1.9 6.6 %collective-permute-start = (f32[1,72,128]{2,1,0:T(8,128)S(1)}, f32[1,72,128]{2,1,0:T(8,128)S(1)}, u32[]{:S(2)}, u32[]{:S(2)}) collective-permute-start(f32[1,72,128]{2,1,0:T(8,128)S(1)} %bitcast.4), channel_id=1, source_target_pairs={{0,2},{1,3},{2,0},{3,1},{4,6},{5,7},{6,4},{7,5},{8,10},{9,11},{10,... | collective-permute-start | bytes 110600 | tf_op jit(solution)/shard_map/ppermute | solution.py:415
  6.1 4.3 %collective-permute-start.1 = (f32[1,72,128]{2,1,0:T(8,128)S(1)}, f32[1,72,128]{2,1,0:T(8,128)S(1)}, u32[]{:S(2)}, u32[]{:S(2)}) collective-permute-start(f32[1,72,128]{2,1,0:T(8,128)S(1)} %bitcast.5), channel_id=1, source_target_pairs={{0,1},{1,0},{2,3},{3,2},{4,5},{5,4},{6,7},{7,6},{8,9},{9,8},{10,11... | collective-permute-start | bytes 110600 | tf_op jit(solution)/shard_map/ppermute | solution.py:415
  8.5 4.0 %collective-permute-start.2 = (f32[1,72,128]{2,1,0:T(8,128)S(1)}, f32[1,72,128]{2,1,0:T(8,128)S(1)}, u32[]{:S(2)}, u32[]{:S(2)}) collective-permute-start(f32[1,72,128]{2,1,0:T(8,128)S(1)} %collective-permute-done.refs_1_), channel_id=1, source_target_pairs={{0,1},{1,0},{2,3},{3,2},{4,5},{5,4},{6,7},{7,6},{8,9},{9,8},{10,11... | collective-permute-start | bytes 110600 | tf_op jit(solution)/shard_map/ppermute | solution.py:415
  13.8 1.8 %collective-permute-start.3 = (f32[4,4,128]{2,1,0:T(4,128)S(1)}, f32[4,4,128]{2,1,0:T(4,128)S(1)}, u32[]{:S(2)}, u32[]{:S(2)}) collective-permute-start(f32[4,4,128]{2,1,0:T(4,128)S(1)} %get-tuple-element.21), channel_id=1, source_target_pairs={{0,4},{1,5},{2,6},{3,7},{4,0},{5,1},{6,2},{7,3},{8,12},{9,13},{10,... | collective-permute-start | bytes 24584 | tf_op jit(solution)/shard_map/ppermute | solution.py:401
  13.8 3.7 %collective-permute-start.4 = (f32[4,4,128]{2,1,0:T(4,128)S(1)}, f32[4,4,128]{2,1,0:T(4,128)S(1)}, u32[]{:S(2)}, u32[]{:S(2)}) collective-permute-start(f32[4,4,128]{2,1,0:T(4,128)S(1)} %get-tuple-element.22), channel_id=1, source_target_pairs={{0,1},{1,0},{2,3},{3,2},{4,8},{5,9},{6,10},{7,11},{8,4},{9,5},{10,... | collective-permute-start | bytes 24584 | tf_op jit(solution)/shard_map/ppermute | solution.py:401
  18.5 2.4 %collective-permute-start.5 = (f32[8,128]{1,0:T(8,128)S(1)}, f32[8,128]{1,0:T(8,128)S(1)}, u32[]{:S(2)}, u32[]{:S(2)}) collective-permute-start(f32[8,128]{1,0:T(8,128)S(1)} %get-tuple-element.32), channel_id=1, source_target_pairs={{0,4},{1,5},{2,6},{3,7},{4,0},{5,1},{6,2},{7,3},{8,12},{9,13},{10,... | collective-permute-start | bytes 12296 | tf_op jit(solution)/shard_map/ppermute | solution.py:401
  18.7 3.6 %collective-permute-start.6 = (f32[8,128]{1,0:T(8,128)S(1)}, f32[8,128]{1,0:T(8,128)S(1)}, u32[]{:S(2)}, u32[]{:S(2)}) collective-permute-start(f32[8,128]{1,0:T(8,128)S(1)} %get-tuple-element.33), channel_id=1, source_target_pairs={{0,1},{1,0},{2,3},{3,2},{4,8},{5,9},{6,10},{7,11},{8,4},{9,5},{10,... | collective-permute-start | bytes 12296 | tf_op jit(solution)/shard_map/ppermute | solution.py:401

commit v6 on v5

--- a/solution.py
+++ b/solution.py
@@ -153,7 +153,7 @@
 
 def pack_kernel(
     place_ref, speed_ref, rest_ref, mass_ref, connect_ref, modulus_ref, stiff_ref, lists_ref, patch_ref, owner_ref,
-    map_ref, out_ref, keep_ref, parts_ref,
+    map_ref, out_ref, mesh_ref, keep_ref, parts_ref,
 ):
     patches = patch_ref.shape[0]
     corners, elements = connect_ref.shape
@@ -169,14 +169,13 @@
     out_ref[ROW_OWNER : ROW_OWNER + 1, 0:patches] = owner_ref[...].astype(jnp.float32)
     out_ref[ROW_PATCH : ROW_PATCH + patches, :] = patch_ref[...].astype(jnp.float32)
     out_ref[ROW_PATCH + patches : ROW_PATCH + 2 * patches, :] = map_ref[...].astype(jnp.float32)
-    base = ROW_PATCH + 2 * patches
-    for k, run in enumerate(runs):
-        out_ref[base + k * corners : base + (k + 1) * corners, :] = connect[k]
-    last = base + len(runs) * corners
-    out_ref[last : last + TILE, :] = jnp.zeros((TILE, LANES), jnp.float32)
-    out_ref[last : last + 3, :] = rest_ref[...]
+    for k in range(len(runs)):
+        mesh_ref[k * corners : (k + 1) * corners, :] = connect[k]
+    last = len(runs) * corners
+    mesh_ref[last : last + TILE, :] = jnp.zeros((TILE, LANES), jnp.float32)
+    mesh_ref[last : last + 3, :] = rest_ref[...]
     for k, scale in enumerate(modulus):
-        out_ref[last + 4 + k : last + 5 + k, :] = scale
+        mesh_ref[last + 4 + k : last + 5 + k, :] = scale
     out_ref[ROW_ELASTIC : ROW_ELASTIC + TILE, :] = scatter(entries)
     out_ref[ROW_LISTS : ROW_LISTS + 4, :] = lists_ref[...].astype(jnp.float32)
 
@@ -236,8 +235,7 @@
     nodes = jnp.concatenate([ref[ROW_PATCH : ROW_PATCH + patches, :] for ref in record], axis=0)
     pairs = jnp.concatenate([ref[ROW_PATCH + patches : ROW_PATCH + 2 * patches, :] for ref in record], axis=0)
     for s, ref in enumerate(record):
-        keep_ref[s, 0:ROW_PATCH, :] = ref[0:ROW_PATCH, :]
-        keep_ref[s, ROW_PATCH:, :] = ref[ROW_PATCH + 2 * patches :, :]
+        keep_ref[s] = ref[0:ROW_PATCH, :]
     lane = lax.broadcasted_iota(jnp.int32, (patches, LANES), 1)
     line = lax.broadcasted_iota(jnp.int32, (patches, LANES), 0)
     owner_col = jnp.concatenate(
@@ -314,17 +312,16 @@
     return faces([pair, jnp.where(inside("mx"), other, 0.0)], [near, far])
 
 
-def elements_of(keep_ref, next_ref, s, corners):
-    last = keep_ref.shape[1] - TILE
-    runs = (last - ROW_PATCH) // corners
-    connect = [keep_ref[s, ROW_PATCH + k * corners : ROW_PATCH + (k + 1) * corners, :] for k in range(runs)]
-    tail = keep_ref[s, last : last + TILE, :]
-    return next_ref[s][0:3], tail[0:3], connect, [tail[4 + k : 5 + k] for k in range(runs)]
+def elements_of(mesh, state, corners):
+    last = mesh.shape[0] - TILE
+    runs = last // corners
+    connect = [mesh[k * corners : (k + 1) * corners] for k in range(runs)]
+    return state[0:3], mesh[last : last + 3], connect, [mesh[last + 4 + k : last + 5 + k] for k in range(runs)]
 
 
 def step_kernel(
     width, patches, corners, keep_ref, base_ref, pair_ref, other_ref, idx_ref, link_ref, coarse_ref, fine_ref, stiff_ref,
-    next_ref, near_ref, send_ref, far_ref, parts_ref, back_ref, element_ref,
+    mesh_ref, next_ref, near_ref, send_ref, far_ref, parts_ref, back_ref, element_ref,
 ):
     side = lax.rem(lax.axis_index("mx"), 2)
     count = width * patches
@@ -339,7 +336,7 @@
         next_ref[s, 4:7, :] = speed
 
     each_unit(width, unit)
-    (elastic,) = elastic_entries([elements_of(keep_ref, next_ref, 0, corners)], stiff_ref[...], element_ref)
+    (elastic,) = elastic_entries([elements_of(mesh_ref[...], next_ref[0], corners)], stiff_ref[...], element_ref)
     state = [next_ref[s] for s in range(width)]
     indices = [idx_ref[g * count : (g + 1) * count, :] for g in range(3)]
     put_contact(width, patches, state, indices, link_ref[...].astype(jnp.bfloat16), parts_ref, back_ref)
@@ -353,11 +350,18 @@
 
 def spare_kernel(
     width, patches, corners, keep_ref, next_ref, near_ref, coarse_ref, fine_ref, parts_ref, back_ref, stiff_ref,
-    total_ref, element_ref,
+    pair_ref, other_ref, total_ref, element_ref,
 ):
     me = lax.axis_index("my")
     around = [jnp.maximum(me - 1, 0) ^ me, jnp.minimum(me + 1, width - 1) ^ me]
-    elastic = elastic_entries([elements_of(keep_ref, next_ref, s, corners) for s in around], stiff_ref[...], element_ref)
+    even = lax.rem(me, 2) == 0
+    pair, other = pair_ref[...], other_ref[...]
+    meshes = [jnp.where(even, other, pair), jnp.where(even, pair, other)]
+    there = [me > 0, me < width - 1]
+    units = [
+        elements_of(jnp.where(exists, mesh, 0.0), next_ref[s], corners) for exists, mesh, s in zip(there, meshes, around)
+    ]
+    elastic = elastic_entries(units, stiff_ref[...], element_ref)
     below, above = [
         scatter(entries + contact_entries(width, patches, s, coarse_ref, fine_ref, parts_ref, back_ref), 1)
         for s, entries in zip(around, elastic)
@@ -365,7 +369,7 @@
     low = face_values(below, keep_ref[around[0], ROW_LISTS + 3 : ROW_LISTS + 4, :])
     high = face_values(above, keep_ref[around[1], ROW_LISTS + 2 : ROW_LISTS + 3, :])
     lists = keep_ref[0, ROW_LISTS : ROW_LISTS + 4, :]
-    tiles = [jnp.where(me > 0, low, 0.0), jnp.where(me < width - 1, high, 0.0)]
+    tiles = [jnp.where(exists, face, 0.0) for exists, face in zip(there, (low, high))]
     total_ref[...] = near_ref[...] + faces(tiles, [lists[2:3], lists[3:4]])
 
 
@@ -390,15 +394,17 @@
 
 def swap(value, axis, first, other):
     size, depth = lax.axis_size(axis), lax.axis_size(other)
+    axes = ("mx", "my")
+    place = (lambda i, k: i * depth + k) if axis == axes[0] else (lambda i, k: k * size + i)
     pairs = []
     for i in range(size):
         partner = i + 1 - 2 * ((i - first) % 2)
         for k in range(depth):
             if 0 <= partner < size:
-                pairs.append((i * depth + k, partner * depth + k))
+                pairs.append((place(i, k), place(partner, k)))
             elif depth % 2 == 0:
-                pairs.append((i * depth + k, i * depth + (k ^ 1)))
-    return lax.ppermute(value, (axis, other), pairs)
+                pairs.append((place(i, k), place(i, k ^ 1)))
+    return lax.ppermute(value, axes, pairs)
 
 
 def both(pair, other):
@@ -441,15 +447,17 @@
     element_parts = (TILE * corners * runs, LANES)
     tile = (TILE, LANES)
     parts = (TILE * count, LANES)
-    record, stiff = call(
+    record, mesh, stiff = call(
         pack_kernel,
-        [(ROW_PATCH + 2 * patches + runs * corners + TILE, LANES), stiffness.shape],
+        [(ROW_PATCH + 2 * patches, LANES), (runs * corners + TILE, LANES), stiffness.shape],
         [element_parts],
         positions, velocities, rest_positions, mass, element_nodes, modulus, stiffness, shared_lists, patch_nodes,
         patch_owner[None], pair_map, placed=False,
     )
     pieces, where = gather_row(record, "my")
-    kept = (width, record.shape[0] - 2 * patches, LANES)
+    kept = (width, ROW_PATCH, LANES)
+    mesh_pair = swap(mesh, "my", 0, "mx")
+    mesh_other = swap(mesh, "my", 1, "mx")
     total, pair, other, keep, indices, link, *spots = call(
         functools.partial(row_kernel, width, patches, where),
         [(width, TILE, LANES), (width, 4, LANES), (width, 4, LANES), kept, (3 * count, LANES), (count, count)]
@@ -463,14 +471,14 @@
     contact = functools.partial(step_kernel, width, patches, corners)
     outs = [states, tile, tile, tile, parts, parts]
     state, near, pair, other, *forces = call(
-        contact, outs, [element_parts], keep, base, pair, other, indices, link, *spots, stiff
+        contact, outs, [element_parts], keep, base, pair, other, indices, link, *spots, stiff, mesh
     )
     pair, other = both(pair, other)
     (total,) = call(
         functools.partial(spare_kernel, width, patches, corners),
         [tile],
         [(2 * element_parts[0], LANES)],
-        keep, state, near, *spots, *forces, stiff,
+        keep, state, near, *spots, *forces, stiff, mesh_pair, mesh_other,
     )
     outs = [(3, LANES), (3, LANES)]
     return tuple(call(end_kernel, outs, [], keep, state, total, pair, other, result=jax.ShapeDtypeStruct))

time: 23.2 us -> 23.3 us (level)
  starting transfers between devices: 10.2 us -> 13.9 us
  waiting for transfers between devices: 6.67 us -> 3.01 us
    ppermute x4 -> x6, starting transfers between devices: 3.04 us -> 6.26 us  [swap(): return lax.ppermute(value, axes, pairs)]
    ppermute x4 -> x6, waiting for transfers between devices: 3.27 us -> 0.84 us  [swap(): return lax.ppermute(value, axes, pairs)]
    ppermute x3, waiting for transfers between devices: 3.41 us -> 2.17 us  [exchange(): return lax.ppermute(value, axis, [(i, i ^ step) for i in range(size)])]
    ppermute x3, starting transfers between devices: 7.12 us -> 7.6 us  [exchange(): return lax.ppermute(value, axis, [(i, i ^ step) for i in range(size)])]
  transfers between devices with their start and end apart: 7 -> 9, of which waited for: 5 -> 5; matrix products, arithmetic and copies ran while one was open for 0% -> 0% of each run, Pallas kernels for 5% -> 9%
where the time goes in v6:
time: 23.3 us; the launch traced here: 23.1 us
  starting transfers between devices  13.9 us (60%)
  Pallas kernels  5.54 us (24%)
  waiting for transfers between devices  3.01 us (13%)
  between operations  0.7 us (3%)
    ppermute x3, starting transfers between devices, exchange(): return lax.ppermute(value, axis, [(i, i ^ step) for i in range(size)])  7.6 us
    ppermute x6, starting transfers between devices, swap(): return lax.ppermute(value, axes, pairs)  6.26 us
    pallas_call x6, Pallas kernels, call(): pl.pallas_call(kernel, out_shape=[result(shape, jnp.float32) for shape in...  5.54 us
    ppermute x3, waiting for transfers between devices, exchange(): return lax.ppermute(value, axis, [(i, i ^ step) for i in range(size)])  2.17 us
    ppermute x6, waiting for transfers between devices, swap(): return lax.ppermute(value, axes, pairs)  0.84 us
  transfers between devices with their start and end apart: 9, of which 5 were waited for; matrix products, arithmetic and copies ran while one was open for 0% of the time, Pallas kernels for 9%

profile of v6, /device:TPU:0, one launch (start us, length us, event | category | flops | bytes accessed | tf_op | source)
XLA Modules:
  0.0 23.1 jit_solution(5571154534828188851)
XLA Ops:
  0.6 1.3 %shard_map.122 = (f32[48,128]{1,0:T(8,128)S(1)}, f32[24,128]{1,0:T(8,128)S(1)}, f32[24,24]{1,0:T(8,128)S(1)}) custom-call(f32[3,128]{1,0:T(4,128)} %place_ref.1, f32[3,128]{1,0:T(4,128)} %speed_ref.1, f32[3,128]{1,0:T(4,128)} %rest_ref.1, f32[1,128]{1,0:T(1,128)} %bitcast.8, s32[8,256]{1,0:T(8,128)} %connect_ref.1, f32[1,256]{1,0:T(1,128)} %bitcast.7, ...), custom_call_target="tpu_custom_call" | custom-call | tf_op jit(solution)/shard_map/pallas_call | solution.py:385
  1.9 4.1 %collective-permute-start = (f32[1,48,128]{2,1,0:T(8,128)S(1)}, f32[1,48,128]{2,1,0:T(8,128)S(1)}, u32[]{:S(2)}, u32[]{:S(2)}) collective-permute-start(f32[1,48,128]{2,1,0:T(8,128)S(1)} %bitcast.4), channel_id=1, source_target_pairs={{0,2},{1,3},{2,0},{3,1},{4,6},{5,7},{6,4},{7,5},{8,10},{9,11},{10,... | collective-permute-start | bytes 73736 | tf_op jit(solution)/shard_map/ppermute | solution.py:421
  6.1 1.6 %collective-permute-start.1 = (f32[1,48,128]{2,1,0:T(8,128)S(1)}, f32[1,48,128]{2,1,0:T(8,128)S(1)}, u32[]{:S(2)}, u32[]{:S(2)}) collective-permute-start(f32[1,48,128]{2,1,0:T(8,128)S(1)} %bitcast.5), channel_id=1, source_target_pairs={{0,1},{1,0},{2,3},{3,2},{4,5},{5,4},{6,7},{7,6},{8,9},{9,8},{10,11... | collective-permute-start | bytes 73736 | tf_op jit(solution)/shard_map/ppermute | solution.py:421
  7.7 0.2 %collective-permute-done.refs_1_ = f32[1,48,128]{2,1,0:T(8,128)S(1)} collective-permute-done((f32[1,48,128]{2,1,0:T(8,128)S(1)}, f32[1,48,128]{2,1,0:T(8,128)S(1)}, u32[]{:S(2)}, u32[]{:S(2)}) %collective-permute-start) | collective-permute-done | bytes 24608 | tf_op jit(solution)/shard_map/ppermute | solution.py:421
  7.9 1.9 %collective-permute-start.2 = (f32[1,48,128]{2,1,0:T(8,128)S(1)}, f32[1,48,128]{2,1,0:T(8,128)S(1)}, u32[]{:S(2)}, u32[]{:S(2)}) collective-permute-start(f32[1,48,128]{2,1,0:T(8,128)S(1)} %collective-permute-done.refs_1_), channel_id=1, source_target_pairs={{0,1},{1,0},{2,3},{3,2},{4,5},{5,4},{6,7},{7,6},{8,9},{9,8},{10,11... | collective-permute-start | bytes 73736 | tf_op jit(solution)/shard_map/ppermute | solution.py:421
  9.8 0.3 %collective-permute-done.1.refs_2_ = f32[1,48,128]{2,1,0:T(8,128)S(1)} collective-permute-done((f32[1,48,128]{2,1,0:T(8,128)S(1)}, f32[1,48,128]{2,1,0:T(8,128)S(1)}, u32[]{:S(2)}, u32[]{:S(2)}) %collective-permute-start.1) | collective-permute-done | bytes 24608 | tf_op jit(solution)/shard_map/ppermute | solution.py:421
  10.1 1.7 %collective-permute-done.2.refs_3_ = f32[1,48,128]{2,1,0:T(8,128)S(1)} collective-permute-done((f32[1,48,128]{2,1,0:T(8,128)S(1)}, f32[1,48,128]{2,1,0:T(8,128)S(1)}, u32[]{:S(2)}, u32[]{:S(2)}) %collective-permute-start.2) | collective-permute-done | bytes 24608 | tf_op jit(solution)/shard_map/ppermute | solution.py:421
  11.7 1.3 %shard_map.123 = (f32[4,8,128]{2,1,0:T(8,128)S(1)}, f32[4,4,128]{2,1,0:T(4,128)S(1)}, f32[4,4,128]{2,1,0:T(4,128)S(1)}, f32[4,16,128]{2,1,0:T(8,128)S(1)}, f32[1...) custom-call(f32[1,48,128]{2,1,0:T(8,128)S(1)} %bitcast.6, ...), custom_call_target="tpu_custom_call" | custom-call | tf_op jit(solution)/shard_map/pallas_call | solution.py:385
  13.0 0.0 collective-permute-start.3
  13.0 2.0 %collective-permute-start.4 = (f32[4,4,128]{2,1,0:T(4,128)S(1)}, f32[4,4,128]{2,1,0:T(4,128)S(1)}, u32[]{:S(2)}, u32[]{:S(2)}) collective-permute-start(f32[4,4,128]{2,1,0:T(4,128)S(1)} %get-tuple-element.23), channel_id=1, source_target_pairs={{0,1},{1,0},{2,3},{3,2},{4,8},{5,9},{6,10},{7,11},{8,4},{9,5},{10,... | collective-permute-start | bytes 24584 | tf_op jit(solution)/shard_map/ppermute | solution.py:407
  15.0 0.1 collective-permute-start.5
  15.1 1.2 %collective-permute-start.6 = (f32[24,128]{1,0:T(8,128)S(1)}, f32[24,128]{1,0:T(8,128)S(1)}, u32[]{:S(2)}, u32[]{:S(2)}) collective-permute-start(f32[24,128]{1,0:T(8,128)S(1)} %get-tuple-element.29.mesh_ref), channel_id=1, source_target_pairs={{0,4},{4,0},{8,12},{12,8},{16,20},{20,16},{24,28},{28,24},{1,2},{5... | collective-permute-start | bytes 36872 | tf_op jit(solution)/shard_map/ppermute | solution.py:407
  16.3 0.3 %shard_map.124.base_ref = f32[4,8,128]{2,1,0:T(8,128)S(1)} custom-call(f32[4,16,128]{2,1,0:T(8,128)S(1)} %get-tuple-element.20.keep_ref, f32[4,8,128]{2,1,0:T(8,128)S(1)} %get-tuple-element.21.total_ref), custom_call_target="tpu_custom_call" | custom-call | tf_op jit(solution)/shard_map/pallas_call | solution.py:385
  16.6 0.0 collective-permute-done.3.pair_ref
  16.6 0.1 collective-permute-done.4.other_ref
  16.8 1.0 %shard_map.125 = (f32[4,8,128]{2,1,0:T(8,128)S(1)}, f32[8,128]{1,0:T(8,128)S(1)}, f32[8,128]{1,0:T(8,128)S(1)}, f32[8,128]{1,0:T(8,128)S(1)}, f32[512,128]{1,0:T(8,128)S(1)}, /*index=5*/f32[512,128]{1,0:T(8,128)S(1)}) custom-call(f32[4,16,128]{2,1,0:T(8,128)S(1)} %get-tuple-element.20.keep_ref, f32[4,8,128]{2,1,0:T(8,128)S(1)} %shard_map.124.base_ref, ...), custom_call_target="tpu_custom_call" | custom-call | tf_op jit(solution)/shard_map/pallas_call | solution.py:385
  17.8 0.1 collective-permute-start.7
  17.9 2.8 %collective-permute-start.8 = (f32[8,128]{1,0:T(8,128)S(1)}, f32[8,128]{1,0:T(8,128)S(1)}, u32[]{:S(2)}, u32[]{:S(2)}) collective-permute-start(f32[8,128]{1,0:T(8,128)S(1)} %get-tuple-element.35), channel_id=1, source_target_pairs={{0,1},{1,0},{2,3},{3,2},{4,8},{5,9},{6,10},{7,11},{8,4},{9,5},{10,... | collective-permute-start | bytes 12296 | tf_op jit(solution)/shard_map/ppermute | solution.py:407
  20.7 0.0 collective-permute-done.5.pair_ref
  20.7 0.0 collective-permute-done.6.other_ref
  20.7 0.8 %shard_map.126.total_ref = f32[8,128]{1,0:T(8,128)S(1)} custom-call(f32[4,16,128]{2,1,0:T(8,128)S(1)} %get-tuple-element.20.keep_ref, f32[4,8,128]{2,1,0:T(8,128)S(1)} %get-tuple-element.30.next_ref, f32[8,128]{1,0:T(8,128)S(1)} %get-tuple-element.31.near_ref, f32[128,128]{1,0:T(8,128)S(1)} %get-tuple-element.26.coarse_ref, ...), custom_call_target="tpu_custom_call" | custom-call | tf_op jit(solution)/shard_map/pallas_call | solution.py:385
  21.6 0.0 collective-permute-done.7.pair_ref
  21.6 0.7 %collective-permute-done.8.other_ref = f32[8,128]{1,0:T(8,128)S(1)} collective-permute-done((f32[8,128]{1,0:T(8,128)S(1)}, f32[8,128]{1,0:T(8,128)S(1)}, u32[]{:S(2)}, u32[]{:S(2)}) %collective-permute-start.8) | collective-permute-done | bytes 4128 | tf_op jit(solution)/shard_map/ppermute | solution.py:407
  22.3 0.8 %shard_map.127 = (f32[3,128]{1,0:T(4,128)}, f32[3,128]{1,0:T(4,128)}) custom-call(f32[4,16,128]{2,1,0:T(8,128)S(1)} %get-tuple-element.20.keep_ref, f32[4,8,128]{2,1,0:T(8,128)S(1)} %get-tuple-element.30.next_ref, f32[8,128]{1,0:T(8,128)S(1)} %shard_map.126.total_ref, f32[8,128]{1,0:T(8,128)S(1)} %collective-permute-done.7.pair_ref, ...), custom_call_target="tpu_custom_call" | custom-call | tf_op jit(solution)/shard_map/pallas_call | solution.py:385
Async XLA Ops:
  1.9 5.9 %collective-permute-start = (f32[1,48,128]{2,1,0:T(8,128)S(1)}, f32[1,48,128]{2,1,0:T(8,128)S(1)}, u32[]{:S(2)}, u32[]{:S(2)}) collective-permute-start(f32[1,48,128]{2,1,0:T(8,128)S(1)} %bitcast.4), channel_id=1, source_target_pairs={{0,2},{1,3},{2,0},{3,1},{4,6},{5,7},{6,4},{7,5},{8,10},{9,11},{10,... | collective-permute-start | bytes 73736 | tf_op jit(solution)/shard_map/ppermute | solution.py:421
  6.1 4.0 %collective-permute-start.1 = (f32[1,48,128]{2,1,0:T(8,128)S(1)}, f32[1,48,128]{2,1,0:T(8,128)S(1)}, u32[]{:S(2)}, u32[]{:S(2)}) collective-permute-start(f32[1,48,128]{2,1,0:T(8,128)S(1)} %bitcast.5), channel_id=1, source_target_pairs={{0,1},{1,0},{2,3},{3,2},{4,5},{5,4},{6,7},{7,6},{8,9},{9,8},{10,11... | collective-permute-start | bytes 73736 | tf_op jit(solution)/shard_map/ppermute | solution.py:421
  7.9 3.8 %collective-permute-start.2 = (f32[1,48,128]{2,1,0:T(8,128)S(1)}, f32[1,48,128]{2,1,0:T(8,128)S(1)}, u32[]{:S(2)}, u32[]{:S(2)}) collective-permute-start(f32[1,48,128]{2,1,0:T(8,128)S(1)} %collective-permute-done.refs_1_), channel_id=1, source_target_pairs={{0,1},{1,0},{2,3},{3,2},{4,5},{5,4},{6,7},{7,6},{8,9},{9,8},{10,11... | collective-permute-start | bytes 73736 | tf_op jit(solution)/shard_map/ppermute | solution.py:421
  13.0 3.6 %collective-permute-start.3 = (f32[4,4,128]{2,1,0:T(4,128)S(1)}, f32[4,4,128]{2,1,0:T(4,128)S(1)}, u32[]{:S(2)}, u32[]{:S(2)}) collective-permute-start(f32[4,4,128]{2,1,0:T(4,128)S(1)} %get-tuple-element.22), channel_id=1, source_target_pairs={{0,4},{1,5},{2,6},{3,7},{4,0},{5,1},{6,2},{7,3},{8,12},{9,13},{10,... | collective-permute-start | bytes 24584 | tf_op jit(solution)/shard_map/ppermute | solution.py:407
  13.0 3.7 %collective-permute-start.4 = (f32[4,4,128]{2,1,0:T(4,128)S(1)}, f32[4,4,128]{2,1,0:T(4,128)S(1)}, u32[]{:S(2)}, u32[]{:S(2)}) collective-permute-start(f32[4,4,128]{2,1,0:T(4,128)S(1)} %get-tuple-element.23), channel_id=1, source_target_pairs={{0,1},{1,0},{2,3},{3,2},{4,8},{5,9},{6,10},{7,11},{8,4},{9,5},{10,... | collective-permute-start | bytes 24584 | tf_op jit(solution)/shard_map/ppermute | solution.py:407
  15.0 5.7 %collective-permute-start.5 = (f32[24,128]{1,0:T(8,128)S(1)}, f32[24,128]{1,0:T(8,128)S(1)}, u32[]{:S(2)}, u32[]{:S(2)}) collective-permute-start(f32[24,128]{1,0:T(8,128)S(1)} %get-tuple-element.29.mesh_ref), channel_id=1, source_target_pairs={{0,1},{4,5},{8,9},{12,13},{16,17},{20,21},{24,25},{28,29},{1,0},{5... | collective-permute-start | bytes 36872 | tf_op jit(solution)/shard_map/ppermute | solution.py:407
  15.1 5.6 %collective-permute-start.6 = (f32[24,128]{1,0:T(8,128)S(1)}, f32[24,128]{1,0:T(8,128)S(1)}, u32[]{:S(2)}, u32[]{:S(2)}) collective-permute-start(f32[24,128]{1,0:T(8,128)S(1)} %get-tuple-element.29.mesh_ref), channel_id=1, source_target_pairs={{0,4},{4,0},{8,12},{12,8},{16,20},{20,16},{24,28},{28,24},{1,2},{5... | collective-permute-start | bytes 36872 | tf_op jit(solution)/shard_map/ppermute | solution.py:407
  17.8 3.8 %collective-permute-start.7 = (f32[8,128]{1,0:T(8,128)S(1)}, f32[8,128]{1,0:T(8,128)S(1)}, u32[]{:S(2)}, u32[]{:S(2)}) collective-permute-start(f32[8,128]{1,0:T(8,128)S(1)} %get-tuple-element.34), channel_id=1, source_target_pairs={{0,4},{1,5},{2,6},{3,7},{4,0},{5,1},{6,2},{7,3},{8,12},{9,13},{10,... | collective-permute-start | bytes 12296 | tf_op jit(solution)/shard_map/ppermute | solution.py:407
  17.9 4.4 %collective-permute-start.8 = (f32[8,128]{1,0:T(8,128)S(1)}, f32[8,128]{1,0:T(8,128)S(1)}, u32[]{:S(2)}, u32[]{:S(2)}) collective-permute-start(f32[8,128]{1,0:T(8,128)S(1)} %get-tuple-element.35), channel_id=1, source_target_pairs={{0,1},{1,0},{2,3},{3,2},{4,8},{5,9},{6,10},{7,11},{8,4},{9,5},{10,... | collective-permute-start | bytes 12296 | tf_op jit(solution)/shard_map/ppermute | solution.py:407

commit v7 on v6

--- a/solution.py
+++ b/solution.py
@@ -204,12 +204,11 @@
                 back_ref[at : at + TILE, :] = routed[b * TILE : (b + 1) * TILE]
 
 
-def contact_entries(width, patches, u, coarse_ref, fine_ref, parts_ref, back_ref):
+def contact_entries(patches, u, base, coarse_ref, fine_ref, parts_ref):
     entries = []
-    for base, ref in ((0, parts_ref), (width * patches, back_ref)):
-        for s in range(patches):
-            at = u * patches + s
-            entries.append((coarse_ref[pl.ds(base + at, 1), :], fine_ref[pl.ds(base + at, 1), :], get_parts(ref, at)))
+    for s in range(patches):
+        at = u * patches + s
+        entries.append((coarse_ref[pl.ds(base + at, 1), :], fine_ref[pl.ds(base + at, 1), :], get_parts(parts_ref, at)))
     return joined(entries)
 
 
@@ -267,14 +266,19 @@
     fine_ref[...] = fine
     put_contact(width, patches, state, (nodes, target, device), back, parts_ref, back_ref)
 
+    def direct(u):
+        info = keep_ref[u, ROW_ELASTIC : ROW_ELASTIC + TILE, :]
+        total_ref[u] = scatter(contact_entries(patches, u, 0, coarse_ref, fine_ref, parts_ref), 1) + info
+
     def unit(u):
         info = keep_ref[u, ROW_ELASTIC : ROW_ELASTIC + TILE, :]
-        total = scatter(contact_entries(width, patches, u, coarse_ref, fine_ref, parts_ref, back_ref), 1) + info
+        total = total_ref[u] + scatter(contact_entries(patches, u, count, coarse_ref, fine_ref, back_ref), 1)
         total_ref[u] = total
         low, high = face_values(total, info[4:5]), face_values(total, info[5:6])
         pair_ref[u] = jnp.where(side == 0, high, low)[0:4]
         other_ref[u] = jnp.where(side == 0, low, high)[0:4]
 
+    each_unit(width, direct)
     each_unit(width, unit)
 
 
@@ -288,8 +292,22 @@
     return jnp.logical_and(partner >= 0, partner < size)
 
 
-def mid_kernel(width, keep_ref, total_ref, base_ref):
+def mid_kernel(width, patches, keep_ref, total_ref, idx_ref, link_ref, base_ref, table_ref):
     me = lax.axis_index("my")
+    count = width * patches
+    back = link_ref[0:patches, :].astype(jnp.bfloat16)
+    nodes, target, device = [idx_ref[g * count : (g + 1) * count, :] for g in range(3)]
+    slot = (lax.broadcasted_iota(jnp.int32, (count, LANES), 0) // patches).astype(jnp.float32)
+    table = [
+        nodes[0:patches],
+        route(back, target),
+        target[0:patches],
+        route(back, nodes),
+        device[0:patches],
+        route(back, slot),
+    ]
+    for g, rows in enumerate(table):
+        table_ref[g * patches : (g + 1) * patches, :] = rows
 
     def unit(s):
         info = keep_ref[s, 0 : 2 * TILE, :]
@@ -320,11 +338,10 @@
 
 
 def step_kernel(
-    width, patches, corners, keep_ref, base_ref, pair_ref, other_ref, idx_ref, link_ref, coarse_ref, fine_ref, stiff_ref,
-    mesh_ref, next_ref, near_ref, send_ref, far_ref, parts_ref, back_ref, element_ref,
+    width, patches, corners, keep_ref, base_ref, pair_ref, other_ref, table_ref, stiff_ref, mesh_ref,
+    next_ref, near_ref, send_ref, far_ref, parts_ref, element_ref,
 ):
     side = lax.rem(lax.axis_index("mx"), 2)
-    count = width * patches
     blank = jnp.zeros((4, LANES), jnp.float32)
 
     def unit(s):
@@ -337,10 +354,19 @@
 
     each_unit(width, unit)
     (elastic,) = elastic_entries([elements_of(mesh_ref[...], next_ref[0], corners)], stiff_ref[...], element_ref)
-    state = [next_ref[s] for s in range(width)]
-    indices = [idx_ref[g * count : (g + 1) * count, :] for g in range(3)]
-    put_contact(width, patches, state, indices, link_ref[...].astype(jnp.bfloat16), parts_ref, back_ref)
-    total = scatter(elastic + contact_entries(width, patches, 0, coarse_ref, fine_ref, parts_ref, back_ref))
+    table = [table_ref[g * patches : (g + 1) * patches, :] for g in range(6)]
+    nodes, landing, target, from_nodes, to_slot, from_slot = [rows.astype(jnp.int32) for rows in table]
+    first, second = [], []
+    for c in (0, 1, 2, 4, 5, 6):
+        rows = [next_ref[s, c : c + 1, :] for s in range(width)]
+        home = jnp.broadcast_to(rows[0], (patches, LANES))
+        first.append(jnp.concatenate([pick(home, nodes), pick(choose(rows, from_slot), from_nodes)], axis=0))
+        second.append(jnp.concatenate([pick(choose(rows, to_slot), target), pick(home, landing)], axis=0))
+    sign = jnp.where(lax.broadcasted_iota(jnp.int32, (2 * patches, LANES), 0) < patches, 1.0, -1.0)
+    put_parts(parts_ref, [sign * force for force in pair_forces(first, second)])
+    coarse, fine = parted(table_ref[0 : 2 * patches, :])
+    contact = [(coarse[k : k + 1], fine[k : k + 1], get_parts(parts_ref, k)) for k in range(2 * patches)]
+    total = scatter(elastic + joined(contact))
     near_ref[...] = total
     lists = keep_ref[0, ROW_LISTS : ROW_LISTS + 4, :]
     low, high = face_values(total, lists[0:1]), face_values(total, lists[1:2])
@@ -349,10 +375,14 @@
 
 
 def spare_kernel(
-    width, patches, corners, keep_ref, next_ref, near_ref, coarse_ref, fine_ref, parts_ref, back_ref, stiff_ref,
-    pair_ref, other_ref, total_ref, element_ref,
+    width, patches, corners, keep_ref, next_ref, near_ref, idx_ref, link_ref, coarse_ref, fine_ref, stiff_ref,
+    pair_ref, other_ref, total_ref, parts_ref, back_ref, element_ref,
 ):
     me = lax.axis_index("my")
+    count = width * patches
+    state = [next_ref[s] for s in range(width)]
+    indices = [idx_ref[g * count : (g + 1) * count, :] for g in range(3)]
+    put_contact(width, patches, state, indices, link_ref[...].astype(jnp.bfloat16), parts_ref, back_ref)
     around = [jnp.maximum(me - 1, 0) ^ me, jnp.minimum(me + 1, width - 1) ^ me]
     even = lax.rem(me, 2) == 0
     pair, other = pair_ref[...], other_ref[...]
@@ -363,7 +393,12 @@
     ]
     elastic = elastic_entries(units, stiff_ref[...], element_ref)
     below, above = [
-        scatter(entries + contact_entries(width, patches, s, coarse_ref, fine_ref, parts_ref, back_ref), 1)
+        scatter(
+            entries
+            + contact_entries(patches, s, 0, coarse_ref, fine_ref, parts_ref)
+            + contact_entries(patches, s, count, coarse_ref, fine_ref, back_ref),
+            1,
+        )
         for s, entries in zip(around, elastic)
     ]
     low = face_values(below, keep_ref[around[0], ROW_LISTS + 3 : ROW_LISTS + 4, :])
@@ -467,18 +502,25 @@
     )
     states = (width, TILE, LANES)
     pair, other = both(pair, other)
-    (base,) = call(functools.partial(mid_kernel, width), [states], [], keep, total)
+    base, table = call(
+        functools.partial(mid_kernel, width, patches),
+        [states, (6 * patches, LANES)],
+        [],
+        keep, total, indices, link,
+    )
     contact = functools.partial(step_kernel, width, patches, corners)
-    outs = [states, tile, tile, tile, parts, parts]
-    state, near, pair, other, *forces = call(
-        contact, outs, [element_parts], keep, base, pair, other, indices, link, *spots, stiff, mesh
+    state, near, pair, other = call(
+        contact,
+        [states, tile, tile, tile],
+        [(TILE * 2 * patches, LANES), element_parts],
+        keep, base, pair, other, table, stiff, mesh,
     )
     pair, other = both(pair, other)
     (total,) = call(
         functools.partial(spare_kernel, width, patches, corners),
         [tile],
-        [(2 * element_parts[0], LANES)],
-        keep, state, near, *spots, *forces, stiff, mesh_pair, mesh_other,
+        [parts, parts, (2 * element_parts[0], LANES)],
+        keep, state, near, indices, link, *spots, stiff, mesh_pair, mesh_other,
     )
     outs = [(3, LANES), (3, LANES)]
     return tuple(call(end_kernel, outs, [], keep, state, total, pair, other, result=jax.ShapeDtypeStruct))

time: 23.3 us -> 22.5 us (0.966)
  the two profiles are of different devices: /device:TPU:0 before, /device:TPU:3 now
where the time goes in v7:
time: 22.5 us; the launch traced here: 22.3 us
  starting transfers between devices  10.2 us (45%)
  waiting for transfers between devices  5.74 us (26%)
  Pallas kernels  5.61 us (25%)
  between operations  0.7 us (3%)
    pallas_call x6, Pallas kernels, call(): pl.pallas_call(kernel, out_shape=[result(shape, jnp.float32) for shape in...  5.61 us
    ppermute x6, starting transfers between devices, swap(): return lax.ppermute(value, axes, pairs)  5.28 us
    ppermute x3, starting transfers between devices, exchange(): return lax.ppermute(value, axis, [(i, i ^ step) for i in range(size)])  4.95 us
    ppermute x6, waiting for transfers between devices, swap(): return lax.ppermute(value, axes, pairs)  4.09 us
    ppermute x3, waiting for transfers between devices, exchange(): return lax.ppermute(value, axis, [(i, i ^ step) for i in range(size)])  1.66 us
  transfers between devices with their start and end apart: 9, of which 4 were waited for; matrix products, arithmetic and copies ran while one was open for 0% of the time, Pallas kernels for 16%

profile of v7, /device:TPU:3, one launch (start us, length us, event | category | flops | bytes accessed | tf_op | source)
XLA Modules:
  0.0 22.3 jit_solution(3874037544738434125)
XLA Ops:
  0.6 1.3 %shard_map.122 = (f32[48,128]{1,0:T(8,128)S(1)}, f32[24,128]{1,0:T(8,128)S(1)}, f32[24,24]{1,0:T(8,128)S(1)}) custom-call(f32[3,128]{1,0:T(4,128)} %place_ref.1, f32[3,128]{1,0:T(4,128)} %speed_ref.1, f32[3,128]{1,0:T(4,128)} %rest_ref.1, f32[1,128]{1,0:T(1,128)} %bitcast.8, s32[8,256]{1,0:T(8,128)} %connect_ref.1, f32[1,256]{1,0:T(1,128)} %bitcast.7, ...), custom_call_target="tpu_custom_call" | custom-call | tf_op jit(solution)/shard_map/pallas_call | solution.py:420
  1.9 2.4 %collective-permute-start = (f32[1,48,128]{2,1,0:T(8,128)S(1)}, f32[1,48,128]{2,1,0:T(8,128)S(1)}, u32[]{:S(2)}, u32[]{:S(2)}) collective-permute-start(f32[1,48,128]{2,1,0:T(8,128)S(1)} %bitcast.4), channel_id=1, source_target_pairs={{0,2},{1,3},{2,0},{3,1},{4,6},{5,7},{6,4},{7,5},{8,10},{9,11},{10,... | collective-permute-start | bytes 73736 | tf_op jit(solution)/shard_map/ppermute | solution.py:456
  4.3 1.3 %collective-permute-start.1 = (f32[1,48,128]{2,1,0:T(8,128)S(1)}, f32[1,48,128]{2,1,0:T(8,128)S(1)}, u32[]{:S(2)}, u32[]{:S(2)}) collective-permute-start(f32[1,48,128]{2,1,0:T(8,128)S(1)} %bitcast.5), channel_id=1, source_target_pairs={{0,1},{1,0},{2,3},{3,2},{4,5},{5,4},{6,7},{7,6},{8,9},{9,8},{10,11... | collective-permute-start | bytes 73736 | tf_op jit(solution)/shard_map/ppermute | solution.py:456
  5.6 0.0 collective-permute-done.refs_1_
  5.6 1.3 %collective-permute-start.2 = (f32[1,48,128]{2,1,0:T(8,128)S(1)}, f32[1,48,128]{2,1,0:T(8,128)S(1)}, u32[]{:S(2)}, u32[]{:S(2)}) collective-permute-start(f32[1,48,128]{2,1,0:T(8,128)S(1)} %collective-permute-done.refs_1_), channel_id=1, source_target_pairs={{0,1},{1,0},{2,3},{3,2},{4,5},{5,4},{6,7},{7,6},{8,9},{9,8},{10,11... | collective-permute-start | bytes 73736 | tf_op jit(solution)/shard_map/ppermute | solution.py:456
  6.9 0.2 collective-permute-start.5
  7.1 0.1 collective-permute-done.1.refs_2_
  7.2 1.6 %collective-permute-done.2.refs_3_ = f32[1,48,128]{2,1,0:T(8,128)S(1)} collective-permute-done((f32[1,48,128]{2,1,0:T(8,128)S(1)}, f32[1,48,128]{2,1,0:T(8,128)S(1)}, u32[]{:S(2)}, u32[]{:S(2)}) %collective-permute-start.2) | collective-permute-done | bytes 24608 | tf_op jit(solution)/shard_map/ppermute | solution.py:456
  8.7 1.2 %shard_map.123 = (f32[4,8,128]{2,1,0:T(8,128)S(1)}, f32[4,4,128]{2,1,0:T(4,128)S(1)}, f32[4,4,128]{2,1,0:T(4,128)S(1)}, f32[4,16,128]{2,1,0:T(8,128)S(1)}, f32[1...) custom-call(f32[1,48,128]{2,1,0:T(8,128)S(1)} %bitcast.6, ...), custom_call_target="tpu_custom_call" | custom-call | tf_op jit(solution)/shard_map/pallas_call | solution.py:420
  10.0 2.7 %collective-permute-start.3 = (f32[4,4,128]{2,1,0:T(4,128)S(1)}, f32[4,4,128]{2,1,0:T(4,128)S(1)}, u32[]{:S(2)}, u32[]{:S(2)}) collective-permute-start(f32[4,4,128]{2,1,0:T(4,128)S(1)} %get-tuple-element.25), channel_id=1, source_target_pairs={{0,4},{1,5},{2,6},{3,7},{4,0},{5,1},{6,2},{7,3},{8,12},{9,13},{10,... | collective-permute-start | bytes 24584 | tf_op jit(solution)/shard_map/ppermute | solution.py:442
  12.6 1.2 %collective-permute-start.4 = (f32[4,4,128]{2,1,0:T(4,128)S(1)}, f32[4,4,128]{2,1,0:T(4,128)S(1)}, u32[]{:S(2)}, u32[]{:S(2)}) collective-permute-start(f32[4,4,128]{2,1,0:T(4,128)S(1)} %get-tuple-element.26), channel_id=1, source_target_pairs={{0,1},{1,0},{2,3},{3,2},{4,8},{5,9},{6,10},{7,11},{8,4},{9,5},{10,... | collective-permute-start | bytes 24584 | tf_op jit(solution)/shard_map/ppermute | solution.py:442
  13.8 0.0 collective-permute-start.6
  13.8 0.3 %shard_map.124 = (f32[4,8,128]{2,1,0:T(8,128)S(1)}, f32[96,128]{1,0:T(8,128)S(1)}) custom-call(f32[4,16,128]{2,1,0:T(8,128)S(1)} %get-tuple-element.20.keep_ref, f32[4,8,128]{2,1,0:T(8,128)S(1)} %get-tuple-element.21.total_ref, f32[192,128]{1,0:T(8,128)S(1)} %get-tuple-element.22.idx_ref, f32[64,64]{1,0:T(8,128)S(1)} %get-tuple-element.23.link_ref), custom_call_target="tpu_custom_call" | custom-call | tf_op jit(solution)/shard_map/pallas_call | solution.py:420
  14.1 0.0 collective-permute-done.3.pair_ref
  14.1 2.5 %collective-permute-done.4.other_ref = f32[4,4,128]{2,1,0:T(4,128)S(1)} collective-permute-done((f32[4,4,128]{2,1,0:T(4,128)S(1)}, f32[4,4,128]{2,1,0:T(4,128)S(1)}, u32[]{:S(2)}, u32[]{:S(2)}) %collective-permute-start.4) | collective-permute-done | bytes 8224 | tf_op jit(solution)/shard_map/ppermute | solution.py:442
  16.6 0.8 %shard_map.125 = (f32[4,8,128]{2,1,0:T(8,128)S(1)}, f32[8,128]{1,0:T(8,128)S(1)}, f32[8,128]{1,0:T(8,128)S(1)}, f32[8,128]{1,0:T(8,128)S(1)}) custom-call(f32[4,16,128]{2,1,0:T(8,128)S(1)} %get-tuple-element.20.keep_ref, f32[4,8,128]{2,1,0:T(8,128)S(1)} %get-tuple-element.24.base_ref, f32[4,4,128]{2,1,0:T(4,128)S(1)} %collective-permute-done.3.pair_ref, ...), custom_call_target="tpu_custom_call" | custom-call | tf_op jit(solution)/shard_map/pallas_call | solution.py:420
  17.5 0.0 collective-permute-start.7
  17.5 1.2 %collective-permute-start.8 = (f32[8,128]{1,0:T(8,128)S(1)}, f32[8,128]{1,0:T(8,128)S(1)}, u32[]{:S(2)}, u32[]{:S(2)}) collective-permute-start(f32[8,128]{1,0:T(8,128)S(1)} %get-tuple-element.35), channel_id=1, source_target_pairs={{0,1},{1,0},{2,3},{3,2},{4,8},{5,9},{6,10},{7,11},{8,4},{9,5},{10,... | collective-permute-start | bytes 12296 | tf_op jit(solution)/shard_map/ppermute | solution.py:442
  18.7 0.0 collective-permute-done.5.pair_ref
  18.7 0.0 collective-permute-done.6.other_ref
  18.7 1.1 %shard_map.126.total_ref = f32[8,128]{1,0:T(8,128)S(1)} custom-call(f32[4,16,128]{2,1,0:T(8,128)S(1)} %get-tuple-element.20.keep_ref, f32[4,8,128]{2,1,0:T(8,128)S(1)} %get-tuple-element.30.next_ref, f32[8,128]{1,0:T(8,128)S(1)} %get-tuple-element.31.near_ref, f32[192,128]{1,0:T(8,128)S(1)} %get-tuple-element.22.idx_ref, ...), custom_call_target="tpu_custom_call" | custom-call | tf_op jit(solution)/shard_map/pallas_call | solution.py:420
  19.9 0.0 collective-permute-done.7.pair_ref
  19.9 1.6 %collective-permute-done.8.other_ref = f32[8,128]{1,0:T(8,128)S(1)} collective-permute-done((f32[8,128]{1,0:T(8,128)S(1)}, f32[8,128]{1,0:T(8,128)S(1)}, u32[]{:S(2)}, u32[]{:S(2)}) %collective-permute-start.8) | collective-permute-done | bytes 4128 | tf_op jit(solution)/shard_map/ppermute | solution.py:442
  21.5 0.8 %shard_map.127 = (f32[3,128]{1,0:T(4,128)}, f32[3,128]{1,0:T(4,128)}) custom-call(f32[4,16,128]{2,1,0:T(8,128)S(1)} %get-tuple-element.20.keep_ref, f32[4,8,128]{2,1,0:T(8,128)S(1)} %get-tuple-element.30.next_ref, f32[8,128]{1,0:T(8,128)S(1)} %shard_map.126.total_ref, f32[8,128]{1,0:T(8,128)S(1)} %collective-permute-done.7.pair_ref, ...), custom_call_target="tpu_custom_call" | custom-call | tf_op jit(solution)/shard_map/pallas_call | solution.py:420
Async XLA Ops:
  1.9 3.7 %collective-permute-start = (f32[1,48,128]{2,1,0:T(8,128)S(1)}, f32[1,48,128]{2,1,0:T(8,128)S(1)}, u32[]{:S(2)}, u32[]{:S(2)}) collective-permute-start(f32[1,48,128]{2,1,0:T(8,128)S(1)} %bitcast.4), channel_id=1, source_target_pairs={{0,2},{1,3},{2,0},{3,1},{4,6},{5,7},{6,4},{7,5},{8,10},{9,11},{10,... | collective-permute-start | bytes 73736 | tf_op jit(solution)/shard_map/ppermute | solution.py:456
  4.3 2.8 %collective-permute-start.1 = (f32[1,48,128]{2,1,0:T(8,128)S(1)}, f32[1,48,128]{2,1,0:T(8,128)S(1)}, u32[]{:S(2)}, u32[]{:S(2)}) collective-permute-start(f32[1,48,128]{2,1,0:T(8,128)S(1)} %bitcast.5), channel_id=1, source_target_pairs={{0,1},{1,0},{2,3},{3,2},{4,5},{5,4},{6,7},{7,6},{8,9},{9,8},{10,11... | collective-permute-start | bytes 73736 | tf_op jit(solution)/shard_map/ppermute | solution.py:456
  5.6 3.1 %collective-permute-start.2 = (f32[1,48,128]{2,1,0:T(8,128)S(1)}, f32[1,48,128]{2,1,0:T(8,128)S(1)}, u32[]{:S(2)}, u32[]{:S(2)}) collective-permute-start(f32[1,48,128]{2,1,0:T(8,128)S(1)} %collective-permute-done.refs_1_), channel_id=1, source_target_pairs={{0,1},{1,0},{2,3},{3,2},{4,5},{5,4},{6,7},{7,6},{8,9},{9,8},{10,11... | collective-permute-start | bytes 73736 | tf_op jit(solution)/shard_map/ppermute | solution.py:456
  6.9 11.8 %collective-permute-start.5 = (f32[24,128]{1,0:T(8,128)S(1)}, f32[24,128]{1,0:T(8,128)S(1)}, u32[]{:S(2)}, u32[]{:S(2)}) collective-permute-start(f32[24,128]{1,0:T(8,128)S(1)} %get-tuple-element.29.mesh_ref), channel_id=1, source_target_pairs={{0,1},{4,5},{8,9},{12,13},{16,17},{20,21},{24,25},{28,29},{1,0},{5... | collective-permute-start | bytes 36872 | tf_op jit(solution)/shard_map/ppermute | solution.py:442
  10.0 4.2 %collective-permute-start.3 = (f32[4,4,128]{2,1,0:T(4,128)S(1)}, f32[4,4,128]{2,1,0:T(4,128)S(1)}, u32[]{:S(2)}, u32[]{:S(2)}) collective-permute-start(f32[4,4,128]{2,1,0:T(4,128)S(1)} %get-tuple-element.25), channel_id=1, source_target_pairs={{0,4},{1,5},{2,6},{3,7},{4,0},{5,1},{6,2},{7,3},{8,12},{9,13},{10,... | collective-permute-start | bytes 24584 | tf_op jit(solution)/shard_map/ppermute | solution.py:442
  12.6 4.0 %collective-permute-start.4 = (f32[4,4,128]{2,1,0:T(4,128)S(1)}, f32[4,4,128]{2,1,0:T(4,128)S(1)}, u32[]{:S(2)}, u32[]{:S(2)}) collective-permute-start(f32[4,4,128]{2,1,0:T(4,128)S(1)} %get-tuple-element.26), channel_id=1, source_target_pairs={{0,1},{1,0},{2,3},{3,2},{4,8},{5,9},{6,10},{7,11},{8,4},{9,5},{10,... | collective-permute-start | bytes 24584 | tf_op jit(solution)/shard_map/ppermute | solution.py:442
  13.8 4.9 %collective-permute-start.6 = (f32[24,128]{1,0:T(8,128)S(1)}, f32[24,128]{1,0:T(8,128)S(1)}, u32[]{:S(2)}, u32[]{:S(2)}) collective-permute-start(f32[24,128]{1,0:T(8,128)S(1)} %get-tuple-element.29.mesh_ref), channel_id=1, source_target_pairs={{0,4},{4,0},{8,12},{12,8},{16,20},{20,16},{24,28},{28,24},{1,2},{5... | collective-permute-start | bytes 36872 | tf_op jit(solution)/shard_map/ppermute | solution.py:442
  17.5 2.4 %collective-permute-start.7 = (f32[8,128]{1,0:T(8,128)S(1)}, f32[8,128]{1,0:T(8,128)S(1)}, u32[]{:S(2)}, u32[]{:S(2)}) collective-permute-start(f32[8,128]{1,0:T(8,128)S(1)} %get-tuple-element.34), channel_id=1, source_target_pairs={{0,4},{1,5},{2,6},{3,7},{4,0},{5,1},{6,2},{7,3},{8,12},{9,13},{10,... | collective-permute-start | bytes 12296 | tf_op jit(solution)/shard_map/ppermute | solution.py:442
  17.5 4.0 %collective-permute-start.8 = (f32[8,128]{1,0:T(8,128)S(1)}, f32[8,128]{1,0:T(8,128)S(1)}, u32[]{:S(2)}, u32[]{:S(2)}) collective-permute-start(f32[8,128]{1,0:T(8,128)S(1)} %get-tuple-element.35), channel_id=1, source_target_pairs={{0,1},{1,0},{2,3},{3,2},{4,8},{5,9},{6,10},{7,11},{8,4},{9,5},{10,... | collective-permute-start | bytes 12296 | tf_op jit(solution)/shard_map/ppermute | solution.py:442

commit v8 on v7

--- a/solution.py
+++ b/solution.py
@@ -292,7 +292,7 @@
     return jnp.logical_and(partner >= 0, partner < size)
 
 
-def mid_kernel(width, patches, keep_ref, total_ref, idx_ref, link_ref, base_ref, table_ref):
+def mid_kernel(width, patches, keep_ref, total_ref, idx_ref, link_ref, base_ref, table_ref, list_ref, split_ref):
     me = lax.axis_index("my")
     count = width * patches
     back = link_ref[0:patches, :].astype(jnp.bfloat16)
@@ -308,6 +308,9 @@
     ]
     for g, rows in enumerate(table):
         table_ref[g * patches : (g + 1) * patches, :] = rows
+    for g, part in enumerate(parted(jnp.concatenate(table[0:2], axis=0))):
+        split_ref[g * 2 * patches : (g + 1) * 2 * patches, :] = part
+    side = lax.rem(lax.axis_index("mx"), 2)
 
     def unit(s):
         info = keep_ref[s, 0 : 2 * TILE, :]
@@ -317,6 +320,9 @@
         high = face_values(total_ref[up], keep_ref[up, ROW_LISTS + 2 : ROW_LISTS + 3, :])
         tiles = [jnp.where(u > 0, low, 0.0), jnp.where(u < width - 1, high, 0.0)]
         total = total_ref[s] + faces(tiles, [info[ROW_LISTS + 2 : ROW_LISTS + 3], info[ROW_LISTS + 3 : ROW_LISTS + 4]])
+        lists = info[ROW_LISTS : ROW_LISTS + 2]
+        near, far = jnp.where(side == 0, lists[1:2], lists[0:1]), jnp.where(side == 0, lists[0:1], lists[1:2])
+        list_ref[s] = jnp.concatenate([*parted(near), *parted(far)], axis=0)
         mass = info[ROW_MASS : ROW_MASS + 1]
         base_ref[s, 0:4, :] = info[0:4]
         base_ref[s, 4:7, :] = info[ROW_SPEED : ROW_SPEED + 3] + time_step * mass * total[0:3]
@@ -324,10 +330,9 @@
     each_unit(width, unit)
 
 
-def mx_faces(lists, pair, other):
-    side = lax.rem(lax.axis_index("mx"), 2)
-    near, far = jnp.where(side == 0, lists[1:2], lists[0:1]), jnp.where(side == 0, lists[0:1], lists[1:2])
-    return faces([pair, jnp.where(inside("mx"), other, 0.0)], [near, far])
+def mx_faces(spots, pair, other):
+    tiles = [pair, jnp.where(inside("mx"), other, 0.0)]
+    return scatter(joined([(spots[2 * k : 2 * k + 1], spots[2 * k + 1 : 2 * k + 2], tile_parts(tiles[k])) for k in (0, 1)]))
 
 
 def elements_of(mesh, state, corners):
@@ -338,7 +343,7 @@
 
 
 def step_kernel(
-    width, patches, corners, keep_ref, base_ref, pair_ref, other_ref, table_ref, stiff_ref, mesh_ref,
+    width, patches, corners, keep_ref, base_ref, pair_ref, other_ref, table_ref, list_ref, split_ref, stiff_ref, mesh_ref,
     next_ref, near_ref, send_ref, far_ref, parts_ref, element_ref,
 ):
     side = lax.rem(lax.axis_index("mx"), 2)
@@ -346,9 +351,8 @@
 
     def unit(s):
         base = base_ref[s]
-        lists = keep_ref[s, ROW_LISTS : ROW_LISTS + 4, :]
         pair, other = [jnp.concatenate([ref[s], blank], axis=0) for ref in (pair_ref, other_ref)]
-        speed = base[4:7] + time_step * base[3:4] * mx_faces(lists, pair, other)[0:3]
+        speed = base[4:7] + time_step * base[3:4] * mx_faces(list_ref[s], pair, other)[0:3]
         next_ref[s, 0:3, :] = base[0:3] + time_step * speed
         next_ref[s, 4:7, :] = speed
 
@@ -364,8 +368,10 @@
         second.append(jnp.concatenate([pick(choose(rows, to_slot), target), pick(home, landing)], axis=0))
     sign = jnp.where(lax.broadcasted_iota(jnp.int32, (2 * patches, LANES), 0) < patches, 1.0, -1.0)
     put_parts(parts_ref, [sign * force for force in pair_forces(first, second)])
-    coarse, fine = parted(table_ref[0 : 2 * patches, :])
-    contact = [(coarse[k : k + 1], fine[k : k + 1], get_parts(parts_ref, k)) for k in range(2 * patches)]
+    contact = [
+        (split_ref[k : k + 1, :], split_ref[2 * patches + k : 2 * patches + k + 1, :], get_parts(parts_ref, k))
+        for k in range(2 * patches)
+    ]
     total = scatter(elastic + joined(contact))
     near_ref[...] = total
     lists = keep_ref[0, ROW_LISTS : ROW_LISTS + 4, :]
@@ -408,9 +414,8 @@
     total_ref[...] = near_ref[...] + faces(tiles, [lists[2:3], lists[3:4]])
 
 
-def end_kernel(keep_ref, next_ref, total_ref, pair_ref, other_ref, place_ref, speed_ref):
-    lists = keep_ref[0, ROW_LISTS : ROW_LISTS + 4, :]
-    total = total_ref[...] + mx_faces(lists, pair_ref[...], other_ref[...])
+def end_kernel(keep_ref, list_ref, next_ref, total_ref, pair_ref, other_ref, place_ref, speed_ref):
+    total = total_ref[...] + mx_faces(list_ref[0], pair_ref[...], other_ref[...])
     speed = next_ref[0, 4:7, :] + time_step * keep_ref[0, ROW_MASS : ROW_MASS + 1, :] * total[0:3]
     speed_ref[...] = speed
     place_ref[...] = next_ref[0, 0:3, :] + time_step * speed
@@ -502,9 +507,9 @@
     )
     states = (width, TILE, LANES)
     pair, other = both(pair, other)
-    base, table = call(
+    base, table, lists, split = call(
         functools.partial(mid_kernel, width, patches),
-        [states, (6 * patches, LANES)],
+        [states, (6 * patches, LANES), (width, 4, LANES), (4 * patches, LANES)],
         [],
         keep, total, indices, link,
     )
@@ -513,7 +518,7 @@
         contact,
         [states, tile, tile, tile],
         [(TILE * 2 * patches, LANES), element_parts],
-        keep, base, pair, other, table, stiff, mesh,
+        keep, base, pair, other, table, lists, split, stiff, mesh,
     )
     pair, other = both(pair, other)
     (total,) = call(
@@ -523,7 +528,7 @@
         keep, state, near, indices, link, *spots, stiff, mesh_pair, mesh_other,
     )
     outs = [(3, LANES), (3, LANES)]
-    return tuple(call(end_kernel, outs, [], keep, state, total, pair, other, result=jax.ShapeDtypeStruct))
+    return tuple(call(end_kernel, outs, [], keep, lists, state, total, pair, other, result=jax.ShapeDtypeStruct))
 
 
 def solution(mesh):

time: 22.5 us -> 23 us (1.022)
  the two profiles are of different devices: /device:TPU:3 before, /device:TPU:0 now
where the time goes in v8:
time: 23 us; the launch traced here: 22.9 us
  starting transfers between devices  13.8 us (60%)
  Pallas kernels  5.59 us (24%)
  waiting for transfers between devices  2.72 us (12%)
  between operations  0.7 us (3%)
    ppermute x3, starting transfers between devices, exchange(): return lax.ppermute(value, axis, [(i, i ^ step) for i in range(size)])  7.6 us
    ppermute x6, starting transfers between devices, swap(): return lax.ppermute(value, axes, pairs)  6.24 us
    pallas_call x6, Pallas kernels, call(): pl.pallas_call(kernel, out_shape=[result(shape, jnp.float32) for shape in...  5.59 us
    ppermute x3, waiting for transfers between devices, exchange(): return lax.ppermute(value, axis, [(i, i ^ step) for i in range(size)])  2.17 us
    ppermute x6, waiting for transfers between devices, swap(): return lax.ppermute(value, axes, pairs)  0.55 us
  transfers between devices with their start and end apart: 9, of which 5 were waited for; matrix products, arithmetic and copies ran while one was open for 0% of the time, Pallas kernels for 10%

profile of v8, /device:TPU:0, one launch (start us, length us, event | category | flops | bytes accessed | tf_op | source)
XLA Modules:
  0.0 22.9 jit_solution(8031155583581492349)
XLA Ops:
  0.6 1.3 %shard_map.122 = (f32[48,128]{1,0:T(8,128)S(1)}, f32[24,128]{1,0:T(8,128)S(1)}, f32[24,24]{1,0:T(8,128)S(1)}) custom-call(f32[3,128]{1,0:T(4,128)} %place_ref.1, f32[3,128]{1,0:T(4,128)} %speed_ref.1, f32[3,128]{1,0:T(4,128)} %rest_ref.1, f32[1,128]{1,0:T(1,128)} %bitcast.8, s32[8,256]{1,0:T(8,128)} %connect_ref.1, f32[1,256]{1,0:T(1,128)} %bitcast.7, ...), custom_call_target="tpu_custom_call" | custom-call | tf_op jit(solution)/shard_map/pallas_call | solution.py:425
  1.9 4.1 %collective-permute-start = (f32[1,48,128]{2,1,0:T(8,128)S(1)}, f32[1,48,128]{2,1,0:T(8,128)S(1)}, u32[]{:S(2)}, u32[]{:S(2)}) collective-permute-start(f32[1,48,128]{2,1,0:T(8,128)S(1)} %bitcast.4), channel_id=1, source_target_pairs={{0,2},{1,3},{2,0},{3,1},{4,6},{5,7},{6,4},{7,5},{8,10},{9,11},{10,... | collective-permute-start | bytes 73736 | tf_op jit(solution)/shard_map/ppermute | solution.py:461
  6.1 1.6 %collective-permute-start.1 = (f32[1,48,128]{2,1,0:T(8,128)S(1)}, f32[1,48,128]{2,1,0:T(8,128)S(1)}, u32[]{:S(2)}, u32[]{:S(2)}) collective-permute-start(f32[1,48,128]{2,1,0:T(8,128)S(1)} %bitcast.5), channel_id=1, source_target_pairs={{0,1},{1,0},{2,3},{3,2},{4,5},{5,4},{6,7},{7,6},{8,9},{9,8},{10,11... | collective-permute-start | bytes 73736 | tf_op jit(solution)/shard_map/ppermute | solution.py:461
  7.7 0.2 %collective-permute-done.refs_1_ = f32[1,48,128]{2,1,0:T(8,128)S(1)} collective-permute-done((f32[1,48,128]{2,1,0:T(8,128)S(1)}, f32[1,48,128]{2,1,0:T(8,128)S(1)}, u32[]{:S(2)}, u32[]{:S(2)}) %collective-permute-start) | collective-permute-done | bytes 24608 | tf_op jit(solution)/shard_map/ppermute | solution.py:461
  7.9 1.9 %collective-permute-start.2 = (f32[1,48,128]{2,1,0:T(8,128)S(1)}, f32[1,48,128]{2,1,0:T(8,128)S(1)}, u32[]{:S(2)}, u32[]{:S(2)}) collective-permute-start(f32[1,48,128]{2,1,0:T(8,128)S(1)} %collective-permute-done.refs_1_), channel_id=1, source_target_pairs={{0,1},{1,0},{2,3},{3,2},{4,5},{5,4},{6,7},{7,6},{8,9},{9,8},{10,11... | collective-permute-start | bytes 73736 | tf_op jit(solution)/shard_map/ppermute | solution.py:461
  9.8 0.3 %collective-permute-done.1.refs_2_ = f32[1,48,128]{2,1,0:T(8,128)S(1)} collective-permute-done((f32[1,48,128]{2,1,0:T(8,128)S(1)}, f32[1,48,128]{2,1,0:T(8,128)S(1)}, u32[]{:S(2)}, u32[]{:S(2)}) %collective-permute-start.1) | collective-permute-done | bytes 24608 | tf_op jit(solution)/shard_map/ppermute | solution.py:461
  10.1 1.7 %collective-permute-done.2.refs_3_ = f32[1,48,128]{2,1,0:T(8,128)S(1)} collective-permute-done((f32[1,48,128]{2,1,0:T(8,128)S(1)}, f32[1,48,128]{2,1,0:T(8,128)S(1)}, u32[]{:S(2)}, u32[]{:S(2)}) %collective-permute-start.2) | collective-permute-done | bytes 24608 | tf_op jit(solution)/shard_map/ppermute | solution.py:461
  11.7 1.2 %shard_map.123 = (f32[4,8,128]{2,1,0:T(8,128)S(1)}, f32[4,4,128]{2,1,0:T(4,128)S(1)}, f32[4,4,128]{2,1,0:T(4,128)S(1)}, f32[4,16,128]{2,1,0:T(8,128)S(1)}, f32[1...) custom-call(f32[1,48,128]{2,1,0:T(8,128)S(1)} %bitcast.6, ...), custom_call_target="tpu_custom_call" | custom-call | tf_op jit(solution)/shard_map/pallas_call | solution.py:425
  13.0 0.0 collective-permute-start.3
  13.0 2.0 %collective-permute-start.4 = (f32[4,4,128]{2,1,0:T(4,128)S(1)}, f32[4,4,128]{2,1,0:T(4,128)S(1)}, u32[]{:S(2)}, u32[]{:S(2)}) collective-permute-start(f32[4,4,128]{2,1,0:T(4,128)S(1)} %get-tuple-element.29), channel_id=1, source_target_pairs={{0,1},{1,0},{2,3},{3,2},{4,8},{5,9},{6,10},{7,11},{8,4},{9,5},{10,... | collective-permute-start | bytes 24584 | tf_op jit(solution)/shard_map/ppermute | solution.py:447
  14.9 0.1 collective-permute-start.5
  15.1 1.2 %collective-permute-start.6 = (f32[24,128]{1,0:T(8,128)S(1)}, f32[24,128]{1,0:T(8,128)S(1)}, u32[]{:S(2)}, u32[]{:S(2)}) collective-permute-start(f32[24,128]{1,0:T(8,128)S(1)} %get-tuple-element.33.mesh_ref), channel_id=1, source_target_pairs={{0,4},{4,0},{8,12},{12,8},{16,20},{20,16},{24,28},{28,24},{1,2},{5... | collective-permute-start | bytes 36872 | tf_op jit(solution)/shard_map/ppermute | solution.py:447
  16.3 0.3 %shard_map.124 = (f32[4,8,128]{2,1,0:T(8,128)S(1)}, f32[96,128]{1,0:T(8,128)S(1)}, f32[4,4,128]{2,1,0:T(4,128)S(1)}, f32[64,128]{1,0:T(8,128)S(1)}) custom-call(f32[4,16,128]{2,1,0:T(8,128)S(1)} %get-tuple-element.22.keep_ref, f32[4,8,128]{2,1,0:T(8,128)S(1)} %get-tuple-element.23.total_ref, f32[192,128]{1,0:T(8,128)S(1)} %get-tuple-element.24.idx_ref, ...), custom_call_target="tpu_custom_call" | custom-call | tf_op jit(solution)/shard_map/pallas_call | solution.py:425
  16.6 0.0 collective-permute-done.3.pair_ref
  16.6 0.1 collective-permute-done.4.other_ref
  16.7 0.8 %shard_map.125 = (f32[4,8,128]{2,1,0:T(8,128)S(1)}, f32[8,128]{1,0:T(8,128)S(1)}, f32[8,128]{1,0:T(8,128)S(1)}, f32[8,128]{1,0:T(8,128)S(1)}) custom-call(f32[4,16,128]{2,1,0:T(8,128)S(1)} %get-tuple-element.22.keep_ref, f32[4,8,128]{2,1,0:T(8,128)S(1)} %get-tuple-element.27.base_ref, f32[4,4,128]{2,1,0:T(4,128)S(1)} %collective-permute-done.3.pair_ref, ...), custom_call_target="tpu_custom_call" | custom-call | tf_op jit(solution)/shard_map/pallas_call | solution.py:425
  17.5 0.1 collective-permute-start.7
  17.7 2.8 %collective-permute-start.8 = (f32[8,128]{1,0:T(8,128)S(1)}, f32[8,128]{1,0:T(8,128)S(1)}, u32[]{:S(2)}, u32[]{:S(2)}) collective-permute-start(f32[8,128]{1,0:T(8,128)S(1)} %get-tuple-element.39), channel_id=1, source_target_pairs={{0,1},{1,0},{2,3},{3,2},{4,8},{5,9},{6,10},{7,11},{8,4},{9,5},{10,... | collective-permute-start | bytes 12296 | tf_op jit(solution)/shard_map/ppermute | solution.py:447
  20.5 0.0 collective-permute-done.5.pair_ref
  20.5 0.0 collective-permute-done.6.other_ref
  20.5 1.1 %shard_map.126.total_ref = f32[8,128]{1,0:T(8,128)S(1)} custom-call(f32[4,16,128]{2,1,0:T(8,128)S(1)} %get-tuple-element.22.keep_ref, f32[4,8,128]{2,1,0:T(8,128)S(1)} %get-tuple-element.34.next_ref, f32[8,128]{1,0:T(8,128)S(1)} %get-tuple-element.35.near_ref, f32[192,128]{1,0:T(8,128)S(1)} %get-tuple-element.24.idx_ref, ...), custom_call_target="tpu_custom_call" | custom-call | tf_op jit(solution)/shard_map/pallas_call | solution.py:425
  21.6 0.0 collective-permute-done.7.pair_ref
  21.6 0.4 %collective-permute-done.8.other_ref = f32[8,128]{1,0:T(8,128)S(1)} collective-permute-done((f32[8,128]{1,0:T(8,128)S(1)}, f32[8,128]{1,0:T(8,128)S(1)}, u32[]{:S(2)}, u32[]{:S(2)}) %collective-permute-start.8) | collective-permute-done | bytes 4128 | tf_op jit(solution)/shard_map/ppermute | solution.py:447
  22.1 0.8 %shard_map.127 = (f32[3,128]{1,0:T(4,128)}, f32[3,128]{1,0:T(4,128)}) custom-call(f32[4,16,128]{2,1,0:T(8,128)S(1)} %get-tuple-element.22.keep_ref, f32[4,4,128]{2,1,0:T(4,128)S(1)} %get-tuple-element.26.list_ref, f32[4,8,128]{2,1,0:T(8,128)S(1)} %get-tuple-element.34.next_ref, f32[8,128]{1,0:T(8,128)S(1)} %shard_map.126.total_ref, ...), custom_call_target="tpu_custom_call" | custom-call | tf_op jit(solution)/shard_map/pallas_call | solution.py:425
Async XLA Ops:
  1.9 5.9 %collective-permute-start = (f32[1,48,128]{2,1,0:T(8,128)S(1)}, f32[1,48,128]{2,1,0:T(8,128)S(1)}, u32[]{:S(2)}, u32[]{:S(2)}) collective-permute-start(f32[1,48,128]{2,1,0:T(8,128)S(1)} %bitcast.4), channel_id=1, source_target_pairs={{0,2},{1,3},{2,0},{3,1},{4,6},{5,7},{6,4},{7,5},{8,10},{9,11},{10,... | collective-permute-start | bytes 73736 | tf_op jit(solution)/shard_map/ppermute | solution.py:461
  6.1 4.0 %collective-permute-start.1 = (f32[1,48,128]{2,1,0:T(8,128)S(1)}, f32[1,48,128]{2,1,0:T(8,128)S(1)}, u32[]{:S(2)}, u32[]{:S(2)}) collective-permute-start(f32[1,48,128]{2,1,0:T(8,128)S(1)} %bitcast.5), channel_id=1, source_target_pairs={{0,1},{1,0},{2,3},{3,2},{4,5},{5,4},{6,7},{7,6},{8,9},{9,8},{10,11... | collective-permute-start | bytes 73736 | tf_op jit(solution)/shard_map/ppermute | solution.py:461
  7.9 3.8 %collective-permute-start.2 = (f32[1,48,128]{2,1,0:T(8,128)S(1)}, f32[1,48,128]{2,1,0:T(8,128)S(1)}, u32[]{:S(2)}, u32[]{:S(2)}) collective-permute-start(f32[1,48,128]{2,1,0:T(8,128)S(1)} %collective-permute-done.refs_1_), channel_id=1, source_target_pairs={{0,1},{1,0},{2,3},{3,2},{4,5},{5,4},{6,7},{7,6},{8,9},{9,8},{10,11... | collective-permute-start | bytes 73736 | tf_op jit(solution)/shard_map/ppermute | solution.py:461
  13.0 3.6 %collective-permute-start.3 = (f32[4,4,128]{2,1,0:T(4,128)S(1)}, f32[4,4,128]{2,1,0:T(4,128)S(1)}, u32[]{:S(2)}, u32[]{:S(2)}) collective-permute-start(f32[4,4,128]{2,1,0:T(4,128)S(1)} %get-tuple-element.28), channel_id=1, source_target_pairs={{0,4},{1,5},{2,6},{3,7},{4,0},{5,1},{6,2},{7,3},{8,12},{9,13},{10,... | collective-permute-start | bytes 24584 | tf_op jit(solution)/shard_map/ppermute | solution.py:447
  13.0 3.7 %collective-permute-start.4 = (f32[4,4,128]{2,1,0:T(4,128)S(1)}, f32[4,4,128]{2,1,0:T(4,128)S(1)}, u32[]{:S(2)}, u32[]{:S(2)}) collective-permute-start(f32[4,4,128]{2,1,0:T(4,128)S(1)} %get-tuple-element.29), channel_id=1, source_target_pairs={{0,1},{1,0},{2,3},{3,2},{4,8},{5,9},{6,10},{7,11},{8,4},{9,5},{10,... | collective-permute-start | bytes 24584 | tf_op jit(solution)/shard_map/ppermute | solution.py:447
  14.9 5.5 %collective-permute-start.5 = (f32[24,128]{1,0:T(8,128)S(1)}, f32[24,128]{1,0:T(8,128)S(1)}, u32[]{:S(2)}, u32[]{:S(2)}) collective-permute-start(f32[24,128]{1,0:T(8,128)S(1)} %get-tuple-element.33.mesh_ref), channel_id=1, source_target_pairs={{0,1},{4,5},{8,9},{12,13},{16,17},{20,21},{24,25},{28,29},{1,0},{5... | collective-permute-start | bytes 36872 | tf_op jit(solution)/shard_map/ppermute | solution.py:447
  15.1 5.4 %collective-permute-start.6 = (f32[24,128]{1,0:T(8,128)S(1)}, f32[24,128]{1,0:T(8,128)S(1)}, u32[]{:S(2)}, u32[]{:S(2)}) collective-permute-start(f32[24,128]{1,0:T(8,128)S(1)} %get-tuple-element.33.mesh_ref), channel_id=1, source_target_pairs={{0,4},{4,0},{8,12},{12,8},{16,20},{20,16},{24,28},{28,24},{1,2},{5... | collective-permute-start | bytes 36872 | tf_op jit(solution)/shard_map/ppermute | solution.py:447
  17.5 4.1 %collective-permute-start.7 = (f32[8,128]{1,0:T(8,128)S(1)}, f32[8,128]{1,0:T(8,128)S(1)}, u32[]{:S(2)}, u32[]{:S(2)}) collective-permute-start(f32[8,128]{1,0:T(8,128)S(1)} %get-tuple-element.38), channel_id=1, source_target_pairs={{0,4},{1,5},{2,6},{3,7},{4,0},{5,1},{6,2},{7,3},{8,12},{9,13},{10,... | collective-permute-start | bytes 12296 | tf_op jit(solution)/shard_map/ppermute | solution.py:447
  17.7 4.4 %collective-permute-start.8 = (f32[8,128]{1,0:T(8,128)S(1)}, f32[8,128]{1,0:T(8,128)S(1)}, u32[]{:S(2)}, u32[]{:S(2)}) collective-permute-start(f32[8,128]{1,0:T(8,128)S(1)} %get-tuple-element.39), channel_id=1, source_target_pairs={{0,1},{1,0},{2,3},{3,2},{4,8},{5,9},{6,10},{7,11},{8,4},{9,5},{10,... | collective-permute-start | bytes 12296 | tf_op jit(solution)/shard_map/ppermute | solution.py:447
